TPU v7x, 256 devices: a whole 4x4x8 slice. The times are simulated.
256 devices in a mesh: dp: 4 (over z_lo), space: 64 (over x, z_hi, y, core).
Axes of the slice: x: 4, y: 4, z: 8 (z_hi: 2, z_lo: 4; z = z_hi * 4 + z_lo), core: 2. Of those that a mesh axis runs over, the one named last changes fastest.
Arguments:
- features: bfloat16 [4, 192, 64, 1024], P('dp', 'space'), may hold values from -6 to 6
- cotangent: bfloat16 [4, 192, 128, 128], P('dp', 'space'), may hold values from -6 to 6
- conv_one: bfloat16 [64, 1728], P('dp'), may hold values from -0.15625 to 0.15625
- down_weight: bfloat16 [128, 512], P('dp'), may hold values from -0.25 to 0.25
- conv_two: bfloat16 [128, 3456], P('dp'), may hold values from -0.109375 to 0.109375
- patch_home: int32 [128], replicated, may hold values from 0 to 191, as said below
- patch_links: int32 [128, 4], replicated, may hold values from -1 to 127, as said below
Outputs:
- level_two: bfloat16 [4, 192, 128, 128], P('dp', 'space')
- grad_conv_one: float32 [64, 1728], P('dp')
- grad_conv_down: float32 [128, 512], P('dp')
- grad_conv_two: float32 [128, 3456], P('dp')
Inputs may be any that keep to these rules, and one draw needn't show every extreme that they name: Patch p sits on device patch_home[p] // 3 of the space axis in slot patch_home[p] % 3; no two patches share a slot; every device holds a run of consecutive patch numbers, the runs in the order of the devices, each of 1 to 3 patches; some device holds exactly 3 and some exactly one. `patch_links`: the patches form a grid of 2 columns and 64 rows, patch 2 r + c in row r and column c; the four entries of a patch name p - 1, p + 1, p - 2, p + 2 or -1 where the grid ends or the link is cut; links are symmetric; the first and the last row are linked across x.
All inputs are finite; a program needn't handle non-finite values.
Results may differ from a plain program's by a relative error of at most 0.014.
Values may be sent and summed in bfloat16 or wider, within the bound.
No kernel may reach another device: no remote copies, remote signals or barrier semaphores. Data moves between devices by JAX's collectives and lax.ppermute only.
A program may use at most 128 MiB of HBM per device.

v0:
```python
import functools
import types

import jax
import jax.numpy as jnp
from jax import lax
from jax.experimental import pallas as pl
from jax.experimental.pallas import tpu as pltpu
from jax.sharding import Mesh
from jax.sharding import PartitionSpec as P


BF = jnp.bfloat16
F32 = jnp.float32
SPACE = ("x", "zh", "y", "core")
NCHIP = 32
ONE = types.SimpleNamespace(C=64, g=64, R=256, N=1024, W=1152, zs=4, nx=16)
TWO = types.SimpleNamespace(C=128, g=16, R=128, N=128, W=256, zs=2, nx=8)
NOWHERE = -8192


def mm(a, b, contract=((1,), (0,))):
    return lax.dot_general(a, b, (contract, ((), ())), preferred_element_type=F32)


NT = ((1,), (1,))
TN = ((0,), (0,))


def one_hot(shape, rule):
    r = lax.broadcasted_iota(jnp.int32, shape, 0)
    l = lax.broadcasted_iota(jnp.int32, shape, 1)
    return jnp.where(rule(r, l), 1.0, 0.0).astype(BF)


def picker(level, off, dst):
    return one_hot(
        (level.R, 128),
        lambda r, l: (r - off == l - dst) & (l >= dst) & (l < dst + level.g),
    )


def corner_picker(level, off, xc):
    g, zs = level.g, level.zs
    return one_hot(
        (level.R, 128),
        lambda r, l: (r - off == l - g) & (l >= g) & (l < 2 * g) & ((l - g) // zs == xc),
    )


def rim_rows(level, y_off):
    g, zs, N, W = level.g, level.zs, level.N, level.W

    def rule(r, l):
        face = (r < g) & (l == (r // zs) * g + r % zs + y_off)
        q = r - g
        low = (q >= 0) & (q < zs) & (l == N + q + y_off)
        high = (q >= g - zs) & (q < g) & (l == W - g + q - (g - zs) + y_off)
        return face | low | high

    return one_hot((128, W), rule)


def where_am_i(sc):
    core = sc[6]
    s = types.SimpleNamespace(core=core, dev=sc[5])
    n0, n1 = sc[2] - sc[1], sc[3] - sc[2]
    s.n0 = n0
    s.total = n0 + n1
    s.start = sc[1]
    s.a = jnp.where(core == 0, sc[1], sc[2])
    s.n = jnp.where(core == 0, n0, n1)
    s.other = jnp.where(core == 0, n1, n0)
    s.chip_before = sc[1] - sc[0]
    s.chip_after = sc[4] - sc[3]
    return s


def locate(s, q, up, level, sub):
    g = level.g
    rec_off = jnp.int32(0 if up else g)
    own = (q >= s.a) & (q < s.a + s.n)
    if up:
        k = s.a - q
        near = jnp.where(s.core == 1, s.other, 0)
        o_idx = 3 + s.other - k
        m_idx = jnp.where(s.core == 0, 6, 8)
        chip = s.chip_before
    else:
        k = q - (s.a + s.n) + 1
        near = jnp.where(s.core == 0, s.other, 0)
        o_idx = 3 + k - 1
        m_idx = jnp.where(s.core == 0, 8, 6)
        chip = s.chip_after
    t = k - near
    in_o = k <= near
    far = t > chip
    idx = jnp.where(own, q - s.a, jnp.where(in_o, o_idx, jnp.where(far, m_idx + 1, m_idx)))
    in_rec = own | in_o
    main = jnp.where(in_rec, rec_off, jnp.where(far, 0, sub * (t - 1) * g))
    corner = jnp.where(in_rec, 3 * g if up else 4 * g, main + g) if sub == 2 else main
    return jnp.clip(idx, 0, 9), main, corner


def locate_x(s, q, level, sub):
    g = level.g
    rec_off = jnp.where(q % 2 == 0, 3 * g, 2 * g) if sub == 1 else jnp.int32(2 * g)
    msg_off = 3 * g if sub == 1 else 6 * g
    own = (q >= s.a) & (q < s.a + s.n)
    before = q < s.a
    in_o = jnp.where(before, s.core == 1, s.core == 0)
    o_idx = jnp.where(before, 3 + s.other - 1, 3)
    m_idx = jnp.where(before == (s.core == 0), 6, 8)
    idx = jnp.where(own, q - s.a, jnp.where(in_o, o_idx, m_idx))
    return jnp.clip(idx, 0, 9), jnp.where(own | in_o, rec_off, msg_off)


def gather_records(recs, own, other, got, swapped):
    for k in range(3):
        recs[k] = own[k]
        recs[3 + k] = other[k]
    for k in range(2):
        recs[6 + k] = got[k][...]
        recs[8 + k] = swapped[k][...]


def link_at(links, q, column):
    return links[jnp.clip(q, 0, 127) * 4 + column]


def x_link(links, q):
    return link_at(links, q, jnp.where(q % 2 == 0, 1, 0))


def extended(level, s, links, recs, rows, field, p):
    even = p % 2 == 0
    partner = jnp.where(even, p + 1, p - 1)
    idx, off = locate_x(s, partner, level, 1)
    off = jnp.where(x_link(links, p) >= 0, off, NOWHERE)
    rim = mm(recs[idx], picker(level, off, jnp.where(even, 0, 128 - level.g)))
    block = jnp.concatenate([field, rim], axis=1)
    rims = []
    for side, up in ((0, True), (1, False)):
        q = p - 2 if up else p + 2
        c = jnp.where(even, q + 1, q - 1)
        ok = link_at(links, p, 2 + side) >= 0
        idx, off, _ = locate(s, q, up, level, 1)
        face = mm(recs[idx], picker(level, jnp.where(ok, off, NOWHERE), 0))
        ok_c = ok & (x_link(links, q) >= 0)
        idx, off, _ = locate(s, c, up, level, 1)
        xc = jnp.where(even, 0, level.nx - 1)
        face += mm(recs[idx], corner_picker(level, jnp.where(ok_c, off, NOWHERE), xc))
        rims.append(mm(face.astype(BF), rows[side]))
    return block, rims[0], rims[1]


def coords(level):
    lane = lax.broadcasted_iota(jnp.int32, (level.C, level.W), 1)
    return (lane % level.g) // level.zs, lane % level.zs


def tap_rows(level, block, low, high, store):
    W, zs = level.W, level.zs
    y, z = coords(level)
    for dy in (-1, 0, 1):
        if dy == 0:
            f = block
        elif dy == -1:
            f = jnp.where(y == 0, low, pltpu.roll(block, zs, 1))
        else:
            f = jnp.where(y == level.nx - 1, high, pltpu.roll(block, W - zs, 1))
        for dz in (-1, 0, 1):
            if dz == 0:
                v = f
            elif dz == -1:
                v = jnp.where(z == 0, 0.0, pltpu.roll(f, 1, 1))
            else:
                v = jnp.where(z == zs - 1, 0.0, pltpu.roll(f, W - 1, 1))
            store(3 * (dy + 1) + dz + 1, v.astype(BF))


def three_shifts(level, y):
    C, W, g = level.C, level.W, level.g
    total = pltpu.roll(y[:C], g, 1) + y[C : 2 * C] + pltpu.roll(y[2 * C :], W - g, 1)
    return total[:, : level.N]


def parity_order():
    def rule(r, l):
        y, z = (r % 64) // 4, r % 4
        e = 4 * (r // 64) + 2 * (y % 2) + z % 2
        return l == e * 16 + (y // 2) * 2 + z // 2

    return one_hot((128, 128), rule)


def swap_groups(arrays):
    group = lax.broadcasted_iota(jnp.int32, (64, 128), 1) // 16
    arrays = list(arrays)
    for b in (1, 2, 4):
        bit = (group & b) != 0
        for i in range(8):
            if i & b:
                continue
            lo, hi = arrays[i], arrays[i + b]
            arrays[i] = jnp.where(bit, pltpu.roll(hi, 16 * b, 1), lo)
            arrays[i + b] = jnp.where(bit, hi, pltpu.roll(lo, 128 - 16 * b, 1))
    return arrays


def faces_kernel(sc, home, x_ref, rec_ref):
    s = where_am_i(sc)

    def rule(r, l):
        group, m = l // 64, l % 64
        high = (group == 0) & (r == (m // 4) * 64 + 60 + m % 4)
        low = (group == 1) & (r == (m // 4) * 64 + m % 4)
        return high | low | ((group == 2) & (r == m)) | ((group == 3) & (r == 960 + m))

    pick = one_hot((1024, 256), rule)
    for i in range(3):
        p = s.a + jnp.minimum(i, s.n - 1)
        slot = home[p] - 3 * s.dev
        rec_ref[i] = mm(x_ref[slot], pick).astype(BF)


def message_kernel(level, sub, sc, own, other, out, both):
    s = where_am_i(sc)
    g = level.g
    for k in range(3):
        both[k] = own[k]
        both[3 + k] = other[k]
    up = s.core == 0
    main = jnp.where(up, 0, g)
    corner = jnp.where(up, 3 * g, 4 * g)
    total = None
    for k in range(3):
        t = jnp.maximum(jnp.where(up, s.total - 1 - k, k), 0)
        t = jnp.minimum(t, s.total - 1)
        first = t < s.n0
        mine = first == (s.core == 0)
        idx = jnp.where(first, t, t - s.n0) + jnp.where(mine, 0, 3)
        q = s.start + t
        base = sub * k * g

        def rule(r, l):
            hit = (r - main == l - base) & (l >= base) & (l < base + g)
            if sub == 2:
                c = base + g
                hit |= (r - corner == l - c) & (l >= c) & (l < c + g)
            if k == 0:
                to = 3 * g if sub == 1 else 6 * g
                src = jnp.where(q % 2 == 0, 3 * g, 2 * g) if sub == 1 else 2 * g
                hit |= (r - src == l - to) & (l >= to) & (l < to + g)
            return hit

        part = mm(both[idx], one_hot((level.R, level.R), rule))
        total = part if total is None else total + part
    out[...] = total.astype(BF)


def stage_one_kernel(sc, home, links, x_ref, own, other, got1, got2, sw1, sw2, w_a, w_b, w_c, w_d,
                     taps, hid, slope, red, rec2, down_out,
                     recs, low_rows, high_rows, w_all, w_one):
    s = where_am_i(sc)
    dp = sc[7]
    gather_records(recs, own, other, (got1, got2), (sw1, sw2))
    low_rows[...] = rim_rows(ONE, 0)
    high_rows[...] = rim_rows(ONE, 60)
    for k, w in enumerate((w_a, w_b, w_c, w_d)):
        w_all[k] = w[...]
    for d in range(4):
        at = jnp.bitwise_xor(jnp.int32(d), dp)
        for dx in range(3):
            w_one[dx * 64 + d * 16 : dx * 64 + d * 16 + 16, :] = w_all[
                at, dx * 16 : dx * 16 + 16, 0:576
            ]
        down_out[d * 32 : d * 32 + 32, :] = w_all[at, 48:80, 0:512]
    order = parity_order()

    @pl.loop(0, 3)
    def _(i):
        at = pl.ds(pl.multiple_of(i * 128, 128), 128)
        p = s.a + jnp.minimum(i, s.n - 1)
        slot = home[p] - 3 * s.dev
        block, low, high = extended(
            ONE, s, links, recs, (low_rows[...], high_rows[...]), x_ref[slot].astype(F32), p
        )

        def store(t, v):
            taps[i, t * 64 : t * 64 + 64, :] = v

        tap_rows(ONE, block, low, high, store)
        taps[i, 576:640, :] = jnp.zeros((64, 1152), BF)
        pre = three_shifts(ONE, mm(w_one[...], taps[i, 0:576, :]))
        tall = jnp.concatenate([pre[:, 128 * b : 128 * b + 128] for b in range(8)], axis=0)
        top = tall.astype(BF)
        rest = (tall - top.astype(F32)).astype(BF)
        tall = mm(top, order) + mm(rest, order)
        parts = swap_groups([tall[64 * b : 64 * b + 64] for b in range(8)])
        for e in range(8):
            v = parts[e]
            sig = 1.0 / (1.0 + jnp.exp(-v))
            hid[e * 64 : e * 64 + 64, at] = (v * sig).astype(BF)
            slope[e * 64 : e * 64 + 64, at] = sig * (1.0 + v * (1.0 - sig))

    red[...] = mm(down_out[...], hid[...]).astype(BF)

    def rule(r, l):
        group, m = l // 16, l % 16
        high = (group == 0) & (r == (m // 2) * 16 + 14 + m % 2)
        low = (group == 1) & (r == (m // 2) * 16 + m % 2)
        return high | low | ((group == 2) & (r == m)) | ((group == 3) & (r == 112 + m))

    pick = one_hot((128, 128), rule)
    for i in range(3):
        rec2[i] = mm(red[:, i * 128 : i * 128 + 128], pick).astype(BF)


def stage_two_kernel(scale, sc, home, links, red, cot, own, other, got1, got2, sw1, sw2,
                     w_a, w_b, w_c, w_d, out, dw, grad, brec,
                     recs, low_rows, high_rows, w_all, w_two, taps, spread):
    s = where_am_i(sc)
    dp = sc[7]
    gather_records(recs, own, other, (got1, got2), (sw1, sw2))
    low_rows[...] = rim_rows(TWO, 0)
    high_rows[...] = rim_rows(TWO, 14)
    for k, w in enumerate((w_a, w_b, w_c, w_d)):
        w_all[k] = w[...]
    for d in range(4):
        at = jnp.bitwise_xor(jnp.int32(d), dp)
        for dx in range(3):
            w_two[dx * 128 + d * 32 : dx * 128 + d * 32 + 32, :] = w_all[
                at, :, dx * 1152 : dx * 1152 + 1152
            ]
    for i in range(3):
        p = s.a + jnp.minimum(i, s.n - 1)
        block, low, high = extended(
            TWO, s, links, recs, (low_rows[...], high_rows[...]),
            red[:, i * 128 : i * 128 + 128].astype(F32), p,
        )

        def store(t, v):
            taps[t * 128 : t * 128 + 128, i * 256 : i * 256 + 256] = v

        tap_rows(TWO, block, low, high, store)
    y = mm(w_two[...], taps[...])
    out[...] = jnp.zeros_like(out)
    for i in range(3):
        p = s.a + jnp.minimum(i, s.n - 1)
        slot = home[p] - 3 * s.dev
        v = three_shifts(TWO, y[:, i * 256 : i * 256 + 256])
        sig = 1.0 / (1.0 + jnp.exp(-v))

        @pl.when(i < s.n)
        def _():
            out[slot] = (v * sig).astype(BF)

        g = cot[slot].astype(F32) * (sig * (1.0 + v * (1.0 - sig))) * scale
        g = jnp.where(i < s.n, g, 0.0).astype(BF).astype(F32)
        g = jnp.concatenate([g, jnp.zeros_like(g)], axis=1)
        for dx in (-1, 0, 1):
            w = g if dx == 0 else pltpu.roll(g, (dx * 16) % 256, 1)
            spread[(dx + 1) * 128 : (dx + 2) * 128, i * 256 : i * 256 + 256] = w.astype(BF)
    whole = mm(spread[...], taps[...], NT)
    for dx in range(3):
        for og in range(2):
            for j in range(9):
                t = (dx * 2 + og) * 9 + j
                row = (t % 2) * 16
                for d in range(4):
                    at = dx * 128 + d * 32 + og * 16
                    dw[t // 2, d, row : row + 16, :] = whole[
                        at : at + 16, j * 128 : j * 128 + 128
                    ].astype(BF)
    dw[27:, :, :, :] = jnp.zeros((5, 4, 32, 128), BF)
    back = mm(w_two[...], spread[...], TN)
    yy, zz = coords(TWO)
    for i in range(3):
        p = s.a + jnp.minimum(i, s.n - 1)
        even = p % 2 == 0
        by_dy = []
        for dy in range(3):
            total = None
            for dz in (-1, 0, 1):
                t = 3 * dy + dz + 1
                v = back[t * 128 : t * 128 + 128, i * 256 : i * 256 + 256]
                if dz == -1:
                    v = pltpu.roll(jnp.where(zz == 0, 0.0, v), 255, 1)
                elif dz == 1:
                    v = pltpu.roll(jnp.where(zz == 1, 0.0, v), 1, 1)
                total = v if total is None else total + v
            by_dy.append(total)
        mid = (
            by_dy[1]
            + pltpu.roll(jnp.where(yy == 0, 0.0, by_dy[0]), 254, 1)
            + pltpu.roll(jnp.where(yy == 7, 0.0, by_dy[2]), 2, 1)
        )
        grad[:, i * 128 : i * 128 + 128] = mid[:, :128]
        rim_low = mm(by_dy[0].astype(BF), low_rows[...], NT).astype(BF)
        rim_high = mm(by_dy[2].astype(BF), high_rows[...], NT).astype(BF)
        xc = jnp.where(even, 0, 7)

        def side(main_to, corner_to):
            def rule(r, l):
                main = (l >= main_to) & (l < main_to + 16) & (r == l - main_to)
                m = l - corner_to
                return main | ((m >= 0) & (m < 16) & (r - 16 == m) & (m // 2 == xc))

            return one_hot((128, 128), rule)

        x_off = jnp.where(even, 0, 112)
        x_pick = one_hot((128, 128), lambda r, l: (l >= 32) & (l < 48) & (r - x_off == l - 32))
        brec[i] = (
            mm(rim_high, side(0, 48))
            + mm(rim_low, side(16, 64))
            + mm(mid[:, 128:].astype(BF), x_pick)
        ).astype(BF)


def stage_three_kernel(sc, links, grad, own, other, got1, got2, sw1, sw2, down, hid, slope, taps,
                       out, recs, gred, g_one, spread, dw):
    s = where_am_i(sc)
    gather_records(recs, own, other, (got1, got2), (sw1, sw2))

    def rows(y_off):
        return one_hot(
            (128, 128), lambda r, l: (r < 32) & (l == ((r % 16) // 2) * 16 + r % 2 + y_off)
        )

    side_rows = (rows(0), rows(14))
    for i in range(3):
        p = s.a + jnp.minimum(i, s.n - 1)
        even = p % 2 == 0
        partner = jnp.where(even, p + 1, p - 1)
        ok_x = x_link(links, p) >= 0
        idx, off = locate_x(s, partner, TWO, 2)
        off = jnp.where(ok_x, off, NOWHERE)
        total = grad[:, i * 128 : i * 128 + 128] + mm(
            recs[idx], picker(TWO, off, jnp.where(even, 112, 0))
        )
        for side, up in ((0, True), (1, False)):
            q = p - 2 if up else p + 2
            c = partner - 2 if up else partner + 2
            ok = link_at(links, p, 2 + side) >= 0
            idx, off, _ = locate(s, q, up, TWO, 2)
            face = mm(recs[idx], picker(TWO, jnp.where(ok, off, NOWHERE), 0))
            ok_c = ok_x & (link_at(links, partner, 2 + side) >= 0)
            idx, _, off = locate(s, c, up, TWO, 2)
            face += mm(recs[idx], picker(TWO, jnp.where(ok_c, off, NOWHERE), 16))
            total += mm(face.astype(BF), side_rows[side])
        gred[:, i * 128 : i * 128 + 128] = jnp.where(i < s.n, total, 0.0).astype(BF)
    dw_down = mm(gred[...], hid[...], NT)
    g_one[...] = (mm(down[...], gred[...], TN) * slope[...]).astype(BF)
    order = parity_order()
    dw[...] = jnp.zeros_like(dw)

    @pl.loop(0, 3)
    def _(i):
        at = pl.ds(pl.multiple_of(i * 128, 128), 128)
        parts = [g_one[e * 64 : e * 64 + 64, at].astype(F32) for e in range(8)]
        tall = jnp.concatenate(swap_groups(parts), axis=0).astype(BF)
        tall = mm(tall, order, NT)
        g = jnp.concatenate(
            [tall[64 * b : 64 * b + 64] for b in range(8)] + [jnp.zeros((64, 128), F32)], axis=1
        )
        for dx in (-1, 0, 1):
            w = g if dx == 0 else pltpu.roll(g, (dx * 64) % 1152, 1)
            spread[(dx + 1) * 64 : (dx + 2) * 64, :] = w.astype(BF)
        dw[...] += mm(spread[...], taps[i], NT)

    for d in range(4):
        for j in range(5):
            for dx in range(3):
                at = dx * 64 + d * 16
                out[dx * 5 + j, d] = dw[at : at + 16, j * 128 : j * 128 + 128].astype(BF)
        for og in range(2):
            for j in range(4):
                at = d * 32 + og * 16
                out[15 + og * 4 + j, d] = dw_down[at : at + 16, j * 128 : j * 128 + 128].astype(BF)
    out[23:, :, :, :] = jnp.zeros((9, 4, 16, 128), BF)


def final_kernel(pieces, one_out, down_out, two_out):
    lane = lax.broadcasted_iota(jnp.int32, (16, 128), 1)
    for dx in range(3):
        for og in range(2):
            for j in range(9):
                t = (dx * 2 + og) * 9 + j
                row = (t % 2) * 16
                two_out[og * 16 : og * 16 + 16, dx * 1152 + j * 128 : dx * 1152 + j * 128 + 128] = (
                    pieces[t // 2, row : row + 16, :].astype(F32)
                )
    for og in range(2):
        for j in range(4):
            down_out[og * 16 : og * 16 + 16, j * 128 : j * 128 + 128] = pieces[
                15 + og * 4 + j, 32:48, :
            ].astype(F32)

    def tile(dx, j):
        return pieces[dx * 5 + j, 32:48, :].astype(F32)

    middle = jnp.concatenate([tile(1, j) for j in range(5)], axis=1)
    middle = pltpu.roll(middle, 64, 1)
    for j in range(4):
        one_out[:, j * 128 : j * 128 + 128] = tile(0, j)
        one_out[:, 1152 + j * 128 : 1280 + j * 128] = tile(2, j)
    one_out[:, 512:640] = jnp.where(lane < 64, tile(0, 4), middle[:, :128])
    one_out[:, 640:1152] = middle[:, 128:]
    one_out[:, 1664:1728] = tile(2, 4)[:, :64]


def call(kernel, scalars, arrays, outs, scratch):
    smem = pl.BlockSpec(memory_space=pltpu.SMEM)
    vmem = pl.BlockSpec(memory_space=pltpu.VMEM)
    return pl.pallas_call(
        kernel,
        out_shape=[jax.ShapeDtypeStruct(*o) for o in outs],
        in_specs=[smem] * len(scalars) + [vmem] * len(arrays),
        out_specs=[vmem] * len(outs),
        scratch_shapes=[pltpu.VMEM(*t) for t in scratch],
        compiler_params=pltpu.CompilerParams(vmem_limit_bytes=60 << 20),
    )(*scalars, *arrays)


def swap_cores(v):
    return lax.ppermute(v, "core", [(0, 1), (1, 0)])


def chips_on(v, by):
    up = [(2 * c, 2 * (c + by)) for c in range(NCHIP - by)]
    down = [(2 * c + 1, 2 * (c - by) + 1) for c in range(by, NCHIP)]
    return lax.ppermute(v, SPACE, up + down)


def across(v, axis, k):
    return lax.ppermute(v, axis, [(i, i ^ k) for i in range(lax.axis_size(axis))])


def exchange(level, sub, sc, own):
    other = swap_cores(own)
    (message,) = call(
        functools.partial(message_kernel, level, sub), (sc,), (own, other),
        [((level.C, level.R), BF)], [((6, level.C, level.R), BF)],
    )
    got1, got2 = chips_on(message, 1), chips_on(message, 2)
    return other, got1, got2, swap_cores(got1), swap_cores(got2)


def gathered(shard):
    return [shard] + [across(shard, "dp", k) for k in (1, 2, 3)]


def scattered(pieces):
    got = lax.all_to_all(pieces, ("x", "y", "core"), 0, 0, tiled=True)
    return got.astype(F32).sum(axis=0).astype(BF)


def on_device(features, cotangent, conv_one, down_weight, conv_two, patch_home, patch_links):
    core, dp = lax.axis_index("core"), lax.axis_index("dp")
    dev = lax.axis_index(SPACE)
    chip = dev // 2
    slots = jnp.arange(8, dtype=jnp.int32)
    marks = jnp.where(slots == 0, -2, jnp.where(slots == 4, 4, slots - 1))
    starts = jnp.sum(
        (patch_home[None, :] < 3 * (2 * chip + marks)[:, None]).astype(jnp.int32), axis=1
    )
    sc = jnp.where(
        slots < 5, starts, jnp.where(slots == 5, dev, jnp.where(slots == 6, core, dp))
    ).astype(jnp.int32)
    links = patch_links.reshape(-1)
    x = features[0]
    (rec_one,) = call(faces_kernel, (sc, patch_home), (x,), [((3, 64, 256), BF)], [])
    rims_one = exchange(ONE, 1, sc, rec_one)
    rows_one = jnp.pad(conv_one.reshape(16, 3, 576).swapaxes(0, 1).reshape(48, 576), ((0, 0), (0, 64)))
    w_one = gathered(jnp.concatenate([rows_one, jnp.pad(down_weight, ((0, 0), (0, 128)))]))
    w_two = gathered(conv_two)
    taps, hid, slope, red, rec_two, down_full = call(
        stage_one_kernel, (sc, patch_home, links),
        (x, rec_one, *rims_one, *w_one),
        [((3, 640, 1152), BF), ((512, 384), BF), ((512, 384), F32), ((128, 384), BF),
         ((3, 128, 128), BF), ((128, 512), BF)],
        [((10, 64, 256), BF), ((128, 1152), BF), ((128, 1152), BF), ((4, 80, 640), BF),
         ((192, 576), BF)],
    )
    rims_two = exchange(TWO, 1, sc, rec_two)
    cells = lax.axis_size("dp") * patch_links.shape[0] * 128
    out, dw_two, grad, rec_back = call(
        functools.partial(stage_two_kernel, float(cells) ** (-0.5)), (sc, patch_home, links),
        (red, cotangent[0], rec_two, *rims_two, *w_two),
        [((3, 128, 128), BF), ((32, 4, 32, 128), BF), ((128, 384), F32), ((3, 128, 128), BF)],
        [((10, 128, 128), BF), ((128, 256), BF), ((128, 256), BF), ((4, 32, 3456), BF),
         ((384, 1152), BF), ((1152, 768), BF), ((384, 768), BF)],
    )
    rims_back = exchange(TWO, 2, sc, rec_back)
    two_sum = scattered(dw_two)
    (small,) = call(
        stage_three_kernel, (sc, links),
        (grad, rec_back, *rims_back, down_full, hid, slope, taps),
        [((32, 4, 16, 128), BF)],
        [((10, 128, 128), BF), ((128, 384), BF), ((512, 384), BF), ((192, 1152), BF),
         ((192, 640), F32)],
    )
    two_sum, small = lax.optimization_barrier((two_sum, small))
    mine = jnp.concatenate([two_sum, scattered(small)], axis=1)
    got = lax.all_to_all(jnp.concatenate([mine, mine]), ("zh", "dp"), 0, 0, tiled=True)
    mine = got.astype(F32).sum(axis=0).astype(BF)
    copies = jnp.broadcast_to(mine[None], (32, *mine.shape))
    pieces = lax.all_to_all(copies, ("x", "y", "core"), 0, 0, tiled=True)
    grads = call(
        final_kernel, (), (pieces,),
        [((16, 1728), F32), ((32, 512), F32), ((32, 3456), F32)], [],
    )
    return (out[None], *grads)


def solution(mesh):
    split = Mesh(
        mesh.devices.reshape(mesh.shape["dp"], 4, 2, 4, 2), ("dp", "x", "zh", "y", "core")
    )
    return jax.shard_map(
        on_device,
        mesh=split,
        in_specs=(
            P("dp", SPACE, None, None),
            P("dp", SPACE, None, None),
            P("dp", None),
            P("dp", None),
            P("dp", None),
            P(),
            P(),
        ),
        out_specs=(P("dp", SPACE, None, None), P("dp", None), P("dp", None), P("dp", None)),
        check_vma=False,
    )
```

profile of v0, /device:TPU:1, one launch (start us, length us, event | category | flops | bytes accessed | tf_op | source)
XLA Modules:
  0.0 158.2 jit_solution(10327483186480667263)
XLA Ops:
  2.1 2.3 %shard_map.102.own = bf16[3,64,256]{2,1,0:T(8,128)(2,1)} custom-call(s32[8]{0:T(128)} %compare_select_fusion.4.sc, s32[128]{0:T(128)} %home.5, bf16[3,64,1024]{2,1,0:T(8,128)(2,1)} %bitcast.5), custom_call_target="tpu_custom_call" | custom-call | tf_op jit(solution)/shard_map/pallas_call | solution.py:516
  4.3 3.2 %collective-permute-start = (bf16[3,64,256]{2,1,0:T(8,128)(2,1)}, bf16[3,64,256]{2,1,0:T(8,128)(2,1)S(1)}, u32[]{:S(2)}, u32[]{:S(2)}) collective-permute-start(bf16[3,64,256]{2,1,0:T(8,128)(2,1)} %shard_map.102.own), channel_id=1, source_target_pairs={{0,1},{1,0},{2,3},{3,2},{4,5},{5,4},{6,7},{7,6},{8,9},{9,8},{10,11... | collective-permute-start | bytes 294920 | tf_op jit(solution)/shard_map/ppermute | solution.py:527
  7.5 0.9 reshape.33
  9.3 2.7 %collective-permute-start.7 = (bf16[80,640]{1,0:T(8,128)(2,1)S(1)}, bf16[80,640]{1,0:T(8,128)(2,1)S(1)}, u32[]{:S(2)}, u32[]{:S(2)}) collective-permute-start(bf16[80,640]{1,0:T(8,128)(2,1)S(1)} %fusion.2.w_a), channel_id=1, source_target_pairs={{0,192},{64,128},{128,64},{192,0},{1,193},{65,129},{129,65},{193,1... | collective-permute-start | bytes 307208 | tf_op jit(solution)/shard_map/ppermute | solution.py:537
  13.6 1.8 %shard_map.103 = bf16[64,256]{1,0:T(8,128)(2,1)} custom-call(s32[8]{0:T(128)} %compare_select_fusion.4.sc, bf16[3,64,256]{2,1,0:T(8,128)(2,1)} %shard_map.102.own, bf16[3,64,256]{2,1,0:T(8,128)(2,1)} %copy-done.1), custom_call_target="tpu_custom_call" | custom-call | tf_op jit(solution)/shard_map/pallas_call | solution.py:516
  15.3 1.3 collective-permute-start.2
  16.6 1.3 collective-permute-start.1
  17.9 1.5 collective-permute-start.14
  19.5 1.1 collective-permute-done.6.w_c
  20.9 2.0 %collective-permute-start.15 = (bf16[32,3456]{1,0:T(8,128)(2,1)}, bf16[32,3456]{1,0:T(8,128)(2,1)S(1)}, u32[]{:S(2)}, u32[]{:S(2)}) collective-permute-start(bf16[32,3456]{1,0:T(8,128)(2,1)} %w_a.1), channel_id=1, source_target_pairs={{0,192},{64,128},{128,64},{192,0},{1,193},{65,129},{129,65},{193,1... | collective-permute-start | bytes 663560 | tf_op jit(solution)/shard_map/ppermute | solution.py:537
  22.9 4.6 %collective-permute-start.4 = (bf16[64,256]{1,0:T(8,128)(2,1)S(1)}, bf16[64,256]{1,0:T(8,128)(2,1)S(1)}, u32[]{:S(2)}, u32[]{:S(2)}) collective-permute-start(bf16[64,256]{1,0:T(8,128)(2,1)S(1)} %collective-permute-done.2.got2), channel_id=1, source_target_pairs={{0,1},{1,0},{2,3},{3,2},{4,5},{5,4},{6,7},{7,6},{8,9},{9,8},{10,11... | collective-permute-start | bytes 98312 | tf_op jit(solution)/shard_map/ppermute | solution.py:527
  30.4 9.8 %shard_map.104 = (bf16[3,640,1152]{2,1,0:T(8,128)(2,1)}, bf16[512,384]{1,0:T(8,128)(2,1)}, f32[512,384]{1,0:T(8,128)}, bf16[128,384]{1,0:T(8,128)(2,1)}, bf16[3,...) custom-call(s32[8]{0:T(128)} %compare_select_fusion.4.sc, s32[128]{0:T(128)} %home.5, s32[512]{0:T(512)} %reshape.32.links, ...), custom_call_target="tpu_custom_call" | custom-call | tf_op jit(solution)/shard_map/pallas_call | solution.py:516
  40.7 1.2 collective-permute-done.8.other
  42.5 1.8 %shard_map.105 = bf16[128,128]{1,0:T(8,128)(2,1)} custom-call(s32[8]{0:T(128)} %compare_select_fusion.4.sc, bf16[3,128,128]{2,1,0:T(8,128)(2,1)} %get-tuple-element.20.own, bf16[3,128,128]{2,1,0:T(8,128)(2,1)} %copy-done.2), custom_call_target="tpu_custom_call" | custom-call | tf_op jit(solution)/shard_map/pallas_call | solution.py:516
  44.2 1.3 collective-permute-start.10
  45.5 1.3 collective-permute-start.9
  46.8 8.1 %collective-permute-done.10.got2 = bf16[128,128]{1,0:T(8,128)(2,1)S(1)} collective-permute-done((bf16[128,128]{1,0:T(8,128)(2,1)}, bf16[128,128]{1,0:T(8,128)(2,1)S(1)}, u32[]{:S(2)}, u32[]{:S(2)}) %collective-permute-start.10) | collective-permute-done | bytes 32800 | tf_op jit(solution)/shard_map/ppermute | solution.py:533
  54.9 2.7 %collective-permute-start.12 = (bf16[128,128]{1,0:T(8,128)(2,1)S(1)}, bf16[128,128]{1,0:T(8,128)(2,1)S(1)}, u32[]{:S(2)}, u32[]{:S(2)}) collective-permute-start(bf16[128,128]{1,0:T(8,128)(2,1)S(1)} %collective-permute-done.10.got2), channel_id=1, source_target_pairs={{0,1},{1,0},{2,3},{3,2},{4,5},{5,4},{6,7},{7,6},{8,9},{9,8},{10,11... | collective-permute-start | bytes 98312 | tf_op jit(solution)/shard_map/ppermute | solution.py:527
  57.6 1.8 %collective-permute-start.11 = (bf16[128,128]{1,0:T(8,128)(2,1)S(1)}, bf16[128,128]{1,0:T(8,128)(2,1)S(1)}, u32[]{:S(2)}, u32[]{:S(2)}) collective-permute-start(bf16[128,128]{1,0:T(8,128)(2,1)S(1)} %collective-permute-done.9.got1), channel_id=1, source_target_pairs={{0,1},{1,0},{2,3},{3,2},{4,5},{5,4},{6,7},{7,6},{8,9},{9,8},{10,11... | collective-permute-start | bytes 98312 | tf_op jit(solution)/shard_map/ppermute | solution.py:527
  60.9 7.5 %shard_map.106 = (bf16[3,128,128]{2,1,0:T(8,128)(2,1)}, bf16[32,4,32,128]{3,2,1,0:T(8,128)(2,1)}, f32[128,384]{1,0:T(8,128)}, bf16[3,128,128]{2,1,0:T(8,128)(2,1)}) custom-call(s32[8]{0:T(128)} %compare_select_fusion.4.sc, s32[128]{0:T(128)} %home.5, s32[512]{0:T(512)} %reshape.32.links, bf16[128,384]{1,0:T(8,128)(2,1)} %get-tuple-element.19.red, ...), custom_call_target="tpu_custom_call" | custom-call | tf_op jit(solution)/shard_map/pallas_call | solution.py:516
  68.4 12.4 %all-to-all-start = ((bf16[32,4,32,128]{3,2,1,0:T(8,128)(2,1)}), bf16[32,4,32,128]{3,2,1,0:T(8,128)(2,1)S(1)}, u32[]{:S(2)}, u32[]{:S(2)}) async-start(bf16[32,4,32,128]{3,2,1,0:T(8,128)(2,1)} %get-tuple-element.22), calls=%async_computation | async-start | bytes 2097152 | tf_op jit(solution)/shard_map/all_to_all | solution.py:555
  81.0 1.3 collective-permute-done.16.other
  83.0 1.9 %shard_map.107 = bf16[128,128]{1,0:T(8,128)(2,1)} custom-call(s32[8]{0:T(128)} %compare_select_fusion.4.sc, bf16[3,128,128]{2,1,0:T(8,128)(2,1)} %get-tuple-element.24.own, bf16[3,128,128]{2,1,0:T(8,128)(2,1)} %copy-done.3), custom_call_target="tpu_custom_call" | custom-call | tf_op jit(solution)/shard_map/pallas_call | solution.py:516
  84.8 1.3 collective-permute-start.18
  86.1 1.3 collective-permute-start.17
  87.4 5.6 %collective-permute-done.18.got2 = bf16[128,128]{1,0:T(8,128)(2,1)S(1)} collective-permute-done((bf16[128,128]{1,0:T(8,128)(2,1)}, bf16[128,128]{1,0:T(8,128)(2,1)S(1)}, u32[]{:S(2)}, u32[]{:S(2)}) %collective-permute-start.18) | collective-permute-done | bytes 32800 | tf_op jit(solution)/shard_map/ppermute | solution.py:533
  93.0 1.6 %collective-permute-start.19 = (bf16[128,128]{1,0:T(8,128)(2,1)S(1)}, bf16[128,128]{1,0:T(8,128)(2,1)S(1)}, u32[]{:S(2)}, u32[]{:S(2)}) collective-permute-start(bf16[128,128]{1,0:T(8,128)(2,1)S(1)} %collective-permute-done.17.got1), channel_id=1, source_target_pairs={{0,1},{1,0},{2,3},{3,2},{4,5},{5,4},{6,7},{7,6},{8,9},{9,8},{10,11... | collective-permute-start | bytes 98312 | tf_op jit(solution)/shard_map/ppermute | solution.py:527
  96.1 8.2 %shard_map.108 = bf16[32,4,16,128]{3,2,1,0:T(8,128)(2,1)} custom-call(s32[8]{0:T(128)} %compare_select_fusion.4.sc, s32[512]{0:T(512)} %reshape.32.links, f32[128,384]{1,0:T(8,128)} %get-tuple-element.23.grad, bf16[3,128,128]{2,1,0:T(8,128)(2,1)} %get-tuple-element.24.own, bf16[3,128,128]{2,1,0:T(8,128)(2,1)} %copy-done.3, bf16[128,128]{1,0:T(8,128)(2,1)} %copy-done.11, ...), custom_call_target="tpu_custom_call" | custom-call | tf_op jit(solution)/shard_map/pallas_call | solution.py:516
  104.5 24.9 %all_to_all.20 = bf16[32,4,16,128]{3,2,1,0:T(8,128)(2,1)S(1)} all-to-all(bf16[32,4,16,128]{3,2,1,0:T(8,128)(2,1)} %shard_map.108), channel_id=1, replica_groups=mesh['dp'=4,'x'=4,'zh'=2,'y'=4,'core'=2] {'x','y','core'}, dimensions={0} | all-to-all | bytes 1048576 | tf_op jit(solution)/shard_map/all_to_all | solution.py:555
  129.5 11.9 %all_to_all.21 = bf16[8,48,128]{2,1,0:T(8,128)(2,1)S(1)} all-to-all(bf16[8,48,128]{2,1,0:T(8,128)(2,1)S(1)} %maximum_maximum_fusion), channel_id=1, replica_groups=mesh['dp'=4,'x'=4,'zh'=2,'y'=4,'core'=2] {'zh','dp'}, dimensions={0} | all-to-all | bytes 196608 | tf_op jit(solution)/shard_map/all_to_all | solution.py:606
  141.5 14.8 %all_to_all.22.pieces = bf16[32,48,128]{2,1,0:T(8,128)(2,1)} all-to-all(bf16[32,48,128]{2,1,0:T(8,128)(2,1)S(1)} %broadcast_in_dim.33), channel_id=1, replica_groups=mesh['dp'=4,'x'=4,'zh'=2,'y'=4,'core'=2] {'x','y','core'}, dimensions={0} | all-to-all | bytes 786432 | tf_op jit(solution)/shard_map/all_to_all | solution.py:609
  156.4 1.8 %shard_map.109 = (f32[16,1728]{1,0:T(8,128)}, f32[32,512]{1,0:T(8,128)}, f32[32,3456]{1,0:T(8,128)}) custom-call(bf16[32,48,128]{2,1,0:T(8,128)(2,1)} %all_to_all.22.pieces), custom_call_target="tpu_custom_call" | custom-call | tf_op jit(solution)/shard_map/pallas_call | solution.py:516
  (80 shorter events, 12.2 us)
Async XLA Ops:
  4.3 8.6 %collective-permute-start = (bf16[3,64,256]{2,1,0:T(8,128)(2,1)}, bf16[3,64,256]{2,1,0:T(8,128)(2,1)S(1)}, u32[]{:S(2)}, u32[]{:S(2)}) collective-permute-start(bf16[3,64,256]{2,1,0:T(8,128)(2,1)} %shard_map.102.own), channel_id=1, source_target_pairs={{0,1},{1,0},{2,3},{3,2},{4,5},{5,4},{6,7},{7,6},{8,9},{9,8},{10,11... | collective-permute-start | bytes 294920 | tf_op jit(solution)/shard_map/ppermute | solution.py:527
  9.3 19.9 %copy-start = (bf16[80,640]{1,0:T(8,128)(2,1)}, bf16[80,640]{1,0:T(8,128)(2,1)S(1)}, u32[]{:S(2)}) copy-start(bf16[80,640]{1,0:T(8,128)(2,1)S(1)} %fusion.2.w_a) | copy-start | bytes 307204
  9.3 8.6 %collective-permute-start.7 = (bf16[80,640]{1,0:T(8,128)(2,1)S(1)}, bf16[80,640]{1,0:T(8,128)(2,1)S(1)}, u32[]{:S(2)}, u32[]{:S(2)}) collective-permute-start(bf16[80,640]{1,0:T(8,128)(2,1)S(1)} %fusion.2.w_a), channel_id=1, source_target_pairs={{0,192},{64,128},{128,64},{192,0},{1,193},{65,129},{129,65},{193,1... | collective-permute-start | bytes 307208 | tf_op jit(solution)/shard_map/ppermute | solution.py:537
  12.0 8.5 %collective-permute-start.6 = (bf16[80,640]{1,0:T(8,128)(2,1)S(1)}, bf16[80,640]{1,0:T(8,128)(2,1)S(1)}, u32[]{:S(2)}, u32[]{:S(2)}) collective-permute-start(bf16[80,640]{1,0:T(8,128)(2,1)S(1)} %fusion.2.w_a), channel_id=1, source_target_pairs={{0,128},{64,192},{128,0},{192,64},{1,129},{65,193},{129,1},{193,65... | collective-permute-start | bytes 307208 | tf_op jit(solution)/shard_map/ppermute | solution.py:537
  12.0 8.9 %collective-permute-start.5 = (bf16[80,640]{1,0:T(8,128)(2,1)S(1)}, bf16[80,640]{1,0:T(8,128)(2,1)S(1)}, u32[]{:S(2)}, u32[]{:S(2)}) collective-permute-start(bf16[80,640]{1,0:T(8,128)(2,1)S(1)} %fusion.2.w_a), channel_id=1, source_target_pairs={{0,64},{64,0},{128,192},{192,128},{1,65},{65,1},{129,193},{193,129... | collective-permute-start | bytes 307208 | tf_op jit(solution)/shard_map/ppermute | solution.py:537
  15.3 7.6 %collective-permute-start.2 = (bf16[64,256]{1,0:T(8,128)(2,1)}, bf16[64,256]{1,0:T(8,128)(2,1)S(1)}, u32[]{:S(2)}, u32[]{:S(2)}) collective-permute-start(bf16[64,256]{1,0:T(8,128)(2,1)} %shard_map.103), channel_id=1, source_target_pairs={{0,4},{2,6},{4,8},{6,10},{8,12},{10,14},{12,16},{14,18},{16,20},{1... | collective-permute-start | bytes 98312 | tf_op jit(solution)/shard_map/ppermute | solution.py:533
  16.6 11.0 %collective-permute-start.1 = (bf16[64,256]{1,0:T(8,128)(2,1)}, bf16[64,256]{1,0:T(8,128)(2,1)S(1)}, u32[]{:S(2)}, u32[]{:S(2)}) collective-permute-start(bf16[64,256]{1,0:T(8,128)(2,1)} %shard_map.103), channel_id=1, source_target_pairs={{0,2},{2,4},{4,6},{6,8},{8,10},{10,12},{12,14},{14,16},{16,18},{18... | collective-permute-start | bytes 98312 | tf_op jit(solution)/shard_map/ppermute | solution.py:533
  17.9 11.3 %copy-start.7 = (bf16[80,640]{1,0:T(8,128)(2,1)}, bf16[80,640]{1,0:T(8,128)(2,1)S(1)}, u32[]{:S(2)}) copy-start(bf16[80,640]{1,0:T(8,128)(2,1)S(1)} %collective-permute-done.7.w_d) | copy-start | bytes 307204
  17.9 41.5 %collective-permute-start.14 = (bf16[32,3456]{1,0:T(8,128)(2,1)}, bf16[32,3456]{1,0:T(8,128)(2,1)S(1)}, u32[]{:S(2)}, u32[]{:S(2)}) collective-permute-start(bf16[32,3456]{1,0:T(8,128)(2,1)} %w_a.1), channel_id=1, source_target_pairs={{0,128},{64,192},{128,0},{192,64},{1,129},{65,193},{129,1},{193,65... | collective-permute-start | bytes 663560 | tf_op jit(solution)/shard_map/ppermute | solution.py:537
  20.5 8.7 %copy-start.8 = (bf16[80,640]{1,0:T(8,128)(2,1)}, bf16[80,640]{1,0:T(8,128)(2,1)S(1)}, u32[]{:S(2)}) copy-start(bf16[80,640]{1,0:T(8,128)(2,1)S(1)} %collective-permute-done.6.w_c) | copy-start | bytes 307204
  20.5 38.9 %collective-permute-start.13 = (bf16[32,3456]{1,0:T(8,128)(2,1)}, bf16[32,3456]{1,0:T(8,128)(2,1)S(1)}, u32[]{:S(2)}, u32[]{:S(2)}) collective-permute-start(bf16[32,3456]{1,0:T(8,128)(2,1)} %w_a.1), channel_id=1, source_target_pairs={{0,64},{64,0},{128,192},{192,128},{1,65},{65,1},{129,193},{193,129... | collective-permute-start | bytes 663560 | tf_op jit(solution)/shard_map/ppermute | solution.py:537
  20.9 8.3 %copy-start.9 = (bf16[80,640]{1,0:T(8,128)(2,1)}, bf16[80,640]{1,0:T(8,128)(2,1)S(1)}, u32[]{:S(2)}) copy-start(bf16[80,640]{1,0:T(8,128)(2,1)S(1)} %collective-permute-done.5.w_b) | copy-start | bytes 307204
  20.9 38.5 %collective-permute-start.15 = (bf16[32,3456]{1,0:T(8,128)(2,1)}, bf16[32,3456]{1,0:T(8,128)(2,1)S(1)}, u32[]{:S(2)}, u32[]{:S(2)}) collective-permute-start(bf16[32,3456]{1,0:T(8,128)(2,1)} %w_a.1), channel_id=1, source_target_pairs={{0,192},{64,128},{128,64},{192,0},{1,193},{65,129},{129,65},{193,1... | collective-permute-start | bytes 663560 | tf_op jit(solution)/shard_map/ppermute | solution.py:537
  22.9 6.3 %copy-start.14 = (bf16[64,256]{1,0:T(8,128)(2,1)}, bf16[64,256]{1,0:T(8,128)(2,1)S(1)}, u32[]{:S(2)}) copy-start(bf16[64,256]{1,0:T(8,128)(2,1)S(1)} %collective-permute-done.2.got2) | copy-start | bytes 98308
  22.9 6.2 %collective-permute-start.4 = (bf16[64,256]{1,0:T(8,128)(2,1)S(1)}, bf16[64,256]{1,0:T(8,128)(2,1)S(1)}, u32[]{:S(2)}, u32[]{:S(2)}) collective-permute-start(bf16[64,256]{1,0:T(8,128)(2,1)S(1)} %collective-permute-done.2.got2), channel_id=1, source_target_pairs={{0,1},{1,0},{2,3},{3,2},{4,5},{5,4},{6,7},{7,6},{8,9},{9,8},{10,11... | collective-permute-start | bytes 98312 | tf_op jit(solution)/shard_map/ppermute | solution.py:527
  27.6 1.7 %copy-start.15 = (bf16[64,256]{1,0:T(8,128)(2,1)}, bf16[64,256]{1,0:T(8,128)(2,1)S(1)}, u32[]{:S(2)}) copy-start(bf16[64,256]{1,0:T(8,128)(2,1)S(1)} %collective-permute-done.1.got1) | copy-start | bytes 98308
  27.6 1.6 %collective-permute-start.3 = (bf16[64,256]{1,0:T(8,128)(2,1)S(1)}, bf16[64,256]{1,0:T(8,128)(2,1)S(1)}, u32[]{:S(2)}, u32[]{:S(2)}) collective-permute-start(bf16[64,256]{1,0:T(8,128)(2,1)S(1)} %collective-permute-done.1.got1), channel_id=1, source_target_pairs={{0,1},{1,0},{2,3},{3,2},{4,5},{5,4},{6,7},{7,6},{8,9},{9,8},{10,11... | collective-permute-start | bytes 98312 | tf_op jit(solution)/shard_map/ppermute | solution.py:527
  40.2 1.6 %collective-permute-start.8 = (bf16[3,128,128]{2,1,0:T(8,128)(2,1)}, bf16[3,128,128]{2,1,0:T(8,128)(2,1)S(1)}, u32[]{:S(2)}, u32[]{:S(2)}) collective-permute-start(bf16[3,128,128]{2,1,0:T(8,128)(2,1)} %get-tuple-element.20.own), channel_id=1, source_target_pairs={{0,1},{1,0},{2,3},{3,2},{4,5},{5,4},{6,7},{7,6},{8,9},{9,8},{10,11... | collective-permute-start | bytes 294920 | tf_op jit(solution)/shard_map/ppermute | solution.py:527
  44.2 10.7 %collective-permute-start.10 = (bf16[128,128]{1,0:T(8,128)(2,1)}, bf16[128,128]{1,0:T(8,128)(2,1)S(1)}, u32[]{:S(2)}, u32[]{:S(2)}) collective-permute-start(bf16[128,128]{1,0:T(8,128)(2,1)} %shard_map.105), channel_id=1, source_target_pairs={{0,4},{2,6},{4,8},{6,10},{8,12},{10,14},{12,16},{14,18},{16,20},{1... | collective-permute-start | bytes 98312 | tf_op jit(solution)/shard_map/ppermute | solution.py:533
  45.5 12.1 %collective-permute-start.9 = (bf16[128,128]{1,0:T(8,128)(2,1)}, bf16[128,128]{1,0:T(8,128)(2,1)S(1)}, u32[]{:S(2)}, u32[]{:S(2)}) collective-permute-start(bf16[128,128]{1,0:T(8,128)(2,1)} %shard_map.105), channel_id=1, source_target_pairs={{0,2},{2,4},{4,6},{6,8},{8,10},{10,12},{12,14},{14,16},{16,18},{18... | collective-permute-start | bytes 98312 | tf_op jit(solution)/shard_map/ppermute | solution.py:533
  54.9 5.4 %copy-start.16 = (bf16[128,128]{1,0:T(8,128)(2,1)}, bf16[128,128]{1,0:T(8,128)(2,1)S(1)}, u32[]{:S(2)}) copy-start(bf16[128,128]{1,0:T(8,128)(2,1)S(1)} %collective-permute-done.10.got2) | copy-start | bytes 98308
  54.9 4.6 %collective-permute-start.12 = (bf16[128,128]{1,0:T(8,128)(2,1)S(1)}, bf16[128,128]{1,0:T(8,128)(2,1)S(1)}, u32[]{:S(2)}, u32[]{:S(2)}) collective-permute-start(bf16[128,128]{1,0:T(8,128)(2,1)S(1)} %collective-permute-done.10.got2), channel_id=1, source_target_pairs={{0,1},{1,0},{2,3},{3,2},{4,5},{5,4},{6,7},{7,6},{8,9},{9,8},{10,11... | collective-permute-start | bytes 98312 | tf_op jit(solution)/shard_map/ppermute | solution.py:527
  57.6 2.7 %copy-start.17 = (bf16[128,128]{1,0:T(8,128)(2,1)}, bf16[128,128]{1,0:T(8,128)(2,1)S(1)}, u32[]{:S(2)}) copy-start(bf16[128,128]{1,0:T(8,128)(2,1)S(1)} %collective-permute-done.9.got1) | copy-start | bytes 98308
  57.6 2.6 %collective-permute-start.11 = (bf16[128,128]{1,0:T(8,128)(2,1)S(1)}, bf16[128,128]{1,0:T(8,128)(2,1)S(1)}, u32[]{:S(2)}, u32[]{:S(2)}) collective-permute-start(bf16[128,128]{1,0:T(8,128)(2,1)S(1)} %collective-permute-done.9.got1), channel_id=1, source_target_pairs={{0,1},{1,0},{2,3},{3,2},{4,5},{5,4},{6,7},{7,6},{8,9},{9,8},{10,11... | collective-permute-start | bytes 98312 | tf_op jit(solution)/shard_map/ppermute | solution.py:527
  68.4 36.0 %all-to-all-start = ((bf16[32,4,32,128]{3,2,1,0:T(8,128)(2,1)}), bf16[32,4,32,128]{3,2,1,0:T(8,128)(2,1)S(1)}, u32[]{:S(2)}, u32[]{:S(2)}) async-start(bf16[32,4,32,128]{3,2,1,0:T(8,128)(2,1)} %get-tuple-element.22), calls=%async_computation | async-start | bytes 2097152 | tf_op jit(solution)/shard_map/all_to_all | solution.py:555
  80.7 1.6 %collective-permute-start.16 = (bf16[3,128,128]{2,1,0:T(8,128)(2,1)}, bf16[3,128,128]{2,1,0:T(8,128)(2,1)S(1)}, u32[]{:S(2)}, u32[]{:S(2)}) collective-permute-start(bf16[3,128,128]{2,1,0:T(8,128)(2,1)} %get-tuple-element.24.own), channel_id=1, source_target_pairs={{0,1},{1,0},{2,3},{3,2},{4,5},{5,4},{6,7},{7,6},{8,9},{9,8},{10,11... | collective-permute-start | bytes 294920 | tf_op jit(solution)/shard_map/ppermute | solution.py:527
  84.8 8.2 %collective-permute-start.18 = (bf16[128,128]{1,0:T(8,128)(2,1)}, bf16[128,128]{1,0:T(8,128)(2,1)S(1)}, u32[]{:S(2)}, u32[]{:S(2)}) collective-permute-start(bf16[128,128]{1,0:T(8,128)(2,1)} %shard_map.107), channel_id=1, source_target_pairs={{0,4},{2,6},{4,8},{6,10},{8,12},{10,14},{12,16},{14,18},{16,20},{1... | collective-permute-start | bytes 98312 | tf_op jit(solution)/shard_map/ppermute | solution.py:533
  86.1 6.9 %collective-permute-start.17 = (bf16[128,128]{1,0:T(8,128)(2,1)}, bf16[128,128]{1,0:T(8,128)(2,1)S(1)}, u32[]{:S(2)}, u32[]{:S(2)}) collective-permute-start(bf16[128,128]{1,0:T(8,128)(2,1)} %shard_map.107), channel_id=1, source_target_pairs={{0,2},{2,4},{4,6},{6,8},{8,10},{10,12},{12,14},{14,16},{16,18},{18... | collective-permute-start | bytes 98312 | tf_op jit(solution)/shard_map/ppermute | solution.py:533
  93.0 2.5 %copy-start.10 = (bf16[128,128]{1,0:T(8,128)(2,1)}, bf16[128,128]{1,0:T(8,128)(2,1)S(1)}, u32[]{:S(2)}) copy-start(bf16[128,128]{1,0:T(8,128)(2,1)S(1)} %collective-permute-done.18.got2) | copy-start | bytes 98308
  93.0 1.6 %collective-permute-start.20 = (bf16[128,128]{1,0:T(8,128)(2,1)S(1)}, bf16[128,128]{1,0:T(8,128)(2,1)S(1)}, u32[]{:S(2)}, u32[]{:S(2)}) collective-permute-start(bf16[128,128]{1,0:T(8,128)(2,1)S(1)} %collective-permute-done.18.got2), channel_id=1, source_target_pairs={{0,1},{1,0},{2,3},{3,2},{4,5},{5,4},{6,7},{7,6},{8,9},{9,8},{10,11... | collective-permute-start | bytes 98312 | tf_op jit(solution)/shard_map/ppermute | solution.py:527
  93.0 2.5 %copy-start.11 = (bf16[128,128]{1,0:T(8,128)(2,1)}, bf16[128,128]{1,0:T(8,128)(2,1)S(1)}, u32[]{:S(2)}) copy-start(bf16[128,128]{1,0:T(8,128)(2,1)S(1)} %collective-permute-done.17.got1) | copy-start | bytes 98308
  93.0 2.5 %collective-permute-start.19 = (bf16[128,128]{1,0:T(8,128)(2,1)S(1)}, bf16[128,128]{1,0:T(8,128)(2,1)S(1)}, u32[]{:S(2)}, u32[]{:S(2)}) collective-permute-start(bf16[128,128]{1,0:T(8,128)(2,1)S(1)} %collective-permute-done.17.got1), channel_id=1, source_target_pairs={{0,1},{1,0},{2,3},{3,2},{4,5},{5,4},{6,7},{7,6},{8,9},{9,8},{10,11... | collective-permute-start | bytes 98312 | tf_op jit(solution)/shard_map/ppermute | solution.py:527
  (12 other events, 8.6 us)
where the time goes:
time: 159 us; the launch traced here: 158 us
  blocking collectives  51.7 us (33%)
  starting transfers between devices  42.5 us (27%)
  Pallas kernels  35 us (22%)
  waiting for transfers between devices  18.9 us (12%)
  local copies, waits for them, and re-layouts  6.75 us (4%)
  other arithmetic  2.47 us (2%)
    pallas_call x8, Pallas kernels, call(): pl.pallas_call(kernel, out_shape=[jax.ShapeDtypeStruct(*o) for o in outs]...  35 us
    all_to_all x1, blocking collectives, scattered(): got = lax.all_to_all(pieces, ('x', 'y', 'core'), 0, 0, tiled=True)  24.9 us
    all_to_all x1, blocking collectives, on_device(): pieces = lax.all_to_all(copies, ('x', 'y', 'core'), 0, 0, tiled=True)  14.8 us
    ppermute x9, starting transfers between devices, swap_cores(): return lax.ppermute(v, 'core', [(0, 1), (1, 0)])  14.8 us
    ppermute x6, waiting for transfers between devices, chips_on(): return lax.ppermute(v, SPACE, up + down)  13.7 us
    all_to_all x1, starting transfers between devices, scattered(): got = lax.all_to_all(pieces, ('x', 'y', 'core'), 0, 0, tiled=True)  12.4 us
    all_to_all x1, blocking collectives, on_device(): lax.all_to_all(jnp.concatenate([mine, mine]), ('zh', 'dp'), 0, 0, tiled=T...  11.9 us
    ppermute x6, starting transfers between devices, chips_on(): return lax.ppermute(v, SPACE, up + down)  7.72 us
  transfers between devices with their start and end apart: 22, of which 7 were waited for; matrix products, arithmetic and copies ran while one was open for 2% of the time, Pallas kernels for 15%

commit v1 on v0

--- a/solution.py
+++ b/solution.py
@@ -8,7 +8,6 @@
 from jax.experimental.pallas import tpu as pltpu
 from jax.sharding import Mesh
 from jax.sharding import PartitionSpec as P
-
 
 BF = jnp.bfloat16
 F32 = jnp.float32
@@ -125,7 +124,7 @@
 
 
 def link_at(links, q, column):
-    return links[jnp.clip(q, 0, 127) * 4 + column]
+    return links[column, jnp.clip(q, 0, 127)]
 
 
 def x_link(links, q):
@@ -364,16 +363,12 @@
             spread[(dx + 1) * 128 : (dx + 2) * 128, i * 256 : i * 256 + 256] = w.astype(BF)
     whole = mm(spread[...], taps[...], NT)
     for dx in range(3):
-        for og in range(2):
-            for j in range(9):
-                t = (dx * 2 + og) * 9 + j
-                row = (t % 2) * 16
+        for j in range(9):
+            for og in range(2):
                 for d in range(4):
                     at = dx * 128 + d * 32 + og * 16
-                    dw[t // 2, d, row : row + 16, :] = whole[
-                        at : at + 16, j * 128 : j * 128 + 128
-                    ].astype(BF)
-    dw[27:, :, :, :] = jnp.zeros((5, 4, 32, 128), BF)
+                    dw[og, dx * 9 + j, d] = whole[at : at + 16, j * 128 : j * 128 + 128].astype(BF)
+    dw[:, 27:, :, :, :] = jnp.zeros((2, 5, 4, 16, 128), BF)
     back = mm(w_two[...], spread[...], TN)
     yy, zz = coords(TWO)
     for i in range(3):
@@ -419,7 +414,7 @@
 
 
 def stage_three_kernel(sc, links, grad, own, other, got1, got2, sw1, sw2, down, hid, slope, taps,
-                       out, recs, gred, g_one, spread, dw):
+                       two, out, recs, gred, g_one, spread, dw):
     s = where_am_i(sc)
     gather_records(recs, own, other, (got1, got2), (sw1, sw2))
 
@@ -473,12 +468,37 @@
         for j in range(5):
             for dx in range(3):
                 at = dx * 64 + d * 16
-                out[dx * 5 + j, d] = dw[at : at + 16, j * 128 : j * 128 + 128].astype(BF)
+                out[dx * 5 + j, d, 0:16, :] = dw[at : at + 16, j * 128 : j * 128 + 128].astype(BF)
         for og in range(2):
             for j in range(4):
                 at = d * 32 + og * 16
-                out[15 + og * 4 + j, d] = dw_down[at : at + 16, j * 128 : j * 128 + 128].astype(BF)
-    out[23:, :, :, :] = jnp.zeros((9, 4, 16, 128), BF)
+                out[15 + og * 4 + j, d, 0:16, :] = dw_down[
+                    at : at + 16, j * 128 : j * 128 + 128
+                ].astype(BF)
+    out[23:, :, 0:16, :] = jnp.zeros((9, 4, 16, 128), BF)
+    out[:, :, 16:32, :] = two[...]
+
+
+def sum_kernel(got, out):
+    for d in range(4):
+        small, halves = [None, None], [None, None]
+        for k in range(32):
+            v = got[k, d].astype(F32)
+            h = k % 2
+            small[h] = v[:16] if small[h] is None else small[h] + v[:16]
+            halves[h] = v[16:] if halves[h] is None else halves[h] + v[16:]
+        total = jnp.concatenate([small[0] + small[1], halves[0], halves[1]], axis=0).astype(BF)
+        out[d] = total
+        out[4 + d] = total
+
+
+def spread_kernel(got, out):
+    total = got[0].astype(F32)
+    for k in range(1, 8):
+        total += got[k].astype(F32)
+    total = total.astype(BF)
+    for k in range(32):
+        out[k] = total
 
 
 def final_kernel(pieces, one_out, down_out, two_out):
@@ -486,19 +506,17 @@
     for dx in range(3):
         for og in range(2):
             for j in range(9):
-                t = (dx * 2 + og) * 9 + j
-                row = (t % 2) * 16
                 two_out[og * 16 : og * 16 + 16, dx * 1152 + j * 128 : dx * 1152 + j * 128 + 128] = (
-                    pieces[t // 2, row : row + 16, :].astype(F32)
+                    pieces[dx * 9 + j, 16 + og * 16 : 32 + og * 16, :].astype(F32)
                 )
     for og in range(2):
         for j in range(4):
             down_out[og * 16 : og * 16 + 16, j * 128 : j * 128 + 128] = pieces[
-                15 + og * 4 + j, 32:48, :
+                15 + og * 4 + j, 0:16, :
             ].astype(F32)
 
     def tile(dx, j):
-        return pieces[dx * 5 + j, 32:48, :].astype(F32)
+        return pieces[dx * 5 + j, 0:16, :].astype(F32)
 
     middle = jnp.concatenate([tile(1, j) for j in range(5)], axis=1)
     middle = pltpu.roll(middle, 64, 1)
@@ -551,11 +569,6 @@
     return [shard] + [across(shard, "dp", k) for k in (1, 2, 3)]
 
 
-def scattered(pieces):
-    got = lax.all_to_all(pieces, ("x", "y", "core"), 0, 0, tiled=True)
-    return got.astype(F32).sum(axis=0).astype(BF)
-
-
 def on_device(features, cotangent, conv_one, down_weight, conv_two, patch_home, patch_links):
     core, dp = lax.axis_index("core"), lax.axis_index("dp")
     dev = lax.axis_index(SPACE)
@@ -568,7 +581,7 @@
     sc = jnp.where(
         slots < 5, starts, jnp.where(slots == 5, dev, jnp.where(slots == 6, core, dp))
     ).astype(jnp.int32)
-    links = patch_links.reshape(-1)
+    links = patch_links.T
     x = features[0]
     (rec_one,) = call(faces_kernel, (sc, patch_home), (x,), [((3, 64, 256), BF)], [])
     rims_one = exchange(ONE, 1, sc, rec_one)
@@ -588,24 +601,25 @@
     out, dw_two, grad, rec_back = call(
         functools.partial(stage_two_kernel, float(cells) ** (-0.5)), (sc, patch_home, links),
         (red, cotangent[0], rec_two, *rims_two, *w_two),
-        [((3, 128, 128), BF), ((32, 4, 32, 128), BF), ((128, 384), F32), ((3, 128, 128), BF)],
+        [((3, 128, 128), BF), ((2, 32, 4, 16, 128), BF), ((128, 384), F32), ((3, 128, 128), BF)],
         [((10, 128, 128), BF), ((128, 256), BF), ((128, 256), BF), ((4, 32, 3456), BF),
          ((384, 1152), BF), ((1152, 768), BF), ((384, 768), BF)],
     )
     rims_back = exchange(TWO, 2, sc, rec_back)
-    two_sum = scattered(dw_two)
+    keep = lax.dynamic_index_in_dim(dw_two, core, 0, keepdims=False)
+    give = lax.dynamic_index_in_dim(dw_two, 1 - core, 0, keepdims=False)
+    two_part = (keep.astype(F32) + swap_cores(give).astype(F32)).astype(BF)
     (small,) = call(
         stage_three_kernel, (sc, links),
-        (grad, rec_back, *rims_back, down_full, hid, slope, taps),
-        [((32, 4, 16, 128), BF)],
+        (grad, rec_back, *rims_back, down_full, hid, slope, taps, two_part),
+        [((32, 4, 32, 128), BF)],
         [((10, 128, 128), BF), ((128, 384), BF), ((512, 384), BF), ((192, 1152), BF),
          ((192, 640), F32)],
     )
-    two_sum, small = lax.optimization_barrier((two_sum, small))
-    mine = jnp.concatenate([two_sum, scattered(small)], axis=1)
-    got = lax.all_to_all(jnp.concatenate([mine, mine]), ("zh", "dp"), 0, 0, tiled=True)
-    mine = got.astype(F32).sum(axis=0).astype(BF)
-    copies = jnp.broadcast_to(mine[None], (32, *mine.shape))
+    got = lax.all_to_all(small, ("x", "y", "core"), 0, 0, tiled=True)
+    (mine,) = call(sum_kernel, (), (got,), [((8, 48, 128), BF)], [])
+    got = lax.all_to_all(mine, ("zh", "dp"), 0, 0, tiled=True)
+    (copies,) = call(spread_kernel, (), (got,), [((32, 48, 128), BF)], [])
     pieces = lax.all_to_all(copies, ("x", "y", "core"), 0, 0, tiled=True)
     grads = call(
         final_kernel, (), (pieces,),

time: 159 us -> 165 us (1.038)
  blocking collectives: 51.7 us -> 60.1 us
  starting transfers between devices: 42.5 us -> 38.9 us
  waiting for transfers between devices: 18.9 us -> 15.7 us
  Pallas kernels: 35 us -> 38.1 us
  other arithmetic: 2.47 us -> 4.18 us
    all_to_all x1 -> x0, starting transfers between devices: 12.4 us -> none  [scattered(): got = lax.all_to_all(pieces, ('x', 'y', 'core'), 0, 0, tiled=True)]
    ppermute x9 -> x10, starting transfers between devices: 14.8 us -> 23.5 us  [swap_cores(): return lax.ppermute(v, 'core', [(0, 1), (1, 0)])]
    all_to_all x2, blocking collectives: 36.9 us -> 43.8 us  [the longest x1 29.7 us: on_device(): got = lax.all_to_all(small, ('x', 'y', 'core'), 0, 0, tiled=True)]
    pallas_call x8 -> x10, Pallas kernels: 35 us -> 38.1 us  [call(): pl.pallas_call(kernel, out_shape=[jax.ShapeDtypeStruct(*o) for o in outs]...]
    ppermute x6, waiting for transfers between devices: 13.7 us -> 10.9 us  [chips_on(): return lax.ppermute(v, SPACE, up + down)]
    convert_element_type x0 -> x1, other arithmetic: none -> 2.03 us  [on_device(): two_part = (keep.astype(F32) + swap_cores(give).astype(F32)).astype(BF)]
    unnamed x45 -> x44, local copies, waits for them, and re-layouts: 5.07 us -> 3.7 us
    ppermute x9 -> x10, waiting for transfers between devices: 4.1 us -> 4.79 us  [swap_cores(): return lax.ppermute(v, 'core', [(0, 1), (1, 0)])]
  transfers between devices with their start and end apart: 22 -> 22, of which waited for: 7 -> 7; matrix products, arithmetic and copies ran while one was open for 2% -> 2% of each run, Pallas kernels for 15% -> 9%
where the time goes in v1:
time: 165 us; the launch traced here: 164 us
  blocking collectives  60.1 us (36%)
  starting transfers between devices  38.9 us (24%)
  Pallas kernels  38.1 us (23%)
  waiting for transfers between devices  15.7 us (10%)
  local copies, waits for them, and re-layouts  5.7 us (3%)
  other arithmetic  4.18 us (3%)
    pallas_call x10, Pallas kernels, call(): pl.pallas_call(kernel, out_shape=[jax.ShapeDtypeStruct(*o) for o in outs]...  38.1 us
    all_to_all x1, blocking collectives, on_device(): got = lax.all_to_all(small, ('x', 'y', 'core'), 0, 0, tiled=True)  29.7 us
    ppermute x10, starting transfers between devices, swap_cores(): return lax.ppermute(v, 'core', [(0, 1), (1, 0)])  23.5 us
    all_to_all x1, blocking collectives, on_device(): pieces = lax.all_to_all(copies, ('x', 'y', 'core'), 0, 0, tiled=True)  16.4 us
    all_to_all x1, blocking collectives, on_device(): got = lax.all_to_all(mine, ('zh', 'dp'), 0, 0, tiled=True)  14.1 us
    ppermute x6, waiting for transfers between devices, chips_on(): return lax.ppermute(v, SPACE, up + down)  10.9 us
    ppermute x6, starting transfers between devices, chips_on(): return lax.ppermute(v, SPACE, up + down)  7.72 us
    ppermute x6, starting transfers between devices, across(): lax.ppermute(v, axis, [(i, i ^ k) for i in range(lax.axis_size(axis))])  7.65 us
  transfers between devices with their start and end apart: 22, of which 7 were waited for; matrix products, arithmetic and copies ran while one was open for 2% of the time, Pallas kernels for 9%

profile of v1, /device:TPU:1, one launch (start us, length us, event | category | flops | bytes accessed | tf_op | source)
XLA Modules:
  0.0 163.7 jit_solution(10608545943003361549)
XLA Ops:
  2.0 2.3 %shard_map.102.own = bf16[3,64,256]{2,1,0:T(8,128)(2,1)} custom-call(s32[8]{0:T(128)} %compare_select_fusion.4.sc, s32[128]{0:T(128)} %home.5, bf16[3,64,1024]{2,1,0:T(8,128)(2,1)} %bitcast.11), custom_call_target="tpu_custom_call" | custom-call | tf_op jit(solution)/shard_map/pallas_call | solution.py:534
  4.3 3.2 %collective-permute-start = (bf16[3,64,256]{2,1,0:T(8,128)(2,1)}, bf16[3,64,256]{2,1,0:T(8,128)(2,1)S(1)}, u32[]{:S(2)}, u32[]{:S(2)}) collective-permute-start(bf16[3,64,256]{2,1,0:T(8,128)(2,1)} %shard_map.102.own), channel_id=1, source_target_pairs={{0,1},{1,0},{2,3},{3,2},{4,5},{5,4},{6,7},{7,6},{8,9},{9,8},{10,11... | collective-permute-start | bytes 294920 | tf_op jit(solution)/shard_map/ppermute | solution.py:545
  9.3 2.9 %collective-permute-start.6 = (bf16[80,640]{1,0:T(8,128)(2,1)S(1)}, bf16[80,640]{1,0:T(8,128)(2,1)S(1)}, u32[]{:S(2)}, u32[]{:S(2)}) collective-permute-start(bf16[80,640]{1,0:T(8,128)(2,1)S(1)} %fusion.3.w_a), channel_id=1, source_target_pairs={{0,128},{64,192},{128,0},{192,64},{1,129},{65,193},{129,1},{193,65... | collective-permute-start | bytes 307208 | tf_op jit(solution)/shard_map/ppermute | solution.py:555
  13.5 1.8 %shard_map.103 = bf16[64,256]{1,0:T(8,128)(2,1)} custom-call(s32[8]{0:T(128)} %compare_select_fusion.4.sc, bf16[3,64,256]{2,1,0:T(8,128)(2,1)} %shard_map.102.own, bf16[3,64,256]{2,1,0:T(8,128)(2,1)} %copy-done.2), custom_call_target="tpu_custom_call" | custom-call | tf_op jit(solution)/shard_map/pallas_call | solution.py:534
  15.3 1.3 collective-permute-start.1
  16.6 1.3 collective-permute-start.2
  18.0 2.9 %collective-permute-start.14 = (bf16[32,3456]{1,0:T(8,128)(2,1)}, bf16[32,3456]{1,0:T(8,128)(2,1)S(1)}, u32[]{:S(2)}, u32[]{:S(2)}) collective-permute-start(bf16[32,3456]{1,0:T(8,128)(2,1)} %w_a.1), channel_id=1, source_target_pairs={{0,128},{64,192},{128,0},{192,64},{1,129},{65,193},{129,1},{193,65... | collective-permute-start | bytes 663560 | tf_op jit(solution)/shard_map/ppermute | solution.py:555
  21.9 6.2 %collective-permute-start.3 = (bf16[64,256]{1,0:T(8,128)(2,1)S(1)}, bf16[64,256]{1,0:T(8,128)(2,1)S(1)}, u32[]{:S(2)}, u32[]{:S(2)}) collective-permute-start(bf16[64,256]{1,0:T(8,128)(2,1)S(1)} %collective-permute-done.1.got1), channel_id=1, source_target_pairs={{0,1},{1,0},{2,3},{3,2},{4,5},{5,4},{6,7},{7,6},{8,9},{9,8},{10,11... | collective-permute-start | bytes 98312 | tf_op jit(solution)/shard_map/ppermute | solution.py:545
  29.9 9.0 %shard_map.104 = (bf16[3,640,1152]{2,1,0:T(8,128)(2,1)}, bf16[512,384]{1,0:T(8,128)(2,1)}, f32[512,384]{1,0:T(8,128)}, bf16[128,384]{1,0:T(8,128)(2,1)}, bf16[3,...) custom-call(s32[8]{0:T(128)} %compare_select_fusion.4.sc, s32[128]{0:T(128)} %home.5, s32[4,128]{1,0:T(4,128)} %bitcast.16, ...), custom_call_target="tpu_custom_call" | custom-call | tf_op jit(solution)/shard_map/pallas_call | solution.py:534
  39.2 1.4 collective-permute-done.8.other
  41.2 1.8 %shard_map.105 = bf16[128,128]{1,0:T(8,128)(2,1)} custom-call(s32[8]{0:T(128)} %compare_select_fusion.4.sc, bf16[3,128,128]{2,1,0:T(8,128)(2,1)} %get-tuple-element.18.own, bf16[3,128,128]{2,1,0:T(8,128)(2,1)} %copy-done.3), custom_call_target="tpu_custom_call" | custom-call | tf_op jit(solution)/shard_map/pallas_call | solution.py:534
  43.0 1.3 collective-permute-start.9
  44.2 1.3 collective-permute-start.10
  45.5 5.9 %collective-permute-done.9.got1 = bf16[128,128]{1,0:T(8,128)(2,1)S(1)} collective-permute-done((bf16[128,128]{1,0:T(8,128)(2,1)}, bf16[128,128]{1,0:T(8,128)(2,1)S(1)}, u32[]{:S(2)}, u32[]{:S(2)}) %collective-permute-start.9) | collective-permute-done | bytes 32800 | tf_op jit(solution)/shard_map/ppermute | solution.py:551
  51.4 4.2 %collective-permute-start.11 = (bf16[128,128]{1,0:T(8,128)(2,1)S(1)}, bf16[128,128]{1,0:T(8,128)(2,1)S(1)}, u32[]{:S(2)}, u32[]{:S(2)}) collective-permute-start(bf16[128,128]{1,0:T(8,128)(2,1)S(1)} %collective-permute-done.9.got1), channel_id=1, source_target_pairs={{0,1},{1,0},{2,3},{3,2},{4,5},{5,4},{6,7},{7,6},{8,9},{9,8},{10,11... | collective-permute-start | bytes 98312 | tf_op jit(solution)/shard_map/ppermute | solution.py:545
  55.6 1.8 %collective-permute-start.12 = (bf16[128,128]{1,0:T(8,128)(2,1)S(1)}, bf16[128,128]{1,0:T(8,128)(2,1)S(1)}, u32[]{:S(2)}, u32[]{:S(2)}) collective-permute-start(bf16[128,128]{1,0:T(8,128)(2,1)S(1)} %collective-permute-done.10.got2), channel_id=1, source_target_pairs={{0,1},{1,0},{2,3},{3,2},{4,5},{5,4},{6,7},{7,6},{8,9},{9,8},{10,11... | collective-permute-start | bytes 98312 | tf_op jit(solution)/shard_map/ppermute | solution.py:545
  58.8 7.5 %shard_map.106 = (bf16[3,128,128]{2,1,0:T(8,128)(2,1)}, bf16[2,32,4,16,128]{4,3,2,1,0:T(8,128)(2,1)}, f32[128,384]{1,0:T(8,128)}, bf16[3,128,128]{2,1,0:T(8,128)(2,1)}) custom-call(s32[8]{0:T(128)} %compare_select_fusion.4.sc, s32[128]{0:T(128)} %home.5, s32[4,128]{1,0:T(4,128)} %bitcast.17, bf16[128,384]{1,0:T(8,128)(2,1)} %get-tuple-element.17.red, ...), custom_call_target="tpu_custom_call" | custom-call | tf_op jit(solution)/shard_map/pallas_call | solution.py:534
  68.0 1.5 collective-permute-done.16.other
  70.2 1.9 %shard_map.107 = bf16[128,128]{1,0:T(8,128)(2,1)} custom-call(s32[8]{0:T(128)} %compare_select_fusion.4.sc, bf16[3,128,128]{2,1,0:T(8,128)(2,1)} %get-tuple-element.21.own, bf16[3,128,128]{2,1,0:T(8,128)(2,1)} %copy-done.1), custom_call_target="tpu_custom_call" | custom-call | tf_op jit(solution)/shard_map/pallas_call | solution.py:534
  72.1 1.3 collective-permute-start.17
  73.4 1.3 collective-permute-start.18
  74.7 5.1 %collective-permute-done.17.got1 = bf16[128,128]{1,0:T(8,128)(2,1)S(1)} collective-permute-done((bf16[128,128]{1,0:T(8,128)(2,1)}, bf16[128,128]{1,0:T(8,128)(2,1)S(1)}, u32[]{:S(2)}, u32[]{:S(2)}) %collective-permute-start.17) | collective-permute-done | bytes 32800 | tf_op jit(solution)/shard_map/ppermute | solution.py:551
  79.7 5.5 %collective-permute-start.19 = (bf16[128,128]{1,0:T(8,128)(2,1)S(1)}, bf16[128,128]{1,0:T(8,128)(2,1)S(1)}, u32[]{:S(2)}, u32[]{:S(2)}) collective-permute-start(bf16[128,128]{1,0:T(8,128)(2,1)S(1)} %collective-permute-done.17.got1), channel_id=1, source_target_pairs={{0,1},{1,0},{2,3},{3,2},{4,5},{5,4},{6,7},{7,6},{8,9},{9,8},{10,11... | collective-permute-start | bytes 98312 | tf_op jit(solution)/shard_map/ppermute | solution.py:545
  85.2 1.8 %collective-permute-start.20 = (bf16[128,128]{1,0:T(8,128)(2,1)S(1)}, bf16[128,128]{1,0:T(8,128)(2,1)S(1)}, u32[]{:S(2)}, u32[]{:S(2)}) collective-permute-start(bf16[128,128]{1,0:T(8,128)(2,1)S(1)} %collective-permute-done.18.got2), channel_id=1, source_target_pairs={{0,1},{1,0},{2,3},{3,2},{4,5},{5,4},{6,7},{7,6},{8,9},{9,8},{10,11... | collective-permute-start | bytes 98312 | tf_op jit(solution)/shard_map/ppermute | solution.py:545
  87.0 2.0 %fusion.two = bf16[32,4,16,128]{3,2,1,0:T(8,128)(2,1)} fusion(bf16[32,4,16,128]{3,2,1,0:T(8,128)(2,1)S(1)} %collective-permute-done.21, bf16[2,32,4,16,128]{4,3,2,1,0:T(8,128)(2,1)} %get-tuple-element.26, s32[]{:T(128)S(6)} %select_n.45), kind=kLoop, calls=%fused_computation.1 | loop fusion | flops 1048576 | bytes 1572868 | tf_op jit(solution)/shard_map/convert_element_type | solution.py:611
  89.6 8.4 %shard_map.108 = bf16[32,4,32,128]{3,2,1,0:T(8,128)(2,1)} custom-call(s32[8]{0:T(128)} %compare_select_fusion.4.sc, s32[4,128]{1,0:T(4,128)} %bitcast.18, f32[128,384]{1,0:T(8,128)} %get-tuple-element.20.grad, bf16[3,128,128]{2,1,0:T(8,128)(2,1)} %get-tuple-element.21.own, bf16[3,128,128]{2,1,0:T(8,128)(2,1)} %copy-done.1, bf16[128,128]{1,0:T(8,128)(2,1)} %copy-done.10, ...), custom_call_target="tpu_custom_call" | custom-call | tf_op jit(solution)/shard_map/pallas_call | solution.py:534
  98.1 29.7 %all_to_all.15.got = bf16[32,4,32,128]{3,2,1,0:T(8,128)(2,1)} all-to-all(bf16[32,4,32,128]{3,2,1,0:T(8,128)(2,1)} %shard_map.108), channel_id=1, replica_groups=mesh['dp'=4,'x'=4,'zh'=2,'y'=4,'core'=2] {'x','y','core'}, dimensions={0} | all-to-all | bytes 2097152 | tf_op jit(solution)/shard_map/all_to_all | solution.py:619
  127.7 2.0 %shard_map.109 = bf16[8,48,128]{2,1,0:T(8,128)(2,1)} custom-call(bf16[32,4,32,128]{3,2,1,0:T(8,128)(2,1)} %all_to_all.15.got), custom_call_target="tpu_custom_call" | custom-call | tf_op jit(solution)/shard_map/pallas_call | solution.py:534
  129.7 14.1 %all_to_all.16.got = bf16[8,48,128]{2,1,0:T(8,128)(2,1)} all-to-all(bf16[8,48,128]{2,1,0:T(8,128)(2,1)} %shard_map.109), channel_id=1, replica_groups=mesh['dp'=4,'x'=4,'zh'=2,'y'=4,'core'=2] {'zh','dp'}, dimensions={0} | all-to-all | bytes 196608 | tf_op jit(solution)/shard_map/all_to_all | solution.py:621
  143.8 1.7 %shard_map.110 = bf16[32,48,128]{2,1,0:T(8,128)(2,1)} custom-call(bf16[8,48,128]{2,1,0:T(8,128)(2,1)} %all_to_all.16.got), custom_call_target="tpu_custom_call" | custom-call | tf_op jit(solution)/shard_map/pallas_call | solution.py:534
  145.5 16.4 %all_to_all.17.pieces = bf16[32,48,128]{2,1,0:T(8,128)(2,1)} all-to-all(bf16[32,48,128]{2,1,0:T(8,128)(2,1)} %shard_map.110), channel_id=1, replica_groups=mesh['dp'=4,'x'=4,'zh'=2,'y'=4,'core'=2] {'x','y','core'}, dimensions={0} | all-to-all | bytes 786432 | tf_op jit(solution)/shard_map/all_to_all | solution.py:623
  161.9 1.8 %shard_map.111 = (f32[16,1728]{1,0:T(8,128)}, f32[32,512]{1,0:T(8,128)}, f32[32,3456]{1,0:T(8,128)}) custom-call(bf16[32,48,128]{2,1,0:T(8,128)(2,1)} %all_to_all.17.pieces), custom_call_target="tpu_custom_call" | custom-call | tf_op jit(solution)/shard_map/pallas_call | solution.py:534
  (77 shorter events, 12.6 us)
Async XLA Ops:
  4.3 8.6 %collective-permute-start = (bf16[3,64,256]{2,1,0:T(8,128)(2,1)}, bf16[3,64,256]{2,1,0:T(8,128)(2,1)S(1)}, u32[]{:S(2)}, u32[]{:S(2)}) collective-permute-start(bf16[3,64,256]{2,1,0:T(8,128)(2,1)} %shard_map.102.own), channel_id=1, source_target_pairs={{0,1},{1,0},{2,3},{3,2},{4,5},{5,4},{6,7},{7,6},{8,9},{9,8},{10,11... | collective-permute-start | bytes 294920 | tf_op jit(solution)/shard_map/ppermute | solution.py:545
  9.2 20.1 %copy-start = (bf16[80,640]{1,0:T(8,128)(2,1)}, bf16[80,640]{1,0:T(8,128)(2,1)S(1)}, u32[]{:S(2)}) copy-start(bf16[80,640]{1,0:T(8,128)(2,1)S(1)} %fusion.3.w_a) | copy-start | bytes 307204
  9.2 8.6 %collective-permute-start.5 = (bf16[80,640]{1,0:T(8,128)(2,1)S(1)}, bf16[80,640]{1,0:T(8,128)(2,1)S(1)}, u32[]{:S(2)}, u32[]{:S(2)}) collective-permute-start(bf16[80,640]{1,0:T(8,128)(2,1)S(1)} %fusion.3.w_a), channel_id=1, source_target_pairs={{0,64},{64,0},{128,192},{192,128},{1,65},{65,1},{129,193},{193,129... | collective-permute-start | bytes 307208 | tf_op jit(solution)/shard_map/ppermute | solution.py:555
  9.3 8.7 %collective-permute-start.6 = (bf16[80,640]{1,0:T(8,128)(2,1)S(1)}, bf16[80,640]{1,0:T(8,128)(2,1)S(1)}, u32[]{:S(2)}, u32[]{:S(2)}) collective-permute-start(bf16[80,640]{1,0:T(8,128)(2,1)S(1)} %fusion.3.w_a), channel_id=1, source_target_pairs={{0,128},{64,192},{128,0},{192,64},{1,129},{65,193},{129,1},{193,65... | collective-permute-start | bytes 307208 | tf_op jit(solution)/shard_map/ppermute | solution.py:555
  12.2 8.7 %collective-permute-start.7 = (bf16[80,640]{1,0:T(8,128)(2,1)S(1)}, bf16[80,640]{1,0:T(8,128)(2,1)S(1)}, u32[]{:S(2)}, u32[]{:S(2)}) collective-permute-start(bf16[80,640]{1,0:T(8,128)(2,1)S(1)} %fusion.3.w_a), channel_id=1, source_target_pairs={{0,192},{64,128},{128,64},{192,0},{1,193},{65,129},{129,65},{193,1... | collective-permute-start | bytes 307208 | tf_op jit(solution)/shard_map/ppermute | solution.py:555
  15.3 6.7 %collective-permute-start.1 = (bf16[64,256]{1,0:T(8,128)(2,1)}, bf16[64,256]{1,0:T(8,128)(2,1)S(1)}, u32[]{:S(2)}, u32[]{:S(2)}) collective-permute-start(bf16[64,256]{1,0:T(8,128)(2,1)} %shard_map.103), channel_id=1, source_target_pairs={{0,2},{2,4},{4,6},{6,8},{8,10},{10,12},{12,14},{14,16},{16,18},{18... | collective-permute-start | bytes 98312 | tf_op jit(solution)/shard_map/ppermute | solution.py:551
  16.6 11.6 %collective-permute-start.2 = (bf16[64,256]{1,0:T(8,128)(2,1)}, bf16[64,256]{1,0:T(8,128)(2,1)S(1)}, u32[]{:S(2)}, u32[]{:S(2)}) collective-permute-start(bf16[64,256]{1,0:T(8,128)(2,1)} %shard_map.103), channel_id=1, source_target_pairs={{0,4},{2,6},{4,8},{6,10},{8,12},{10,14},{12,16},{14,18},{16,20},{1... | collective-permute-start | bytes 98312 | tf_op jit(solution)/shard_map/ppermute | solution.py:551
  17.9 11.5 %copy-start.7 = (bf16[80,640]{1,0:T(8,128)(2,1)}, bf16[80,640]{1,0:T(8,128)(2,1)S(1)}, u32[]{:S(2)}) copy-start(bf16[80,640]{1,0:T(8,128)(2,1)S(1)} %collective-permute-done.5.w_b) | copy-start | bytes 307204
  17.9 39.5 %collective-permute-start.13 = (bf16[32,3456]{1,0:T(8,128)(2,1)}, bf16[32,3456]{1,0:T(8,128)(2,1)S(1)}, u32[]{:S(2)}, u32[]{:S(2)}) collective-permute-start(bf16[32,3456]{1,0:T(8,128)(2,1)} %w_a.1), channel_id=1, source_target_pairs={{0,64},{64,0},{128,192},{192,128},{1,65},{65,1},{129,193},{193,129... | collective-permute-start | bytes 663560 | tf_op jit(solution)/shard_map/ppermute | solution.py:555
  18.0 11.4 %copy-start.8 = (bf16[80,640]{1,0:T(8,128)(2,1)}, bf16[80,640]{1,0:T(8,128)(2,1)S(1)}, u32[]{:S(2)}) copy-start(bf16[80,640]{1,0:T(8,128)(2,1)S(1)} %collective-permute-done.6.w_c) | copy-start | bytes 307204
  18.0 39.4 %collective-permute-start.14 = (bf16[32,3456]{1,0:T(8,128)(2,1)}, bf16[32,3456]{1,0:T(8,128)(2,1)S(1)}, u32[]{:S(2)}, u32[]{:S(2)}) collective-permute-start(bf16[32,3456]{1,0:T(8,128)(2,1)} %w_a.1), channel_id=1, source_target_pairs={{0,128},{64,192},{128,0},{192,64},{1,129},{65,193},{129,1},{193,65... | collective-permute-start | bytes 663560 | tf_op jit(solution)/shard_map/ppermute | solution.py:555
  20.9 8.5 %copy-start.9 = (bf16[80,640]{1,0:T(8,128)(2,1)}, bf16[80,640]{1,0:T(8,128)(2,1)S(1)}, u32[]{:S(2)}) copy-start(bf16[80,640]{1,0:T(8,128)(2,1)S(1)} %collective-permute-done.7.w_d) | copy-start | bytes 307204
  20.9 36.5 %collective-permute-start.15 = (bf16[32,3456]{1,0:T(8,128)(2,1)}, bf16[32,3456]{1,0:T(8,128)(2,1)S(1)}, u32[]{:S(2)}, u32[]{:S(2)}) collective-permute-start(bf16[32,3456]{1,0:T(8,128)(2,1)} %w_a.1), channel_id=1, source_target_pairs={{0,192},{64,128},{128,64},{192,0},{1,193},{65,129},{129,65},{193,1... | collective-permute-start | bytes 663560 | tf_op jit(solution)/shard_map/ppermute | solution.py:555
  21.9 7.4 %copy-start.14 = (bf16[64,256]{1,0:T(8,128)(2,1)}, bf16[64,256]{1,0:T(8,128)(2,1)S(1)}, u32[]{:S(2)}) copy-start(bf16[64,256]{1,0:T(8,128)(2,1)S(1)} %collective-permute-done.1.got1) | copy-start | bytes 98308
  21.9 7.0 %collective-permute-start.3 = (bf16[64,256]{1,0:T(8,128)(2,1)S(1)}, bf16[64,256]{1,0:T(8,128)(2,1)S(1)}, u32[]{:S(2)}, u32[]{:S(2)}) collective-permute-start(bf16[64,256]{1,0:T(8,128)(2,1)S(1)} %collective-permute-done.1.got1), channel_id=1, source_target_pairs={{0,1},{1,0},{2,3},{3,2},{4,5},{5,4},{6,7},{7,6},{8,9},{9,8},{10,11... | collective-permute-start | bytes 98312 | tf_op jit(solution)/shard_map/ppermute | solution.py:545
  28.1 1.2 copy-start.15
  28.1 1.2 collective-permute-start.4
  39.0 1.6 collective-permute-start.8
  43.0 8.5 %collective-permute-start.9 = (bf16[128,128]{1,0:T(8,128)(2,1)}, bf16[128,128]{1,0:T(8,128)(2,1)S(1)}, u32[]{:S(2)}, u32[]{:S(2)}) collective-permute-start(bf16[128,128]{1,0:T(8,128)(2,1)} %shard_map.105), channel_id=1, source_target_pairs={{0,2},{2,4},{4,6},{6,8},{8,10},{10,12},{12,14},{14,16},{16,18},{18... | collective-permute-start | bytes 98312 | tf_op jit(solution)/shard_map/ppermute | solution.py:551
  44.2 11.3 %collective-permute-start.10 = (bf16[128,128]{1,0:T(8,128)(2,1)}, bf16[128,128]{1,0:T(8,128)(2,1)S(1)}, u32[]{:S(2)}, u32[]{:S(2)}) collective-permute-start(bf16[128,128]{1,0:T(8,128)(2,1)} %shard_map.105), channel_id=1, source_target_pairs={{0,4},{2,6},{4,8},{6,10},{8,12},{10,14},{12,16},{14,18},{16,20},{1... | collective-permute-start | bytes 98312 | tf_op jit(solution)/shard_map/ppermute | solution.py:551
  51.4 6.8 %copy-start.16 = (bf16[128,128]{1,0:T(8,128)(2,1)}, bf16[128,128]{1,0:T(8,128)(2,1)S(1)}, u32[]{:S(2)}) copy-start(bf16[128,128]{1,0:T(8,128)(2,1)S(1)} %collective-permute-done.9.got1) | copy-start | bytes 98308
  51.4 6.0 %collective-permute-start.11 = (bf16[128,128]{1,0:T(8,128)(2,1)S(1)}, bf16[128,128]{1,0:T(8,128)(2,1)S(1)}, u32[]{:S(2)}, u32[]{:S(2)}) collective-permute-start(bf16[128,128]{1,0:T(8,128)(2,1)S(1)} %collective-permute-done.9.got1), channel_id=1, source_target_pairs={{0,1},{1,0},{2,3},{3,2},{4,5},{5,4},{6,7},{7,6},{8,9},{9,8},{10,11... | collective-permute-start | bytes 98312 | tf_op jit(solution)/shard_map/ppermute | solution.py:545
  55.6 2.7 %copy-start.17 = (bf16[128,128]{1,0:T(8,128)(2,1)}, bf16[128,128]{1,0:T(8,128)(2,1)S(1)}, u32[]{:S(2)}) copy-start(bf16[128,128]{1,0:T(8,128)(2,1)S(1)} %collective-permute-done.10.got2) | copy-start | bytes 98308
  55.6 2.6 %collective-permute-start.12 = (bf16[128,128]{1,0:T(8,128)(2,1)S(1)}, bf16[128,128]{1,0:T(8,128)(2,1)S(1)}, u32[]{:S(2)}, u32[]{:S(2)}) collective-permute-start(bf16[128,128]{1,0:T(8,128)(2,1)S(1)} %collective-permute-done.10.got2), channel_id=1, source_target_pairs={{0,1},{1,0},{2,3},{3,2},{4,5},{5,4},{6,7},{7,6},{8,9},{9,8},{10,11... | collective-permute-start | bytes 98312 | tf_op jit(solution)/shard_map/ppermute | solution.py:545
  67.4 19.6 %collective-permute-start.21 = (bf16[32,4,16,128]{3,2,1,0:T(8,128)(2,1)S(1)}, bf16[32,4,16,128]{3,2,1,0:T(8,128)(2,1)S(1)}, u32[]{:S(2)}, u32[]{:S(2)}) collective-permute-start(bf16[32,4,16,128]{3,2,1,0:T(8,128)(2,1)S(1)} %dynamic-slice_bitcast_fusion), channel_id=1, source_target_pairs={{0,1},{1,0},{2,3},{3,2},{4,5},{5,4},{6,7},{7,6},{8,9},{9,8},{10,11... | collective-permute-start | bytes 1572872 | tf_op jit(solution)/shard_map/ppermute | solution.py:545
  67.9 1.7 %collective-permute-start.16 = (bf16[3,128,128]{2,1,0:T(8,128)(2,1)}, bf16[3,128,128]{2,1,0:T(8,128)(2,1)S(1)}, u32[]{:S(2)}, u32[]{:S(2)}) collective-permute-start(bf16[3,128,128]{2,1,0:T(8,128)(2,1)} %get-tuple-element.21.own), channel_id=1, source_target_pairs={{0,1},{1,0},{2,3},{3,2},{4,5},{5,4},{6,7},{7,6},{8,9},{9,8},{10,11... | collective-permute-start | bytes 294920 | tf_op jit(solution)/shard_map/ppermute | solution.py:545
  72.1 7.6 %collective-permute-start.17 = (bf16[128,128]{1,0:T(8,128)(2,1)}, bf16[128,128]{1,0:T(8,128)(2,1)S(1)}, u32[]{:S(2)}, u32[]{:S(2)}) collective-permute-start(bf16[128,128]{1,0:T(8,128)(2,1)} %shard_map.107), channel_id=1, source_target_pairs={{0,2},{2,4},{4,6},{6,8},{8,10},{10,12},{12,14},{14,16},{16,18},{18... | collective-permute-start | bytes 98312 | tf_op jit(solution)/shard_map/ppermute | solution.py:551
  73.4 11.8 %collective-permute-start.18 = (bf16[128,128]{1,0:T(8,128)(2,1)}, bf16[128,128]{1,0:T(8,128)(2,1)S(1)}, u32[]{:S(2)}, u32[]{:S(2)}) collective-permute-start(bf16[128,128]{1,0:T(8,128)(2,1)} %shard_map.107), channel_id=1, source_target_pairs={{0,4},{2,6},{4,8},{6,10},{8,12},{10,14},{12,16},{14,18},{16,20},{1... | collective-permute-start | bytes 98312 | tf_op jit(solution)/shard_map/ppermute | solution.py:551
  79.7 9.3 %copy-start.10 = (bf16[128,128]{1,0:T(8,128)(2,1)}, bf16[128,128]{1,0:T(8,128)(2,1)S(1)}, u32[]{:S(2)}) copy-start(bf16[128,128]{1,0:T(8,128)(2,1)S(1)} %collective-permute-done.17.got1) | copy-start | bytes 98308
  79.7 9.3 %collective-permute-start.19 = (bf16[128,128]{1,0:T(8,128)(2,1)S(1)}, bf16[128,128]{1,0:T(8,128)(2,1)S(1)}, u32[]{:S(2)}, u32[]{:S(2)}) collective-permute-start(bf16[128,128]{1,0:T(8,128)(2,1)S(1)} %collective-permute-done.17.got1), channel_id=1, source_target_pairs={{0,1},{1,0},{2,3},{3,2},{4,5},{5,4},{6,7},{7,6},{8,9},{9,8},{10,11... | collective-permute-start | bytes 98312 | tf_op jit(solution)/shard_map/ppermute | solution.py:545
  85.2 3.9 %copy-start.11 = (bf16[128,128]{1,0:T(8,128)(2,1)}, bf16[128,128]{1,0:T(8,128)(2,1)S(1)}, u32[]{:S(2)}) copy-start(bf16[128,128]{1,0:T(8,128)(2,1)S(1)} %collective-permute-done.18.got2) | copy-start | bytes 98308
  85.2 3.8 %collective-permute-start.20 = (bf16[128,128]{1,0:T(8,128)(2,1)S(1)}, bf16[128,128]{1,0:T(8,128)(2,1)S(1)}, u32[]{:S(2)}, u32[]{:S(2)}) collective-permute-start(bf16[128,128]{1,0:T(8,128)(2,1)S(1)} %collective-permute-done.18.got2), channel_id=1, source_target_pairs={{0,1},{1,0},{2,3},{3,2},{4,5},{5,4},{6,7},{7,6},{8,9},{9,8},{10,11... | collective-permute-start | bytes 98312 | tf_op jit(solution)/shard_map/ppermute | solution.py:545
  (12 other events, 8.4 us)

commit v2 on v0

--- a/solution.py
+++ b/solution.py
@@ -125,7 +125,7 @@
 
 
 def link_at(links, q, column):
-    return links[jnp.clip(q, 0, 127) * 4 + column]
+    return links[column, jnp.clip(q, 0, 127)]
 
 
 def x_link(links, q):
@@ -318,7 +318,7 @@
 
 
 def stage_two_kernel(scale, sc, home, links, red, cot, own, other, got1, got2, sw1, sw2,
-                     w_a, w_b, w_c, w_d, out, dw, grad, brec,
+                     w_a, w_b, w_c, w_d, out, keep, give, grad, brec,
                      recs, low_rows, high_rows, w_all, w_two, taps, spread):
     s = where_am_i(sc)
     dp = sc[7]
@@ -364,16 +364,14 @@
             spread[(dx + 1) * 128 : (dx + 2) * 128, i * 256 : i * 256 + 256] = w.astype(BF)
     whole = mm(spread[...], taps[...], NT)
     for dx in range(3):
-        for og in range(2):
-            for j in range(9):
-                t = (dx * 2 + og) * 9 + j
-                row = (t % 2) * 16
-                for d in range(4):
-                    at = dx * 128 + d * 32 + og * 16
-                    dw[t // 2, d, row : row + 16, :] = whole[
-                        at : at + 16, j * 128 : j * 128 + 128
-                    ].astype(BF)
-    dw[27:, :, :, :] = jnp.zeros((5, 4, 32, 128), BF)
+        for j in range(9):
+            for d in range(4):
+                at, lanes = dx * 128 + d * 32, slice(j * 128, j * 128 + 128)
+                first, second = whole[at : at + 16, lanes], whole[at + 16 : at + 32, lanes]
+                keep[dx * 9 + j, d] = jnp.where(s.core == 0, first, second).astype(BF)
+                give[dx * 9 + j, d] = jnp.where(s.core == 0, second, first).astype(BF)
+    keep[27:, :, :, :] = jnp.zeros((5, 4, 16, 128), BF)
+    give[27:, :, :, :] = jnp.zeros((5, 4, 16, 128), BF)
     back = mm(w_two[...], spread[...], TN)
     yy, zz = coords(TWO)
     for i in range(3):
@@ -477,7 +475,9 @@
         for og in range(2):
             for j in range(4):
                 at = d * 32 + og * 16
-                out[15 + og * 4 + j, d] = dw_down[at : at + 16, j * 128 : j * 128 + 128].astype(BF)
+                out[15 + og * 4 + j, d] = dw_down[
+                    at : at + 16, j * 128 : j * 128 + 128
+                ].astype(BF)
     out[23:, :, :, :] = jnp.zeros((9, 4, 16, 128), BF)
 
 
@@ -486,19 +486,17 @@
     for dx in range(3):
         for og in range(2):
             for j in range(9):
-                t = (dx * 2 + og) * 9 + j
-                row = (t % 2) * 16
                 two_out[og * 16 : og * 16 + 16, dx * 1152 + j * 128 : dx * 1152 + j * 128 + 128] = (
-                    pieces[t // 2, row : row + 16, :].astype(F32)
+                    pieces[dx * 9 + j, 16 + og * 16 : 32 + og * 16, :].astype(F32)
                 )
     for og in range(2):
         for j in range(4):
             down_out[og * 16 : og * 16 + 16, j * 128 : j * 128 + 128] = pieces[
-                15 + og * 4 + j, 32:48, :
+                15 + og * 4 + j, 0:16, :
             ].astype(F32)
 
     def tile(dx, j):
-        return pieces[dx * 5 + j, 32:48, :].astype(F32)
+        return pieces[dx * 5 + j, 0:16, :].astype(F32)
 
     middle = jnp.concatenate([tile(1, j) for j in range(5)], axis=1)
     middle = pltpu.roll(middle, 64, 1)
@@ -551,11 +549,6 @@
     return [shard] + [across(shard, "dp", k) for k in (1, 2, 3)]
 
 
-def scattered(pieces):
-    got = lax.all_to_all(pieces, ("x", "y", "core"), 0, 0, tiled=True)
-    return got.astype(F32).sum(axis=0).astype(BF)
-
-
 def on_device(features, cotangent, conv_one, down_weight, conv_two, patch_home, patch_links):
     core, dp = lax.axis_index("core"), lax.axis_index("dp")
     dev = lax.axis_index(SPACE)
@@ -568,7 +561,7 @@
     sc = jnp.where(
         slots < 5, starts, jnp.where(slots == 5, dev, jnp.where(slots == 6, core, dp))
     ).astype(jnp.int32)
-    links = patch_links.reshape(-1)
+    links = patch_links.T
     x = features[0]
     (rec_one,) = call(faces_kernel, (sc, patch_home), (x,), [((3, 64, 256), BF)], [])
     rims_one = exchange(ONE, 1, sc, rec_one)
@@ -585,15 +578,17 @@
     )
     rims_two = exchange(TWO, 1, sc, rec_two)
     cells = lax.axis_size("dp") * patch_links.shape[0] * 128
-    out, dw_two, grad, rec_back = call(
+    out, keep, give, grad, rec_back = call(
         functools.partial(stage_two_kernel, float(cells) ** (-0.5)), (sc, patch_home, links),
         (red, cotangent[0], rec_two, *rims_two, *w_two),
-        [((3, 128, 128), BF), ((32, 4, 32, 128), BF), ((128, 384), F32), ((3, 128, 128), BF)],
+        [((3, 128, 128), BF), ((32, 4, 16, 128), BF), ((32, 4, 16, 128), BF),
+         ((128, 384), F32), ((3, 128, 128), BF)],
         [((10, 128, 128), BF), ((128, 256), BF), ((128, 256), BF), ((4, 32, 3456), BF),
          ((384, 1152), BF), ((1152, 768), BF), ((384, 768), BF)],
     )
     rims_back = exchange(TWO, 2, sc, rec_back)
-    two_sum = scattered(dw_two)
+    two = (keep.astype(F32) + swap_cores(give).astype(F32)).astype(BF)
+    two = lax.all_to_all(two, ("x", "y", "core"), 0, 0, tiled=True)
     (small,) = call(
         stage_three_kernel, (sc, links),
         (grad, rec_back, *rims_back, down_full, hid, slope, taps),
@@ -601,8 +596,11 @@
         [((10, 128, 128), BF), ((128, 384), BF), ((512, 384), BF), ((192, 1152), BF),
          ((192, 640), F32)],
     )
-    two_sum, small = lax.optimization_barrier((two_sum, small))
-    mine = jnp.concatenate([two_sum, scattered(small)], axis=1)
+    two = two.astype(F32).reshape(16, 2, 4, 16, 128).sum(axis=0).astype(BF)
+    two, small = lax.optimization_barrier((two, small))
+    small = lax.all_to_all(small, ("x", "y", "core"), 0, 0, tiled=True)
+    small = small.astype(F32).sum(axis=0).astype(BF)
+    mine = jnp.concatenate([small, two[0], two[1]], axis=1)
     got = lax.all_to_all(jnp.concatenate([mine, mine]), ("zh", "dp"), 0, 0, tiled=True)
     mine = got.astype(F32).sum(axis=0).astype(BF)
     copies = jnp.broadcast_to(mine[None], (32, *mine.shape))

time: 159 us -> 161 us (1.013)
  blocking collectives: 51.7 us -> 27 us
  starting transfers between devices: 42.5 us -> 56.7 us
  waiting for transfers between devices: 18.9 us -> 32.5 us
  local copies, waits for them, and re-layouts: 6.75 us -> 4.7 us
  other arithmetic: 2.47 us -> 4.39 us
    all_to_all x1 -> x0, blocking collectives: 24.9 us -> none  [scattered(): got = lax.all_to_all(pieces, ('x', 'y', 'core'), 0, 0, tiled=True)]
    all_to_all x1 -> x2, starting transfers between devices: 12.4 us -> 25.7 us  [the longest x1 13.3 us: on_device(): small = lax.all_to_all(small, ('x', 'y', 'core'), 0, 0, tiled=True)]
    all_to_all x1 -> x2, waiting for transfers between devices: 0.01 us -> 11.6 us  [the longest x1 11.6 us: on_device(): small = lax.all_to_all(small, ('x', 'y', 'core'), 0, 0, tiled=True)]
    ppermute x9 -> x10, waiting for transfers between devices: 4.1 us -> 7.14 us  [swap_cores(): return lax.ppermute(v, 'core', [(0, 1), (1, 0)])]
    convert_element_type x0 -> x1, other arithmetic: none -> 2.03 us  [on_device(): two = (keep.astype(F32) + swap_cores(give).astype(F32)).astype(BF)]
    unnamed x45 -> x44, local copies, waits for them, and re-layouts: 5.07 us -> 3.71 us
    ppermute x9 -> x10, starting transfers between devices: 14.8 us -> 15.8 us  [swap_cores(): return lax.ppermute(v, 'core', [(0, 1), (1, 0)])]
  transfers between devices with their start and end apart: 22 -> 24, of which waited for: 7 -> 11; matrix products, arithmetic and copies ran while one was open for 2% -> 1% of each run, Pallas kernels for 15% -> 14%
where the time goes in v2:
time: 161 us; the launch traced here: 160 us
  starting transfers between devices  56.7 us (35%)
  Pallas kernels  34.2 us (21%)
  waiting for transfers between devices  32.5 us (20%)
  blocking collectives  27 us (17%)
  local copies, waits for them, and re-layouts  4.7 us (3%)
  other arithmetic  4.39 us (3%)
    pallas_call x8, Pallas kernels, call(): pl.pallas_call(kernel, out_shape=[jax.ShapeDtypeStruct(*o) for o in outs]...  34.2 us
    ppermute x10, starting transfers between devices, swap_cores(): return lax.ppermute(v, 'core', [(0, 1), (1, 0)])  15.8 us
    all_to_all x1, blocking collectives, on_device(): pieces = lax.all_to_all(copies, ('x', 'y', 'core'), 0, 0, tiled=True)  14.9 us
    all_to_all x1, starting transfers between devices, on_device(): small = lax.all_to_all(small, ('x', 'y', 'core'), 0, 0, tiled=True)  13.3 us
    ppermute x6, waiting for transfers between devices, chips_on(): return lax.ppermute(v, SPACE, up + down)  12.7 us
    all_to_all x1, starting transfers between devices, on_device(): two = lax.all_to_all(two, ('x', 'y', 'core'), 0, 0, tiled=True)  12.3 us
    all_to_all x1, blocking collectives, on_device(): lax.all_to_all(jnp.concatenate([mine, mine]), ('zh', 'dp'), 0, 0, tiled=T...  12.1 us
    all_to_all x1, waiting for transfers between devices, on_device(): small = lax.all_to_all(small, ('x', 'y', 'core'), 0, 0, tiled=True)  11.6 us
  transfers between devices with their start and end apart: 24, of which 11 were waited for; matrix products, arithmetic and copies ran while one was open for 1% of the time, Pallas kernels for 14%

profile of v2, /device:TPU:1, one launch (start us, length us, event | category | flops | bytes accessed | tf_op | source)
XLA Modules:
  0.0 160.5 jit_solution(8406897205937415428)
XLA Ops:
  2.1 2.3 %shard_map.102.own = bf16[3,64,256]{2,1,0:T(8,128)(2,1)} custom-call(s32[8]{0:T(128)} %compare_select_fusion.4.sc, s32[128]{0:T(128)} %home.5, bf16[3,64,1024]{2,1,0:T(8,128)(2,1)} %bitcast.12), custom_call_target="tpu_custom_call" | custom-call | tf_op jit(solution)/shard_map/pallas_call | solution.py:514
  4.3 3.2 %collective-permute-start = (bf16[3,64,256]{2,1,0:T(8,128)(2,1)}, bf16[3,64,256]{2,1,0:T(8,128)(2,1)S(1)}, u32[]{:S(2)}, u32[]{:S(2)}) collective-permute-start(bf16[3,64,256]{2,1,0:T(8,128)(2,1)} %shard_map.102.own), channel_id=1, source_target_pairs={{0,1},{1,0},{2,3},{3,2},{4,5},{5,4},{6,7},{7,6},{8,9},{9,8},{10,11... | collective-permute-start | bytes 294920 | tf_op jit(solution)/shard_map/ppermute | solution.py:525
  9.2 2.7 %collective-permute-start.7 = (bf16[80,640]{1,0:T(8,128)(2,1)S(1)}, bf16[80,640]{1,0:T(8,128)(2,1)S(1)}, u32[]{:S(2)}, u32[]{:S(2)}) collective-permute-start(bf16[80,640]{1,0:T(8,128)(2,1)S(1)} %fusion.2.w_a), channel_id=1, source_target_pairs={{0,192},{64,128},{128,64},{192,0},{1,193},{65,129},{129,65},{193,1... | collective-permute-start | bytes 307208 | tf_op jit(solution)/shard_map/ppermute | solution.py:535
  13.5 1.8 %shard_map.103 = bf16[64,256]{1,0:T(8,128)(2,1)} custom-call(s32[8]{0:T(128)} %compare_select_fusion.4.sc, bf16[3,64,256]{2,1,0:T(8,128)(2,1)} %shard_map.102.own, bf16[3,64,256]{2,1,0:T(8,128)(2,1)} %copy-done.1), custom_call_target="tpu_custom_call" | custom-call | tf_op jit(solution)/shard_map/pallas_call | solution.py:514
  15.3 1.3 collective-permute-start.2
  16.6 1.3 collective-permute-start.1
  17.9 1.5 collective-permute-start.14
  20.9 2.0 %collective-permute-start.15 = (bf16[32,3456]{1,0:T(8,128)(2,1)}, bf16[32,3456]{1,0:T(8,128)(2,1)S(1)}, u32[]{:S(2)}, u32[]{:S(2)}) collective-permute-start(bf16[32,3456]{1,0:T(8,128)(2,1)} %w_a.1), channel_id=1, source_target_pairs={{0,192},{64,128},{128,64},{192,0},{1,193},{65,129},{129,65},{193,1... | collective-permute-start | bytes 663560 | tf_op jit(solution)/shard_map/ppermute | solution.py:535
  22.9 4.6 %collective-permute-start.4 = (bf16[64,256]{1,0:T(8,128)(2,1)S(1)}, bf16[64,256]{1,0:T(8,128)(2,1)S(1)}, u32[]{:S(2)}, u32[]{:S(2)}) collective-permute-start(bf16[64,256]{1,0:T(8,128)(2,1)S(1)} %collective-permute-done.2.got2), channel_id=1, source_target_pairs={{0,1},{1,0},{2,3},{3,2},{4,5},{5,4},{6,7},{7,6},{8,9},{9,8},{10,11... | collective-permute-start | bytes 98312 | tf_op jit(solution)/shard_map/ppermute | solution.py:525
  29.3 9.0 %shard_map.104 = (bf16[3,640,1152]{2,1,0:T(8,128)(2,1)}, bf16[512,384]{1,0:T(8,128)(2,1)}, f32[512,384]{1,0:T(8,128)}, bf16[128,384]{1,0:T(8,128)(2,1)}, bf16[3,...) custom-call(s32[8]{0:T(128)} %compare_select_fusion.4.sc, s32[128]{0:T(128)} %home.5, s32[4,128]{1,0:T(4,128)} %bitcast.17, ...), custom_call_target="tpu_custom_call" | custom-call | tf_op jit(solution)/shard_map/pallas_call | solution.py:514
  38.6 1.3 collective-permute-done.8.other
  40.6 1.8 %shard_map.105 = bf16[128,128]{1,0:T(8,128)(2,1)} custom-call(s32[8]{0:T(128)} %compare_select_fusion.4.sc, bf16[3,128,128]{2,1,0:T(8,128)(2,1)} %get-tuple-element.21.own, bf16[3,128,128]{2,1,0:T(8,128)(2,1)} %copy-done.2), custom_call_target="tpu_custom_call" | custom-call | tf_op jit(solution)/shard_map/pallas_call | solution.py:514
  42.4 1.3 collective-permute-start.10
  43.6 1.3 collective-permute-start.9
  44.9 8.1 %collective-permute-done.10.got2 = bf16[128,128]{1,0:T(8,128)(2,1)S(1)} collective-permute-done((bf16[128,128]{1,0:T(8,128)(2,1)}, bf16[128,128]{1,0:T(8,128)(2,1)S(1)}, u32[]{:S(2)}, u32[]{:S(2)}) %collective-permute-start.10) | collective-permute-done | bytes 32800 | tf_op jit(solution)/shard_map/ppermute | solution.py:531
  53.1 2.5 %collective-permute-start.12 = (bf16[128,128]{1,0:T(8,128)(2,1)S(1)}, bf16[128,128]{1,0:T(8,128)(2,1)S(1)}, u32[]{:S(2)}, u32[]{:S(2)}) collective-permute-start(bf16[128,128]{1,0:T(8,128)(2,1)S(1)} %collective-permute-done.10.got2), channel_id=1, source_target_pairs={{0,1},{1,0},{2,3},{3,2},{4,5},{5,4},{6,7},{7,6},{8,9},{9,8},{10,11... | collective-permute-start | bytes 98312 | tf_op jit(solution)/shard_map/ppermute | solution.py:525
  55.6 1.8 %collective-permute-start.11 = (bf16[128,128]{1,0:T(8,128)(2,1)S(1)}, bf16[128,128]{1,0:T(8,128)(2,1)S(1)}, u32[]{:S(2)}, u32[]{:S(2)}) collective-permute-start(bf16[128,128]{1,0:T(8,128)(2,1)S(1)} %collective-permute-done.9.got1), channel_id=1, source_target_pairs={{0,1},{1,0},{2,3},{3,2},{4,5},{5,4},{6,7},{7,6},{8,9},{9,8},{10,11... | collective-permute-start | bytes 98312 | tf_op jit(solution)/shard_map/ppermute | solution.py:525
  58.9 7.5 %shard_map.106 = (bf16[3,128,128]{2,1,0:T(8,128)(2,1)}, bf16[32,4,16,128]{3,2,1,0:T(8,128)(2,1)}, bf16[32,4,16,128]{3,2,1,0:T(8,128)(2,1)}, f32[128,384]{1,0:T(8,128)}, bf16[3,128,128]{2,1,0:T(8,128)(2,1)}) custom-call(s32[8]{0:T(128)} %compare_select_fusion.4.sc, s32[128]{0:T(128)} %home.5, s32[4,128]{1,0:T(4,128)} %bitcast.18, ...), custom_call_target="tpu_custom_call" | custom-call | tf_op jit(solution)/shard_map/pallas_call | solution.py:514
  66.7 1.8 %collective-permute-done.16 = bf16[32,4,16,128]{3,2,1,0:T(8,128)(2,1)S(1)} collective-permute-done((bf16[32,4,16,128]{3,2,1,0:T(8,128)(2,1)}, bf16[32,4,16,128]{3,2,1,0:T(8,128)(2,1)S(1)}, u32[]{:S(2)}, u32[]{:S(2)}) %collective-permute-start.16) | collective-permute-done | bytes 524320 | tf_op jit(solution)/shard_map/ppermute | solution.py:525
  68.5 2.0 %add_convert_fusion = bf16[32,4,16,128]{3,2,1,0:T(8,128)(2,1)} fusion(bf16[32,4,16,128]{3,2,1,0:T(8,128)(2,1)S(1)} %collective-permute-done.16, bf16[32,4,16,128]{3,2,1,0:T(8,128)(2,1)} %get-tuple-element.23), kind=kLoop, calls=%fused_computation | loop fusion | flops 1048576 | bytes 1572864 | tf_op jit(solution)/shard_map/convert_element_type | solution.py:590
  70.5 12.3 %all-to-all-start = ((bf16[32,4,16,128]{3,2,1,0:T(8,128)(2,1)}), bf16[32,4,16,128]{3,2,1,0:T(8,128)(2,1)S(1)}, u32[]{:S(2)}, u32[]{:S(2)}) async-start(bf16[32,4,16,128]{3,2,1,0:T(8,128)(2,1)} %add_convert_fusion), calls=%async_computation | async-start | bytes 1048576 | tf_op jit(solution)/shard_map/all_to_all | solution.py:591
  85.1 1.9 %shard_map.107 = bf16[128,128]{1,0:T(8,128)(2,1)} custom-call(s32[8]{0:T(128)} %compare_select_fusion.4.sc, bf16[3,128,128]{2,1,0:T(8,128)(2,1)} %get-tuple-element.26.own, bf16[3,128,128]{2,1,0:T(8,128)(2,1)} %copy-done.3), custom_call_target="tpu_custom_call" | custom-call | tf_op jit(solution)/shard_map/pallas_call | solution.py:514
  87.0 1.3 collective-permute-start.19
  88.3 1.3 collective-permute-start.18
  89.6 4.6 %collective-permute-done.19.got2 = bf16[128,128]{1,0:T(8,128)(2,1)S(1)} collective-permute-done((bf16[128,128]{1,0:T(8,128)(2,1)}, bf16[128,128]{1,0:T(8,128)(2,1)S(1)}, u32[]{:S(2)}, u32[]{:S(2)}) %collective-permute-start.19) | collective-permute-done | bytes 32800 | tf_op jit(solution)/shard_map/ppermute | solution.py:531
  95.0 1.8 %collective-permute-start.20 = (bf16[128,128]{1,0:T(8,128)(2,1)S(1)}, bf16[128,128]{1,0:T(8,128)(2,1)S(1)}, u32[]{:S(2)}, u32[]{:S(2)}) collective-permute-start(bf16[128,128]{1,0:T(8,128)(2,1)S(1)} %collective-permute-done.18.got1), channel_id=1, source_target_pairs={{0,1},{1,0},{2,3},{3,2},{4,5},{5,4},{6,7},{7,6},{8,9},{9,8},{10,11... | collective-permute-start | bytes 98312 | tf_op jit(solution)/shard_map/ppermute | solution.py:525
  98.3 8.2 %shard_map.108 = bf16[32,4,16,128]{3,2,1,0:T(8,128)(2,1)} custom-call(s32[8]{0:T(128)} %compare_select_fusion.4.sc, s32[4,128]{1,0:T(4,128)} %bitcast.19, f32[128,384]{1,0:T(8,128)} %get-tuple-element.25.grad, bf16[3,128,128]{2,1,0:T(8,128)(2,1)} %get-tuple-element.26.own, bf16[3,128,128]{2,1,0:T(8,128)(2,1)} %copy-done.3, bf16[128,128]{1,0:T(8,128)(2,1)} %copy-done.11, ...), custom_call_target="tpu_custom_call" | custom-call | tf_op jit(solution)/shard_map/pallas_call | solution.py:514
  106.5 13.3 %all-to-all-start.1 = ((bf16[32,4,16,128]{3,2,1,0:T(8,128)(2,1)}), bf16[32,4,16,128]{3,2,1,0:T(8,128)(2,1)S(1)}, u32[]{:S(2)}, u32[]{:S(2)}) async-start(bf16[32,4,16,128]{3,2,1,0:T(8,128)(2,1)} %shard_map.108), calls=%async_computation.1 | async-start | bytes 1048576 | tf_op jit(solution)/shard_map/all_to_all | solution.py:601
  119.9 11.6 %all-to-all-done.1 = bf16[32,4,16,128]{3,2,1,0:T(8,128)(2,1)S(1)} async-done(((bf16[32,4,16,128]{3,2,1,0:T(8,128)(2,1)}), bf16[32,4,16,128]{3,2,1,0:T(8,128)(2,1)S(1)}, u32[]{:S(2)}, u32[]{:S(2)}) %all-to-all-start.1) | async-done | bytes 524320 | tf_op jit(solution)/shard_map/all_to_all | solution.py:601
  131.6 12.1 %all_to_all.20 = bf16[8,48,128]{2,1,0:T(8,128)(2,1)S(1)} all-to-all(bf16[8,48,128]{2,1,0:T(8,128)(2,1)S(1)} %maximum_maximum_fusion), channel_id=1, replica_groups=mesh['dp'=4,'x'=4,'zh'=2,'y'=4,'core'=2] {'zh','dp'}, dimensions={0} | all-to-all | bytes 196608 | tf_op jit(solution)/shard_map/all_to_all | solution.py:604
  143.8 14.9 %all_to_all.21.pieces = bf16[32,48,128]{2,1,0:T(8,128)(2,1)} all-to-all(bf16[32,48,128]{2,1,0:T(8,128)(2,1)S(1)} %broadcast_in_dim.33), channel_id=1, replica_groups=mesh['dp'=4,'x'=4,'zh'=2,'y'=4,'core'=2] {'x','y','core'}, dimensions={0} | all-to-all | bytes 786432 | tf_op jit(solution)/shard_map/all_to_all | solution.py:607
  158.6 1.8 %shard_map.109 = (f32[16,1728]{1,0:T(8,128)}, f32[32,512]{1,0:T(8,128)}, f32[32,3456]{1,0:T(8,128)}) custom-call(bf16[32,48,128]{2,1,0:T(8,128)(2,1)} %all_to_all.21.pieces), custom_call_target="tpu_custom_call" | custom-call | tf_op jit(solution)/shard_map/pallas_call | solution.py:514
  (83 shorter events, 15.4 us)
Async XLA Ops:
  4.3 8.6 %collective-permute-start = (bf16[3,64,256]{2,1,0:T(8,128)(2,1)}, bf16[3,64,256]{2,1,0:T(8,128)(2,1)S(1)}, u32[]{:S(2)}, u32[]{:S(2)}) collective-permute-start(bf16[3,64,256]{2,1,0:T(8,128)(2,1)} %shard_map.102.own), channel_id=1, source_target_pairs={{0,1},{1,0},{2,3},{3,2},{4,5},{5,4},{6,7},{7,6},{8,9},{9,8},{10,11... | collective-permute-start | bytes 294920 | tf_op jit(solution)/shard_map/ppermute | solution.py:525
  9.2 19.5 %copy-start = (bf16[80,640]{1,0:T(8,128)(2,1)}, bf16[80,640]{1,0:T(8,128)(2,1)S(1)}, u32[]{:S(2)}) copy-start(bf16[80,640]{1,0:T(8,128)(2,1)S(1)} %fusion.2.w_a) | copy-start | bytes 307204
  9.2 8.6 %collective-permute-start.7 = (bf16[80,640]{1,0:T(8,128)(2,1)S(1)}, bf16[80,640]{1,0:T(8,128)(2,1)S(1)}, u32[]{:S(2)}, u32[]{:S(2)}) collective-permute-start(bf16[80,640]{1,0:T(8,128)(2,1)S(1)} %fusion.2.w_a), channel_id=1, source_target_pairs={{0,192},{64,128},{128,64},{192,0},{1,193},{65,129},{129,65},{193,1... | collective-permute-start | bytes 307208 | tf_op jit(solution)/shard_map/ppermute | solution.py:535
  12.0 8.5 %collective-permute-start.6 = (bf16[80,640]{1,0:T(8,128)(2,1)S(1)}, bf16[80,640]{1,0:T(8,128)(2,1)S(1)}, u32[]{:S(2)}, u32[]{:S(2)}) collective-permute-start(bf16[80,640]{1,0:T(8,128)(2,1)S(1)} %fusion.2.w_a), channel_id=1, source_target_pairs={{0,128},{64,192},{128,0},{192,64},{1,129},{65,193},{129,1},{193,65... | collective-permute-start | bytes 307208 | tf_op jit(solution)/shard_map/ppermute | solution.py:535
  12.0 8.9 %collective-permute-start.5 = (bf16[80,640]{1,0:T(8,128)(2,1)S(1)}, bf16[80,640]{1,0:T(8,128)(2,1)S(1)}, u32[]{:S(2)}, u32[]{:S(2)}) collective-permute-start(bf16[80,640]{1,0:T(8,128)(2,1)S(1)} %fusion.2.w_a), channel_id=1, source_target_pairs={{0,64},{64,0},{128,192},{192,128},{1,65},{65,1},{129,193},{193,129... | collective-permute-start | bytes 307208 | tf_op jit(solution)/shard_map/ppermute | solution.py:535
  15.3 7.6 %collective-permute-start.2 = (bf16[64,256]{1,0:T(8,128)(2,1)}, bf16[64,256]{1,0:T(8,128)(2,1)S(1)}, u32[]{:S(2)}, u32[]{:S(2)}) collective-permute-start(bf16[64,256]{1,0:T(8,128)(2,1)} %shard_map.103), channel_id=1, source_target_pairs={{0,4},{2,6},{4,8},{6,10},{8,12},{10,14},{12,16},{14,18},{16,20},{1... | collective-permute-start | bytes 98312 | tf_op jit(solution)/shard_map/ppermute | solution.py:531
  16.6 11.0 %collective-permute-start.1 = (bf16[64,256]{1,0:T(8,128)(2,1)}, bf16[64,256]{1,0:T(8,128)(2,1)S(1)}, u32[]{:S(2)}, u32[]{:S(2)}) collective-permute-start(bf16[64,256]{1,0:T(8,128)(2,1)} %shard_map.103), channel_id=1, source_target_pairs={{0,2},{2,4},{4,6},{6,8},{8,10},{10,12},{12,14},{14,16},{16,18},{18... | collective-permute-start | bytes 98312 | tf_op jit(solution)/shard_map/ppermute | solution.py:531
  17.9 10.9 %copy-start.7 = (bf16[80,640]{1,0:T(8,128)(2,1)}, bf16[80,640]{1,0:T(8,128)(2,1)S(1)}, u32[]{:S(2)}) copy-start(bf16[80,640]{1,0:T(8,128)(2,1)S(1)} %collective-permute-done.7.w_d) | copy-start | bytes 307204
  17.9 39.5 %collective-permute-start.14 = (bf16[32,3456]{1,0:T(8,128)(2,1)}, bf16[32,3456]{1,0:T(8,128)(2,1)S(1)}, u32[]{:S(2)}, u32[]{:S(2)}) collective-permute-start(bf16[32,3456]{1,0:T(8,128)(2,1)} %w_a.1), channel_id=1, source_target_pairs={{0,128},{64,192},{128,0},{192,64},{1,129},{65,193},{129,1},{193,65... | collective-permute-start | bytes 663560 | tf_op jit(solution)/shard_map/ppermute | solution.py:535
  20.5 8.2 %copy-start.8 = (bf16[80,640]{1,0:T(8,128)(2,1)}, bf16[80,640]{1,0:T(8,128)(2,1)S(1)}, u32[]{:S(2)}) copy-start(bf16[80,640]{1,0:T(8,128)(2,1)S(1)} %collective-permute-done.6.w_c) | copy-start | bytes 307204
  20.5 36.9 %collective-permute-start.13 = (bf16[32,3456]{1,0:T(8,128)(2,1)}, bf16[32,3456]{1,0:T(8,128)(2,1)S(1)}, u32[]{:S(2)}, u32[]{:S(2)}) collective-permute-start(bf16[32,3456]{1,0:T(8,128)(2,1)} %w_a.1), channel_id=1, source_target_pairs={{0,64},{64,0},{128,192},{192,128},{1,65},{65,1},{129,193},{193,129... | collective-permute-start | bytes 663560 | tf_op jit(solution)/shard_map/ppermute | solution.py:535
  20.9 7.8 %copy-start.9 = (bf16[80,640]{1,0:T(8,128)(2,1)}, bf16[80,640]{1,0:T(8,128)(2,1)S(1)}, u32[]{:S(2)}) copy-start(bf16[80,640]{1,0:T(8,128)(2,1)S(1)} %collective-permute-done.5.w_b) | copy-start | bytes 307204
  20.9 36.5 %collective-permute-start.15 = (bf16[32,3456]{1,0:T(8,128)(2,1)}, bf16[32,3456]{1,0:T(8,128)(2,1)S(1)}, u32[]{:S(2)}, u32[]{:S(2)}) collective-permute-start(bf16[32,3456]{1,0:T(8,128)(2,1)} %w_a.1), channel_id=1, source_target_pairs={{0,192},{64,128},{128,64},{192,0},{1,193},{65,129},{129,65},{193,1... | collective-permute-start | bytes 663560 | tf_op jit(solution)/shard_map/ppermute | solution.py:535
  22.9 5.9 %copy-start.14 = (bf16[64,256]{1,0:T(8,128)(2,1)}, bf16[64,256]{1,0:T(8,128)(2,1)S(1)}, u32[]{:S(2)}) copy-start(bf16[64,256]{1,0:T(8,128)(2,1)S(1)} %collective-permute-done.2.got2) | copy-start | bytes 98308
  22.9 5.5 %collective-permute-start.4 = (bf16[64,256]{1,0:T(8,128)(2,1)S(1)}, bf16[64,256]{1,0:T(8,128)(2,1)S(1)}, u32[]{:S(2)}, u32[]{:S(2)}) collective-permute-start(bf16[64,256]{1,0:T(8,128)(2,1)S(1)} %collective-permute-done.2.got2), channel_id=1, source_target_pairs={{0,1},{1,0},{2,3},{3,2},{4,5},{5,4},{6,7},{7,6},{8,9},{9,8},{10,11... | collective-permute-start | bytes 98312 | tf_op jit(solution)/shard_map/ppermute | solution.py:525
  27.5 1.2 collective-permute-start.3
  38.4 1.6 collective-permute-start.8
  42.4 10.7 %collective-permute-start.10 = (bf16[128,128]{1,0:T(8,128)(2,1)}, bf16[128,128]{1,0:T(8,128)(2,1)S(1)}, u32[]{:S(2)}, u32[]{:S(2)}) collective-permute-start(bf16[128,128]{1,0:T(8,128)(2,1)} %shard_map.105), channel_id=1, source_target_pairs={{0,4},{2,6},{4,8},{6,10},{8,12},{10,14},{12,16},{14,18},{16,20},{1... | collective-permute-start | bytes 98312 | tf_op jit(solution)/shard_map/ppermute | solution.py:531
  43.6 11.9 %collective-permute-start.9 = (bf16[128,128]{1,0:T(8,128)(2,1)}, bf16[128,128]{1,0:T(8,128)(2,1)S(1)}, u32[]{:S(2)}, u32[]{:S(2)}) collective-permute-start(bf16[128,128]{1,0:T(8,128)(2,1)} %shard_map.105), channel_id=1, source_target_pairs={{0,2},{2,4},{4,6},{6,8},{8,10},{10,12},{12,14},{14,16},{16,18},{18... | collective-permute-start | bytes 98312 | tf_op jit(solution)/shard_map/ppermute | solution.py:531
  53.1 5.2 %copy-start.16 = (bf16[128,128]{1,0:T(8,128)(2,1)}, bf16[128,128]{1,0:T(8,128)(2,1)S(1)}, u32[]{:S(2)}) copy-start(bf16[128,128]{1,0:T(8,128)(2,1)S(1)} %collective-permute-done.10.got2) | copy-start | bytes 98308
  53.1 4.4 %collective-permute-start.12 = (bf16[128,128]{1,0:T(8,128)(2,1)S(1)}, bf16[128,128]{1,0:T(8,128)(2,1)S(1)}, u32[]{:S(2)}, u32[]{:S(2)}) collective-permute-start(bf16[128,128]{1,0:T(8,128)(2,1)S(1)} %collective-permute-done.10.got2), channel_id=1, source_target_pairs={{0,1},{1,0},{2,3},{3,2},{4,5},{5,4},{6,7},{7,6},{8,9},{9,8},{10,11... | collective-permute-start | bytes 98312 | tf_op jit(solution)/shard_map/ppermute | solution.py:525
  55.6 2.7 %copy-start.17 = (bf16[128,128]{1,0:T(8,128)(2,1)}, bf16[128,128]{1,0:T(8,128)(2,1)S(1)}, u32[]{:S(2)}) copy-start(bf16[128,128]{1,0:T(8,128)(2,1)S(1)} %collective-permute-done.9.got1) | copy-start | bytes 98308
  55.6 2.6 %collective-permute-start.11 = (bf16[128,128]{1,0:T(8,128)(2,1)S(1)}, bf16[128,128]{1,0:T(8,128)(2,1)S(1)}, u32[]{:S(2)}, u32[]{:S(2)}) collective-permute-start(bf16[128,128]{1,0:T(8,128)(2,1)S(1)} %collective-permute-done.9.got1), channel_id=1, source_target_pairs={{0,1},{1,0},{2,3},{3,2},{4,5},{5,4},{6,7},{7,6},{8,9},{9,8},{10,11... | collective-permute-start | bytes 98312 | tf_op jit(solution)/shard_map/ppermute | solution.py:525
  66.4 2.1 %collective-permute-start.16 = (bf16[32,4,16,128]{3,2,1,0:T(8,128)(2,1)}, bf16[32,4,16,128]{3,2,1,0:T(8,128)(2,1)S(1)}, u32[]{:S(2)}, u32[]{:S(2)}) collective-permute-start(bf16[32,4,16,128]{3,2,1,0:T(8,128)(2,1)} %get-tuple-element.24), channel_id=1, source_target_pairs={{0,1},{1,0},{2,3},{3,2},{4,5},{5,4},{6,7},{7,6},{8,9},{9,8},{10,11... | collective-permute-start | bytes 1572872 | tf_op jit(solution)/shard_map/ppermute | solution.py:525
  70.5 35.9 %all-to-all-start = ((bf16[32,4,16,128]{3,2,1,0:T(8,128)(2,1)}), bf16[32,4,16,128]{3,2,1,0:T(8,128)(2,1)S(1)}, u32[]{:S(2)}, u32[]{:S(2)}) async-start(bf16[32,4,16,128]{3,2,1,0:T(8,128)(2,1)} %add_convert_fusion), calls=%async_computation | async-start | bytes 1048576 | tf_op jit(solution)/shard_map/all_to_all | solution.py:591
  82.9 1.6 collective-permute-start.17
  87.0 7.2 %collective-permute-start.19 = (bf16[128,128]{1,0:T(8,128)(2,1)}, bf16[128,128]{1,0:T(8,128)(2,1)S(1)}, u32[]{:S(2)}, u32[]{:S(2)}) collective-permute-start(bf16[128,128]{1,0:T(8,128)(2,1)} %shard_map.107), channel_id=1, source_target_pairs={{0,4},{2,6},{4,8},{6,10},{8,12},{10,14},{12,16},{14,18},{16,20},{1... | collective-permute-start | bytes 98312 | tf_op jit(solution)/shard_map/ppermute | solution.py:531
  88.3 6.7 %collective-permute-start.18 = (bf16[128,128]{1,0:T(8,128)(2,1)}, bf16[128,128]{1,0:T(8,128)(2,1)S(1)}, u32[]{:S(2)}, u32[]{:S(2)}) collective-permute-start(bf16[128,128]{1,0:T(8,128)(2,1)} %shard_map.107), channel_id=1, source_target_pairs={{0,2},{2,4},{4,6},{6,8},{8,10},{10,12},{12,14},{14,16},{16,18},{18... | collective-permute-start | bytes 98312 | tf_op jit(solution)/shard_map/ppermute | solution.py:531
  94.1 3.5 %copy-start.10 = (bf16[128,128]{1,0:T(8,128)(2,1)}, bf16[128,128]{1,0:T(8,128)(2,1)S(1)}, u32[]{:S(2)}) copy-start(bf16[128,128]{1,0:T(8,128)(2,1)S(1)} %collective-permute-done.19.got2) | copy-start | bytes 98308
  94.1 2.7 %collective-permute-start.21 = (bf16[128,128]{1,0:T(8,128)(2,1)S(1)}, bf16[128,128]{1,0:T(8,128)(2,1)S(1)}, u32[]{:S(2)}, u32[]{:S(2)}) collective-permute-start(bf16[128,128]{1,0:T(8,128)(2,1)S(1)} %collective-permute-done.19.got2), channel_id=1, source_target_pairs={{0,1},{1,0},{2,3},{3,2},{4,5},{5,4},{6,7},{7,6},{8,9},{9,8},{10,11... | collective-permute-start | bytes 98312 | tf_op jit(solution)/shard_map/ppermute | solution.py:525
  95.0 2.6 %collective-permute-start.20 = (bf16[128,128]{1,0:T(8,128)(2,1)S(1)}, bf16[128,128]{1,0:T(8,128)(2,1)S(1)}, u32[]{:S(2)}, u32[]{:S(2)}) collective-permute-start(bf16[128,128]{1,0:T(8,128)(2,1)S(1)} %collective-permute-done.18.got1), channel_id=1, source_target_pairs={{0,1},{1,0},{2,3},{3,2},{4,5},{5,4},{6,7},{7,6},{8,9},{9,8},{10,11... | collective-permute-start | bytes 98312 | tf_op jit(solution)/shard_map/ppermute | solution.py:525
  106.5 24.9 %all-to-all-start.1 = ((bf16[32,4,16,128]{3,2,1,0:T(8,128)(2,1)}), bf16[32,4,16,128]{3,2,1,0:T(8,128)(2,1)S(1)}, u32[]{:S(2)}, u32[]{:S(2)}) async-start(bf16[32,4,16,128]{3,2,1,0:T(8,128)(2,1)} %shard_map.108), calls=%async_computation.1 | async-start | bytes 1048576 | tf_op jit(solution)/shard_map/all_to_all | solution.py:601
  (14 other events, 12.5 us)

commit v3 on v2

--- a/solution.py
+++ b/solution.py
@@ -259,23 +259,30 @@
     out[...] = total.astype(BF)
 
 
-def stage_one_kernel(sc, home, links, x_ref, own, other, got1, got2, sw1, sw2, w_a, w_b, w_c, w_d,
-                     taps, hid, slope, red, rec2, down_out,
-                     recs, low_rows, high_rows, w_all, w_one):
+def both_halves(s, dp, w_all, d):
+    at = jnp.bitwise_xor(jnp.int32(d), dp)
+    mine, other = w_all[at].astype(F32), w_all[4 + at].astype(F32)
+    return jnp.where(s.core == 0, mine, other), jnp.where(s.core == 0, other, mine)
+
+
+def stage_one_kernel(sc, home, links, x_ref, own, other, got1, got2, sw1, sw2, *rest):
+    weights, (taps, hid, slope, red, rec2, down_out,
+                       recs, low_rows, high_rows, w_all, w_one) = rest[:8], rest[8:]
     s = where_am_i(sc)
     dp = sc[7]
     gather_records(recs, own, other, (got1, got2), (sw1, sw2))
     low_rows[...] = rim_rows(ONE, 0)
     high_rows[...] = rim_rows(ONE, 60)
-    for k, w in enumerate((w_a, w_b, w_c, w_d)):
-        w_all[k] = w[...]
+    for k in range(8):
+        w_all[k] = weights[k][:, :1408]
     for d in range(4):
-        at = jnp.bitwise_xor(jnp.int32(d), dp)
-        for dx in range(3):
-            w_one[dx * 64 + d * 16 : dx * 64 + d * 16 + 16, :] = w_all[
-                at, dx * 16 : dx * 16 + 16, 0:576
-            ]
-        down_out[d * 32 : d * 32 + 32, :] = w_all[at, 48:80, 0:512]
+        first, second = both_halves(s, dp, w_all, d)
+        w = jnp.concatenate([first[:, :896], second[:, :896]], axis=1)
+        w_one[d * 16 : d * 16 + 16, :] = w[:, :576].astype(BF)
+        w_one[64 + d * 16 : 80 + d * 16, :] = pltpu.roll(w, 1792 - 576, 1)[:, :576].astype(BF)
+        w_one[128 + d * 16 : 144 + d * 16, :] = w[:, 1152:1728].astype(BF)
+        down_out[d * 32 : d * 32 + 16, :] = first[:, 896:].astype(BF)
+        down_out[d * 32 + 16 : d * 32 + 32, :] = second[:, 896:].astype(BF)
     order = parity_order()
 
     @pl.loop(0, 3)
@@ -318,21 +325,22 @@
 
 
 def stage_two_kernel(scale, sc, home, links, red, cot, own, other, got1, got2, sw1, sw2,
-                     w_a, w_b, w_c, w_d, out, keep, give, grad, brec,
-                     recs, low_rows, high_rows, w_all, w_two, taps, spread):
+                     *rest):
+    weights, (out, keep, give, grad, brec, recs, low_rows, high_rows, w_all, w_two, taps,
+              spread) = rest[:8], rest[8:]
     s = where_am_i(sc)
     dp = sc[7]
     gather_records(recs, own, other, (got1, got2), (sw1, sw2))
     low_rows[...] = rim_rows(TWO, 0)
     high_rows[...] = rim_rows(TWO, 14)
-    for k, w in enumerate((w_a, w_b, w_c, w_d)):
-        w_all[k] = w[...]
+    for k in range(8):
+        w_all[k] = weights[k][:, 1408:]
     for d in range(4):
-        at = jnp.bitwise_xor(jnp.int32(d), dp)
+        first, second = both_halves(s, dp, w_all, d)
         for dx in range(3):
-            w_two[dx * 128 + d * 32 : dx * 128 + d * 32 + 32, :] = w_all[
-                at, :, dx * 1152 : dx * 1152 + 1152
-            ]
+            row = dx * 128 + d * 32
+            w_two[row : row + 16, :] = first[:, dx * 1152 : dx * 1152 + 1152].astype(BF)
+            w_two[row + 16 : row + 32, :] = second[:, dx * 1152 : dx * 1152 + 1152].astype(BF)
     for i in range(3):
         p = s.a + jnp.minimum(i, s.n - 1)
         block, low, high = extended(
@@ -565,25 +573,28 @@
     x = features[0]
     (rec_one,) = call(faces_kernel, (sc, patch_home), (x,), [((3, 64, 256), BF)], [])
     rims_one = exchange(ONE, 1, sc, rec_one)
-    rows_one = jnp.pad(conv_one.reshape(16, 3, 576).swapaxes(0, 1).reshape(48, 576), ((0, 0), (0, 64)))
-    w_one = gathered(jnp.concatenate([rows_one, jnp.pad(down_weight, ((0, 0), (0, 128)))]))
-    w_two = gathered(conv_two)
+    one_half = jnp.where(core == 0, conv_one[:, :896], jnp.pad(conv_one[:, 896:], ((0, 0), (0, 64))))
+    halves = [one_half]
+    for w in (down_weight, conv_two):
+        halves.append(lax.dynamic_index_in_dim(w.reshape(2, 16, -1), core, 0, keepdims=False))
+    mine = gathered(jnp.concatenate(halves, axis=1))
+    weights = mine + [swap_cores(w) for w in mine]
     taps, hid, slope, red, rec_two, down_full = call(
         stage_one_kernel, (sc, patch_home, links),
-        (x, rec_one, *rims_one, *w_one),
+        (x, rec_one, *rims_one, *weights),
         [((3, 640, 1152), BF), ((512, 384), BF), ((512, 384), F32), ((128, 384), BF),
          ((3, 128, 128), BF), ((128, 512), BF)],
-        [((10, 64, 256), BF), ((128, 1152), BF), ((128, 1152), BF), ((4, 80, 640), BF),
+        [((10, 64, 256), BF), ((128, 1152), BF), ((128, 1152), BF), ((8, 16, 1408), BF),
          ((192, 576), BF)],
     )
     rims_two = exchange(TWO, 1, sc, rec_two)
     cells = lax.axis_size("dp") * patch_links.shape[0] * 128
     out, keep, give, grad, rec_back = call(
         functools.partial(stage_two_kernel, float(cells) ** (-0.5)), (sc, patch_home, links),
-        (red, cotangent[0], rec_two, *rims_two, *w_two),
+        (red, cotangent[0], rec_two, *rims_two, *weights),
         [((3, 128, 128), BF), ((32, 4, 16, 128), BF), ((32, 4, 16, 128), BF),
          ((128, 384), F32), ((3, 128, 128), BF)],
-        [((10, 128, 128), BF), ((128, 256), BF), ((128, 256), BF), ((4, 32, 3456), BF),
+        [((10, 128, 128), BF), ((128, 256), BF), ((128, 256), BF), ((8, 16, 3456), BF),
          ((384, 1152), BF), ((1152, 768), BF), ((384, 768), BF)],
     )
     rims_back = exchange(TWO, 2, sc, rec_back)

time: 161 us -> 179 us (1.11)
  waiting for transfers between devices: 32.5 us -> 45.6 us
  starting transfers between devices: 56.7 us -> 59.8 us
    ppermute x6, waiting for transfers between devices: 12.7 us -> 21.3 us  [chips_on(): return lax.ppermute(v, SPACE, up + down)]
    ppermute x6 -> x3, waiting for transfers between devices: 1.09 us -> 5.53 us  [across(): lax.ppermute(v, axis, [(i, i ^ k) for i in range(lax.axis_size(axis))])]
    ppermute x10 -> x14, starting transfers between devices: 15.8 us -> 18.2 us  [swap_cores(): return lax.ppermute(v, 'core', [(0, 1), (1, 0)])]
    all_to_all x1, starting transfers between devices: 12.3 us -> 14.5 us  [on_device(): two = lax.all_to_all(two, ('x', 'y', 'core'), 0, 0, tiled=True)]
    ppermute x6 -> x3, starting transfers between devices: 7.55 us -> 5.63 us  [across(): lax.ppermute(v, axis, [(i, i ^ k) for i in range(lax.axis_size(axis))])]
    unnamed x44 -> x48, local copies, waits for them, and re-layouts: 3.71 us -> 3.88 us
    ppermute x10 -> x14, waiting for transfers between devices: 7.14 us -> 7.23 us  [swap_cores(): return lax.ppermute(v, 'core', [(0, 1), (1, 0)])]
  transfers between devices with their start and end apart: 24 -> 25, of which waited for: 11 -> 13; matrix products, arithmetic and copies ran while one was open for 1% -> 1% of each run, Pallas kernels for 14% -> 8%
where the time goes in v3:
time: 179 us; the launch traced here: 178 us
  starting transfers between devices  59.8 us (33%)
  waiting for transfers between devices  45.6 us (25%)
  Pallas kernels  34.6 us (19%)
  blocking collectives  27.1 us (15%)
  local copies, waits for them, and re-layouts  5.46 us (3%)
  other arithmetic  4.4 us (2%)
    pallas_call x8, Pallas kernels, call(): pl.pallas_call(kernel, out_shape=[jax.ShapeDtypeStruct(*o) for o in outs]...  34.6 us
    ppermute x6, waiting for transfers between devices, chips_on(): return lax.ppermute(v, SPACE, up + down)  21.3 us
    ppermute x14, starting transfers between devices, swap_cores(): return lax.ppermute(v, 'core', [(0, 1), (1, 0)])  18.2 us
    all_to_all x1, blocking collectives, on_device(): pieces = lax.all_to_all(copies, ('x', 'y', 'core'), 0, 0, tiled=True)  14.9 us
    all_to_all x1, starting transfers between devices, on_device(): two = lax.all_to_all(two, ('x', 'y', 'core'), 0, 0, tiled=True)  14.5 us
    all_to_all x1, starting transfers between devices, on_device(): small = lax.all_to_all(small, ('x', 'y', 'core'), 0, 0, tiled=True)  13.7 us
    all_to_all x1, blocking collectives, on_device(): lax.all_to_all(jnp.concatenate([mine, mine]), ('zh', 'dp'), 0, 0, tiled=T...  12.2 us
    all_to_all x1, waiting for transfers between devices, on_device(): small = lax.all_to_all(small, ('x', 'y', 'core'), 0, 0, tiled=True)  11.6 us
  transfers between devices with their start and end apart: 25, of which 13 were waited for; matrix products, arithmetic and copies ran while one was open for 1% of the time, Pallas kernels for 8%

profile of v3, /device:TPU:1, one launch (start us, length us, event | category | flops | bytes accessed | tf_op | source)
XLA Modules:
  0.0 177.8 jit_solution(15437724118944853948)
XLA Ops:
  3.0 5.2 %collective-permute-start.7 = (bf16[16,4864]{1,0:T(8,128)(2,1)S(1)}, bf16[16,4864]{1,0:T(8,128)(2,1)S(1)}, u32[]{:S(2)}, u32[]{:S(2)}) collective-permute-start(bf16[16,4864]{1,0:T(8,128)(2,1)S(1)} %pad_maximum_fusion.rest_0_), channel_id=1, source_target_pairs={{0,192},{64,128},{128,64},{192,0},{1,193},{65,129},{129,65},{193,1... | collective-permute-start | bytes 466952 | tf_op jit(solution)/shard_map/ppermute | solution.py:543
  10.0 2.3 %shard_map.102.own = bf16[3,64,256]{2,1,0:T(8,128)(2,1)} custom-call(s32[8]{0:T(128)} %compare_select_fusion.4.sc, s32[128]{0:T(128)} %home.5, bf16[3,64,1024]{2,1,0:T(8,128)(2,1)} %bitcast.17), custom_call_target="tpu_custom_call" | custom-call | tf_op jit(solution)/shard_map/pallas_call | solution.py:522
  12.2 2.0 %collective-permute-start = (bf16[3,64,256]{2,1,0:T(8,128)(2,1)}, bf16[3,64,256]{2,1,0:T(8,128)(2,1)S(1)}, u32[]{:S(2)}, u32[]{:S(2)}) collective-permute-start(bf16[3,64,256]{2,1,0:T(8,128)(2,1)} %shard_map.102.own), channel_id=1, source_target_pairs={{0,1},{1,0},{2,3},{3,2},{4,5},{5,4},{6,7},{7,6},{8,9},{9,8},{10,11... | collective-permute-start | bytes 294920 | tf_op jit(solution)/shard_map/ppermute | solution.py:533
  15.0 5.5 %collective-permute-done.6.rest_2_ = bf16[16,4864]{1,0:T(8,128)(2,1)S(1)} collective-permute-done((bf16[16,4864]{1,0:T(8,128)(2,1)S(1)}, bf16[16,4864]{1,0:T(8,128)(2,1)S(1)}, u32[]{:S(2)}, u32[]{:S(2)}) %collective-permute-start.6) | collective-permute-done | bytes 155680 | tf_op jit(solution)/shard_map/ppermute | solution.py:543
  20.5 1.4 collective-permute-start.10
  22.6 1.8 shard_map.103
  24.4 1.3 collective-permute-start.2
  25.7 5.1 %collective-permute-done.2.got2 = bf16[64,256]{1,0:T(8,128)(2,1)S(1)} collective-permute-done((bf16[64,256]{1,0:T(8,128)(2,1)}, bf16[64,256]{1,0:T(8,128)(2,1)S(1)}, u32[]{:S(2)}, u32[]{:S(2)}) %collective-permute-start.2) | collective-permute-done | bytes 32800 | tf_op jit(solution)/shard_map/ppermute | solution.py:539
  30.7 1.3 collective-permute-start.1
  32.0 3.6 %collective-permute-done.1.got1 = bf16[64,256]{1,0:T(8,128)(2,1)S(1)} collective-permute-done((bf16[64,256]{1,0:T(8,128)(2,1)}, bf16[64,256]{1,0:T(8,128)(2,1)S(1)}, u32[]{:S(2)}, u32[]{:S(2)}) %collective-permute-start.1) | collective-permute-done | bytes 32800 | tf_op jit(solution)/shard_map/ppermute | solution.py:539
  38.3 9.4 %shard_map.104 = (bf16[3,640,1152]{2,1,0:T(8,128)(2,1)}, bf16[512,384]{1,0:T(8,128)(2,1)}, f32[512,384]{1,0:T(8,128)}, bf16[128,384]{1,0:T(8,128)(2,1)}, bf16[3,...) custom-call(s32[8]{0:T(128)} %compare_select_fusion.4.sc, s32[128]{0:T(128)} %home.5, s32[4,128]{1,0:T(4,128)} %bitcast.20, ...), custom_call_target="tpu_custom_call" | custom-call | tf_op jit(solution)/shard_map/pallas_call | solution.py:522
  48.0 1.3 collective-permute-done.12.other
  50.0 1.8 shard_map.105
  51.8 1.3 collective-permute-start.14
  53.0 1.3 collective-permute-start.13
  54.3 8.0 %collective-permute-done.14.got2 = bf16[128,128]{1,0:T(8,128)(2,1)S(1)} collective-permute-done((bf16[128,128]{1,0:T(8,128)(2,1)}, bf16[128,128]{1,0:T(8,128)(2,1)S(1)}, u32[]{:S(2)}, u32[]{:S(2)}) %collective-permute-start.14) | collective-permute-done | bytes 32800 | tf_op jit(solution)/shard_map/ppermute | solution.py:539
  62.4 7.9 %collective-permute-start.16 = (bf16[128,128]{1,0:T(8,128)(2,1)S(1)}, bf16[128,128]{1,0:T(8,128)(2,1)S(1)}, u32[]{:S(2)}, u32[]{:S(2)}) collective-permute-start(bf16[128,128]{1,0:T(8,128)(2,1)S(1)} %collective-permute-done.14.got2), channel_id=1, source_target_pairs={{0,1},{1,0},{2,3},{3,2},{4,5},{5,4},{6,7},{7,6},{8,9},{9,8},{10,11... | collective-permute-start | bytes 98312 | tf_op jit(solution)/shard_map/ppermute | solution.py:533
  70.3 1.8 %collective-permute-start.15 = (bf16[128,128]{1,0:T(8,128)(2,1)S(1)}, bf16[128,128]{1,0:T(8,128)(2,1)S(1)}, u32[]{:S(2)}, u32[]{:S(2)}) collective-permute-start(bf16[128,128]{1,0:T(8,128)(2,1)S(1)} %collective-permute-done.13.got1), channel_id=1, source_target_pairs={{0,1},{1,0},{2,3},{3,2},{4,5},{5,4},{6,7},{7,6},{8,9},{9,8},{10,11... | collective-permute-start | bytes 98312 | tf_op jit(solution)/shard_map/ppermute | solution.py:533
  73.5 7.4 %shard_map.106 = (bf16[3,128,128]{2,1,0:T(8,128)(2,1)}, bf16[32,4,16,128]{3,2,1,0:T(8,128)(2,1)}, bf16[32,4,16,128]{3,2,1,0:T(8,128)(2,1)}, f32[128,384]{1,0:T(8,128)}, bf16[3,128,128]{2,1,0:T(8,128)(2,1)}) custom-call(s32[8]{0:T(128)} %compare_select_fusion.4.sc, s32[128]{0:T(128)} %home.5, s32[4,128]{1,0:T(4,128)} %bitcast.21, ...), custom_call_target="tpu_custom_call" | custom-call | tf_op jit(solution)/shard_map/pallas_call | solution.py:522
  81.3 1.8 collective-permute-done.17
  83.1 2.1 %add_convert_fusion = bf16[32,4,16,128]{3,2,1,0:T(8,128)(2,1)} fusion(bf16[32,4,16,128]{3,2,1,0:T(8,128)(2,1)S(1)} %collective-permute-done.17, bf16[32,4,16,128]{3,2,1,0:T(8,128)(2,1)} %get-tuple-element.23), kind=kLoop, calls=%fused_computation | loop fusion | flops 1048576 | bytes 1572864 | tf_op jit(solution)/shard_map/convert_element_type | solution.py:601
  85.2 14.5 %all-to-all-start = ((bf16[32,4,16,128]{3,2,1,0:T(8,128)(2,1)}), bf16[32,4,16,128]{3,2,1,0:T(8,128)(2,1)S(1)}, u32[]{:S(2)}, u32[]{:S(2)}) async-start(bf16[32,4,16,128]{3,2,1,0:T(8,128)(2,1)} %add_convert_fusion), calls=%async_computation | async-start | bytes 1048576 | tf_op jit(solution)/shard_map/all_to_all | solution.py:602
  101.9 1.9 %shard_map.107 = bf16[128,128]{1,0:T(8,128)(2,1)} custom-call(s32[8]{0:T(128)} %compare_select_fusion.4.sc, bf16[3,128,128]{2,1,0:T(8,128)(2,1)} %get-tuple-element.26.own, bf16[3,128,128]{2,1,0:T(8,128)(2,1)} %copy-done.11), custom_call_target="tpu_custom_call" | custom-call | tf_op jit(solution)/shard_map/pallas_call | solution.py:522
  105.1 1.3 collective-permute-start.19
  106.4 4.6 %collective-permute-done.20.got2 = bf16[128,128]{1,0:T(8,128)(2,1)S(1)} collective-permute-done((bf16[128,128]{1,0:T(8,128)(2,1)}, bf16[128,128]{1,0:T(8,128)(2,1)S(1)}, u32[]{:S(2)}, u32[]{:S(2)}) %collective-permute-start.20) | collective-permute-done | bytes 32800 | tf_op jit(solution)/shard_map/ppermute | solution.py:539
  111.8 1.8 %collective-permute-start.21 = (bf16[128,128]{1,0:T(8,128)(2,1)S(1)}, bf16[128,128]{1,0:T(8,128)(2,1)S(1)}, u32[]{:S(2)}, u32[]{:S(2)}) collective-permute-start(bf16[128,128]{1,0:T(8,128)(2,1)S(1)} %collective-permute-done.19.got1), channel_id=1, source_target_pairs={{0,1},{1,0},{2,3},{3,2},{4,5},{5,4},{6,7},{7,6},{8,9},{9,8},{10,11... | collective-permute-start | bytes 98312 | tf_op jit(solution)/shard_map/ppermute | solution.py:533
  115.1 8.2 %shard_map.108 = bf16[32,4,16,128]{3,2,1,0:T(8,128)(2,1)} custom-call(s32[8]{0:T(128)} %compare_select_fusion.4.sc, s32[4,128]{1,0:T(4,128)} %bitcast.22, f32[128,384]{1,0:T(8,128)} %get-tuple-element.25.grad, bf16[3,128,128]{2,1,0:T(8,128)(2,1)} %get-tuple-element.26.own, bf16[3,128,128]{2,1,0:T(8,128)(2,1)} %copy-done.11, bf16[128,128]{1,0:T(8,128)(2,1)} %copy-done.16, ...), custom_call_target="tpu_custom_call" | custom-call | tf_op jit(solution)/shard_map/pallas_call | solution.py:522
  123.4 13.7 %all-to-all-start.1 = ((bf16[32,4,16,128]{3,2,1,0:T(8,128)(2,1)}), bf16[32,4,16,128]{3,2,1,0:T(8,128)(2,1)S(1)}, u32[]{:S(2)}, u32[]{:S(2)}) async-start(bf16[32,4,16,128]{3,2,1,0:T(8,128)(2,1)} %shard_map.108), calls=%async_computation.1 | async-start | bytes 1048576 | tf_op jit(solution)/shard_map/all_to_all | solution.py:612
  137.1 11.6 %all-to-all-done.1 = bf16[32,4,16,128]{3,2,1,0:T(8,128)(2,1)S(1)} async-done(((bf16[32,4,16,128]{3,2,1,0:T(8,128)(2,1)}), bf16[32,4,16,128]{3,2,1,0:T(8,128)(2,1)S(1)}, u32[]{:S(2)}, u32[]{:S(2)}) %all-to-all-start.1) | async-done | bytes 524320 | tf_op jit(solution)/shard_map/all_to_all | solution.py:612
  148.8 12.2 %all_to_all.20 = bf16[8,48,128]{2,1,0:T(8,128)(2,1)S(1)} all-to-all(bf16[8,48,128]{2,1,0:T(8,128)(2,1)S(1)} %maximum_maximum_fusion), channel_id=1, replica_groups=mesh['dp'=4,'x'=4,'zh'=2,'y'=4,'core'=2] {'zh','dp'}, dimensions={0} | all-to-all | bytes 196608 | tf_op jit(solution)/shard_map/all_to_all | solution.py:615
  161.1 14.9 %all_to_all.21.pieces = bf16[32,48,128]{2,1,0:T(8,128)(2,1)} all-to-all(bf16[32,48,128]{2,1,0:T(8,128)(2,1)S(1)} %broadcast_in_dim.33), channel_id=1, replica_groups=mesh['dp'=4,'x'=4,'zh'=2,'y'=4,'core'=2] {'x','y','core'}, dimensions={0} | all-to-all | bytes 786432 | tf_op jit(solution)/shard_map/all_to_all | solution.py:618
  175.9 1.8 %shard_map.109 = (f32[16,1728]{1,0:T(8,128)}, f32[32,512]{1,0:T(8,128)}, f32[32,3456]{1,0:T(8,128)}) custom-call(bf16[32,48,128]{2,1,0:T(8,128)(2,1)} %all_to_all.21.pieces), custom_call_target="tpu_custom_call" | custom-call | tf_op jit(solution)/shard_map/pallas_call | solution.py:522
  (91 shorter events, 17.0 us)
Async XLA Ops:
  3.0 34.6 %copy-start.1 = (bf16[16,4864]{1,0:T(8,128)(2,1)}, bf16[16,4864]{1,0:T(8,128)(2,1)S(1)}, u32[]{:S(2)}) copy-start(bf16[16,4864]{1,0:T(8,128)(2,1)S(1)} %pad_maximum_fusion.rest_0_) | copy-start | bytes 466948
  3.0 11.3 %collective-permute-start.7 = (bf16[16,4864]{1,0:T(8,128)(2,1)S(1)}, bf16[16,4864]{1,0:T(8,128)(2,1)S(1)}, u32[]{:S(2)}, u32[]{:S(2)}) collective-permute-start(bf16[16,4864]{1,0:T(8,128)(2,1)S(1)} %pad_maximum_fusion.rest_0_), channel_id=1, source_target_pairs={{0,192},{64,128},{128,64},{192,0},{1,193},{65,129},{129,65},{193,1... | collective-permute-start | bytes 466952 | tf_op jit(solution)/shard_map/ppermute | solution.py:543
  8.2 12.3 %collective-permute-start.6 = (bf16[16,4864]{1,0:T(8,128)(2,1)S(1)}, bf16[16,4864]{1,0:T(8,128)(2,1)S(1)}, u32[]{:S(2)}, u32[]{:S(2)}) collective-permute-start(bf16[16,4864]{1,0:T(8,128)(2,1)S(1)} %pad_maximum_fusion.rest_0_), channel_id=1, source_target_pairs={{0,128},{64,192},{128,0},{192,64},{1,129},{65,193},{129,1},{193,65... | collective-permute-start | bytes 466952 | tf_op jit(solution)/shard_map/ppermute | solution.py:543
  8.2 13.6 %collective-permute-start.5 = (bf16[16,4864]{1,0:T(8,128)(2,1)S(1)}, bf16[16,4864]{1,0:T(8,128)(2,1)S(1)}, u32[]{:S(2)}, u32[]{:S(2)}) collective-permute-start(bf16[16,4864]{1,0:T(8,128)(2,1)S(1)} %pad_maximum_fusion.rest_0_), channel_id=1, source_target_pairs={{0,64},{64,0},{128,192},{192,128},{1,65},{65,1},{129,193},{193,129... | collective-permute-start | bytes 466952 | tf_op jit(solution)/shard_map/ppermute | solution.py:543
  12.2 9.7 %collective-permute-start = (bf16[3,64,256]{2,1,0:T(8,128)(2,1)}, bf16[3,64,256]{2,1,0:T(8,128)(2,1)S(1)}, u32[]{:S(2)}, u32[]{:S(2)}) collective-permute-start(bf16[3,64,256]{2,1,0:T(8,128)(2,1)} %shard_map.102.own), channel_id=1, source_target_pairs={{0,1},{1,0},{2,3},{3,2},{4,5},{5,4},{6,7},{7,6},{8,9},{9,8},{10,11... | collective-permute-start | bytes 294920 | tf_op jit(solution)/shard_map/ppermute | solution.py:533
  14.3 22.0 %collective-permute-start.8 = (bf16[16,4864]{1,0:T(8,128)(2,1)S(1)}, bf16[16,4864]{1,0:T(8,128)(2,1)S(1)}, u32[]{:S(2)}, u32[]{:S(2)}) collective-permute-start(bf16[16,4864]{1,0:T(8,128)(2,1)S(1)} %pad_maximum_fusion.rest_0_), channel_id=1, source_target_pairs={{0,1},{1,0},{2,3},{3,2},{4,5},{5,4},{6,7},{7,6},{8,9},{9,8},{10,11... | collective-permute-start | bytes 466952 | tf_op jit(solution)/shard_map/ppermute | solution.py:533
  14.3 23.3 %copy-start.2 = (bf16[16,4864]{1,0:T(8,128)(2,1)}, bf16[16,4864]{1,0:T(8,128)(2,1)S(1)}, u32[]{:S(2)}) copy-start(bf16[16,4864]{1,0:T(8,128)(2,1)S(1)} %collective-permute-done.7.rest_3_) | copy-start | bytes 466948
  14.3 23.2 %collective-permute-start.11 = (bf16[16,4864]{1,0:T(8,128)(2,1)S(1)}, bf16[16,4864]{1,0:T(8,128)(2,1)S(1)}, u32[]{:S(2)}, u32[]{:S(2)}) collective-permute-start(bf16[16,4864]{1,0:T(8,128)(2,1)S(1)} %collective-permute-done.7.rest_3_), channel_id=1, source_target_pairs={{0,1},{1,0},{2,3},{3,2},{4,5},{5,4},{6,7},{7,6},{8,9},{9,8},{10,11... | collective-permute-start | bytes 466952 | tf_op jit(solution)/shard_map/ppermute | solution.py:533
  20.5 17.0 %copy-start.3 = (bf16[16,4864]{1,0:T(8,128)(2,1)}, bf16[16,4864]{1,0:T(8,128)(2,1)S(1)}, u32[]{:S(2)}) copy-start(bf16[16,4864]{1,0:T(8,128)(2,1)S(1)} %collective-permute-done.6.rest_2_) | copy-start | bytes 466948
  20.5 17.0 %collective-permute-start.10 = (bf16[16,4864]{1,0:T(8,128)(2,1)S(1)}, bf16[16,4864]{1,0:T(8,128)(2,1)S(1)}, u32[]{:S(2)}, u32[]{:S(2)}) collective-permute-start(bf16[16,4864]{1,0:T(8,128)(2,1)S(1)} %collective-permute-done.6.rest_2_), channel_id=1, source_target_pairs={{0,1},{1,0},{2,3},{3,2},{4,5},{5,4},{6,7},{7,6},{8,9},{9,8},{10,11... | collective-permute-start | bytes 466952 | tf_op jit(solution)/shard_map/ppermute | solution.py:533
  21.9 15.7 %copy-start.4 = (bf16[16,4864]{1,0:T(8,128)(2,1)}, bf16[16,4864]{1,0:T(8,128)(2,1)S(1)}, u32[]{:S(2)}) copy-start(bf16[16,4864]{1,0:T(8,128)(2,1)S(1)} %collective-permute-done.5.rest_1_) | copy-start | bytes 466948
  21.9 15.6 %collective-permute-start.9 = (bf16[16,4864]{1,0:T(8,128)(2,1)S(1)}, bf16[16,4864]{1,0:T(8,128)(2,1)S(1)}, u32[]{:S(2)}, u32[]{:S(2)}) collective-permute-start(bf16[16,4864]{1,0:T(8,128)(2,1)S(1)} %collective-permute-done.5.rest_1_), channel_id=1, source_target_pairs={{0,1},{1,0},{2,3},{3,2},{4,5},{5,4},{6,7},{7,6},{8,9},{9,8},{10,11... | collective-permute-start | bytes 466952 | tf_op jit(solution)/shard_map/ppermute | solution.py:533
  24.4 6.4 %collective-permute-start.2 = (bf16[64,256]{1,0:T(8,128)(2,1)}, bf16[64,256]{1,0:T(8,128)(2,1)S(1)}, u32[]{:S(2)}, u32[]{:S(2)}) collective-permute-start(bf16[64,256]{1,0:T(8,128)(2,1)} %shard_map.103), channel_id=1, source_target_pairs={{0,4},{2,6},{4,8},{6,10},{8,12},{10,14},{12,16},{14,18},{16,20},{1... | collective-permute-start | bytes 98312 | tf_op jit(solution)/shard_map/ppermute | solution.py:539
  30.7 6.8 %copy-start.12 = (bf16[64,256]{1,0:T(8,128)(2,1)}, bf16[64,256]{1,0:T(8,128)(2,1)S(1)}, u32[]{:S(2)}) copy-start(bf16[64,256]{1,0:T(8,128)(2,1)S(1)} %collective-permute-done.2.got2) | copy-start | bytes 98308
  30.7 4.9 %collective-permute-start.1 = (bf16[64,256]{1,0:T(8,128)(2,1)}, bf16[64,256]{1,0:T(8,128)(2,1)S(1)}, u32[]{:S(2)}, u32[]{:S(2)}) collective-permute-start(bf16[64,256]{1,0:T(8,128)(2,1)} %shard_map.103), channel_id=1, source_target_pairs={{0,2},{2,4},{4,6},{6,8},{8,10},{10,12},{12,14},{14,16},{16,18},{18... | collective-permute-start | bytes 98312 | tf_op jit(solution)/shard_map/ppermute | solution.py:539
  35.6 1.5 collective-permute-start.4
  36.3 1.2 collective-permute-start.3
  47.7 1.6 collective-permute-start.12
  51.8 10.6 %collective-permute-start.14 = (bf16[128,128]{1,0:T(8,128)(2,1)}, bf16[128,128]{1,0:T(8,128)(2,1)S(1)}, u32[]{:S(2)}, u32[]{:S(2)}) collective-permute-start(bf16[128,128]{1,0:T(8,128)(2,1)} %shard_map.105), channel_id=1, source_target_pairs={{0,4},{2,6},{4,8},{6,10},{8,12},{10,14},{12,16},{14,18},{16,20},{1... | collective-permute-start | bytes 98312 | tf_op jit(solution)/shard_map/ppermute | solution.py:539
  53.0 17.3 %collective-permute-start.13 = (bf16[128,128]{1,0:T(8,128)(2,1)}, bf16[128,128]{1,0:T(8,128)(2,1)S(1)}, u32[]{:S(2)}, u32[]{:S(2)}) collective-permute-start(bf16[128,128]{1,0:T(8,128)(2,1)} %shard_map.105), channel_id=1, source_target_pairs={{0,2},{2,4},{4,6},{6,8},{8,10},{10,12},{12,14},{14,16},{16,18},{18... | collective-permute-start | bytes 98312 | tf_op jit(solution)/shard_map/ppermute | solution.py:539
  62.4 10.6 %copy-start.20 = (bf16[128,128]{1,0:T(8,128)(2,1)}, bf16[128,128]{1,0:T(8,128)(2,1)S(1)}, u32[]{:S(2)}) copy-start(bf16[128,128]{1,0:T(8,128)(2,1)S(1)} %collective-permute-done.14.got2) | copy-start | bytes 98308
  62.4 9.7 %collective-permute-start.16 = (bf16[128,128]{1,0:T(8,128)(2,1)S(1)}, bf16[128,128]{1,0:T(8,128)(2,1)S(1)}, u32[]{:S(2)}, u32[]{:S(2)}) collective-permute-start(bf16[128,128]{1,0:T(8,128)(2,1)S(1)} %collective-permute-done.14.got2), channel_id=1, source_target_pairs={{0,1},{1,0},{2,3},{3,2},{4,5},{5,4},{6,7},{7,6},{8,9},{9,8},{10,11... | collective-permute-start | bytes 98312 | tf_op jit(solution)/shard_map/ppermute | solution.py:533
  70.3 2.6 %collective-permute-start.15 = (bf16[128,128]{1,0:T(8,128)(2,1)S(1)}, bf16[128,128]{1,0:T(8,128)(2,1)S(1)}, u32[]{:S(2)}, u32[]{:S(2)}) collective-permute-start(bf16[128,128]{1,0:T(8,128)(2,1)S(1)} %collective-permute-done.13.got1), channel_id=1, source_target_pairs={{0,1},{1,0},{2,3},{3,2},{4,5},{5,4},{6,7},{7,6},{8,9},{9,8},{10,11... | collective-permute-start | bytes 98312 | tf_op jit(solution)/shard_map/ppermute | solution.py:533
  80.9 2.2 %collective-permute-start.17 = (bf16[32,4,16,128]{3,2,1,0:T(8,128)(2,1)}, bf16[32,4,16,128]{3,2,1,0:T(8,128)(2,1)S(1)}, u32[]{:S(2)}, u32[]{:S(2)}) collective-permute-start(bf16[32,4,16,128]{3,2,1,0:T(8,128)(2,1)} %get-tuple-element.24), channel_id=1, source_target_pairs={{0,1},{1,0},{2,3},{3,2},{4,5},{5,4},{6,7},{7,6},{8,9},{9,8},{10,11... | collective-permute-start | bytes 1572872 | tf_op jit(solution)/shard_map/ppermute | solution.py:533
  85.2 38.1 %all-to-all-start = ((bf16[32,4,16,128]{3,2,1,0:T(8,128)(2,1)}), bf16[32,4,16,128]{3,2,1,0:T(8,128)(2,1)S(1)}, u32[]{:S(2)}, u32[]{:S(2)}) async-start(bf16[32,4,16,128]{3,2,1,0:T(8,128)(2,1)} %add_convert_fusion), calls=%async_computation | async-start | bytes 1048576 | tf_op jit(solution)/shard_map/all_to_all | solution.py:602
  99.7 1.6 collective-permute-start.18
  103.8 7.2 %collective-permute-start.20 = (bf16[128,128]{1,0:T(8,128)(2,1)}, bf16[128,128]{1,0:T(8,128)(2,1)S(1)}, u32[]{:S(2)}, u32[]{:S(2)}) collective-permute-start(bf16[128,128]{1,0:T(8,128)(2,1)} %shard_map.107), channel_id=1, source_target_pairs={{0,4},{2,6},{4,8},{6,10},{8,12},{10,14},{12,16},{14,18},{16,20},{1... | collective-permute-start | bytes 98312 | tf_op jit(solution)/shard_map/ppermute | solution.py:539
  105.1 6.7 %collective-permute-start.19 = (bf16[128,128]{1,0:T(8,128)(2,1)}, bf16[128,128]{1,0:T(8,128)(2,1)S(1)}, u32[]{:S(2)}, u32[]{:S(2)}) collective-permute-start(bf16[128,128]{1,0:T(8,128)(2,1)} %shard_map.107), channel_id=1, source_target_pairs={{0,2},{2,4},{4,6},{6,8},{8,10},{10,12},{12,14},{14,16},{16,18},{18... | collective-permute-start | bytes 98312 | tf_op jit(solution)/shard_map/ppermute | solution.py:539
  111.0 3.5 %copy-start.14 = (bf16[128,128]{1,0:T(8,128)(2,1)}, bf16[128,128]{1,0:T(8,128)(2,1)S(1)}, u32[]{:S(2)}) copy-start(bf16[128,128]{1,0:T(8,128)(2,1)S(1)} %collective-permute-done.20.got2) | copy-start | bytes 98308
  111.0 2.7 %collective-permute-start.22 = (bf16[128,128]{1,0:T(8,128)(2,1)S(1)}, bf16[128,128]{1,0:T(8,128)(2,1)S(1)}, u32[]{:S(2)}, u32[]{:S(2)}) collective-permute-start(bf16[128,128]{1,0:T(8,128)(2,1)S(1)} %collective-permute-done.20.got2), channel_id=1, source_target_pairs={{0,1},{1,0},{2,3},{3,2},{4,5},{5,4},{6,7},{7,6},{8,9},{9,8},{10,11... | collective-permute-start | bytes 98312 | tf_op jit(solution)/shard_map/ppermute | solution.py:533
  111.8 2.6 %collective-permute-start.21 = (bf16[128,128]{1,0:T(8,128)(2,1)S(1)}, bf16[128,128]{1,0:T(8,128)(2,1)S(1)}, u32[]{:S(2)}, u32[]{:S(2)}) collective-permute-start(bf16[128,128]{1,0:T(8,128)(2,1)S(1)} %collective-permute-done.19.got1), channel_id=1, source_target_pairs={{0,1},{1,0},{2,3},{3,2},{4,5},{5,4},{6,7},{7,6},{8,9},{9,8},{10,11... | collective-permute-start | bytes 98312 | tf_op jit(solution)/shard_map/ppermute | solution.py:533
  123.4 25.3 %all-to-all-start.1 = ((bf16[32,4,16,128]{3,2,1,0:T(8,128)(2,1)}), bf16[32,4,16,128]{3,2,1,0:T(8,128)(2,1)S(1)}, u32[]{:S(2)}, u32[]{:S(2)}) async-start(bf16[32,4,16,128]{3,2,1,0:T(8,128)(2,1)} %shard_map.108), calls=%async_computation.1 | async-start | bytes 1048576 | tf_op jit(solution)/shard_map/all_to_all | solution.py:612
  (17 other events, 18.5 us)

commit v4 on v2

--- a/solution.py
+++ b/solution.py
@@ -208,7 +208,7 @@
     return arrays
 
 
-def faces_kernel(sc, home, x_ref, rec_ref):
+def faces_kernel(sc, home, x_ref, w_ref, d_ref, rec_ref, pack_ref, wide):
     s = where_am_i(sc)
 
     def rule(r, l):
@@ -222,6 +222,14 @@
         p = s.a + jnp.minimum(i, s.n - 1)
         slot = home[p] - 3 * s.dev
         rec_ref[i] = mm(x_ref[slot], pick).astype(BF)
+    wide[:, 1664:1792] = jnp.zeros((16, 128), F32)
+    wide[:, 0:1728] = w_ref[...].astype(F32)
+    w = wide[...]
+    pack_ref[0:16, :] = w[:, :640].astype(BF)
+    pack_ref[16:32, :] = pltpu.roll(w, 1792 - 576, 1)[:, :640].astype(BF)
+    pack_ref[32:48, :] = w[:, 1152:].astype(BF)
+    pack_ref[48:80, 0:512] = d_ref[...]
+    pack_ref[48:80, 512:640] = jnp.zeros((32, 128), BF)
 
 
 def message_kernel(level, sub, sc, own, other, out, both):
@@ -261,7 +269,7 @@
 
 def stage_one_kernel(sc, home, links, x_ref, own, other, got1, got2, sw1, sw2, w_a, w_b, w_c, w_d,
                      taps, hid, slope, red, rec2, down_out,
-                     recs, low_rows, high_rows, w_all, w_one):
+                     recs, low_rows, high_rows, w_all, w_one, tap_buf, sems):
     s = where_am_i(sc)
     dp = sc[7]
     gather_records(recs, own, other, (got1, got2), (sw1, sw2))
@@ -288,11 +296,12 @@
         )
 
         def store(t, v):
-            taps[i, t * 64 : t * 64 + 64, :] = v
+            tap_buf[i, t * 64 : t * 64 + 64, :] = v
 
         tap_rows(ONE, block, low, high, store)
-        taps[i, 576:640, :] = jnp.zeros((64, 1152), BF)
-        pre = three_shifts(ONE, mm(w_one[...], taps[i, 0:576, :]))
+        tap_buf[i, 576:640, :] = jnp.zeros((64, 1152), BF)
+        pltpu.make_async_copy(tap_buf.at[i], taps.at[i], sems.at[i]).start()
+        pre = three_shifts(ONE, mm(w_one[...], tap_buf[i, 0:576, :]))
         tall = jnp.concatenate([pre[:, 128 * b : 128 * b + 128] for b in range(8)], axis=0)
         top = tall.astype(BF)
         rest = (tall - top.astype(F32)).astype(BF)
@@ -315,6 +324,8 @@
     pick = one_hot((128, 128), rule)
     for i in range(3):
         rec2[i] = mm(red[:, i * 128 : i * 128 + 128], pick).astype(BF)
+    for i in range(3):
+        pltpu.make_async_copy(tap_buf.at[i], taps.at[i], sems.at[i]).wait()
 
 
 def stage_two_kernel(scale, sc, home, links, red, cot, own, other, got1, got2, sw1, sw2,
@@ -417,7 +428,9 @@
 
 
 def stage_three_kernel(sc, links, grad, own, other, got1, got2, sw1, sw2, down, hid, slope, taps,
-                       out, recs, gred, g_one, spread, dw):
+                       out, recs, gred, g_one, spread, dw, tap_buf, sems):
+    for i in range(3):
+        pltpu.make_async_copy(taps.at[i], tap_buf.at[i], sems.at[i]).start()
     s = where_am_i(sc)
     gather_records(recs, own, other, (got1, got2), (sw1, sw2))
 
@@ -465,7 +478,8 @@
         for dx in (-1, 0, 1):
             w = g if dx == 0 else pltpu.roll(g, (dx * 64) % 1152, 1)
             spread[(dx + 1) * 64 : (dx + 2) * 64, :] = w.astype(BF)
-        dw[...] += mm(spread[...], taps[i], NT)
+        pltpu.make_async_copy(taps.at[i], tap_buf.at[i], sems.at[i]).wait()
+        dw[...] += mm(spread[...], tap_buf[i], NT)
 
     for d in range(4):
         for j in range(5):
@@ -508,15 +522,18 @@
     one_out[:, 1664:1728] = tile(2, 4)[:, :64]
 
 
-def call(kernel, scalars, arrays, outs, scratch):
+def call(kernel, scalars, arrays, outs, scratch, far_in=(), far_out=(), copies=0):
     smem = pl.BlockSpec(memory_space=pltpu.SMEM)
     vmem = pl.BlockSpec(memory_space=pltpu.VMEM)
+    far = pl.BlockSpec(memory_space=pl.ANY)
+    sems = [pltpu.SemaphoreType.DMA((copies,))] if copies else []
     return pl.pallas_call(
         kernel,
         out_shape=[jax.ShapeDtypeStruct(*o) for o in outs],
-        in_specs=[smem] * len(scalars) + [vmem] * len(arrays),
-        out_specs=[vmem] * len(outs),
-        scratch_shapes=[pltpu.VMEM(*t) for t in scratch],
+        in_specs=[smem] * len(scalars)
+        + [far if k in far_in else vmem for k in range(len(arrays))],
+        out_specs=[far if k in far_out else vmem for k in range(len(outs))],
+        scratch_shapes=[pltpu.VMEM(*t) for t in scratch] + sems,
         compiler_params=pltpu.CompilerParams(vmem_limit_bytes=60 << 20),
     )(*scalars, *arrays)
 
@@ -563,10 +580,12 @@
     ).astype(jnp.int32)
     links = patch_links.T
     x = features[0]
-    (rec_one,) = call(faces_kernel, (sc, patch_home), (x,), [((3, 64, 256), BF)], [])
+    rec_one, packed = call(
+        faces_kernel, (sc, patch_home), (x, conv_one, down_weight),
+        [((3, 64, 256), BF), ((80, 640), BF)], [((16, 1792), F32)],
+    )
     rims_one = exchange(ONE, 1, sc, rec_one)
-    rows_one = jnp.pad(conv_one.reshape(16, 3, 576).swapaxes(0, 1).reshape(48, 576), ((0, 0), (0, 64)))
-    w_one = gathered(jnp.concatenate([rows_one, jnp.pad(down_weight, ((0, 0), (0, 128)))]))
+    w_one = gathered(packed)
     w_two = gathered(conv_two)
     taps, hid, slope, red, rec_two, down_full = call(
         stage_one_kernel, (sc, patch_home, links),
@@ -574,7 +593,8 @@
         [((3, 640, 1152), BF), ((512, 384), BF), ((512, 384), F32), ((128, 384), BF),
          ((3, 128, 128), BF), ((128, 512), BF)],
         [((10, 64, 256), BF), ((128, 1152), BF), ((128, 1152), BF), ((4, 80, 640), BF),
-         ((192, 576), BF)],
+         ((192, 576), BF), ((3, 640, 1152), BF)],
+        far_out=(0,), copies=3,
     )
     rims_two = exchange(TWO, 1, sc, rec_two)
     cells = lax.axis_size("dp") * patch_links.shape[0] * 128
@@ -594,7 +614,8 @@
         (grad, rec_back, *rims_back, down_full, hid, slope, taps),
         [((32, 4, 16, 128), BF)],
         [((10, 128, 128), BF), ((128, 384), BF), ((512, 384), BF), ((192, 1152), BF),
-         ((192, 640), F32)],
+         ((192, 640), F32), ((3, 640, 1152), BF)],
+        far_in=(10,), copies=3,
     )
     two = two.astype(F32).reshape(16, 2, 4, 16, 128).sum(axis=0).astype(BF)
     two, small = lax.optimization_barrier((two, small))

time: 161 us -> 159 us (0.988)
    unnamed x44 -> x42, local copies, waits for them, and re-layouts: 3.71 us -> 3.71 us
  transfers between devices with their start and end apart: 24 -> 24, of which waited for: 11 -> 11; matrix products, arithmetic and copies ran while one was open for 1% -> 0% of each run, Pallas kernels for 14% -> 14%
where the time goes in v4:
time: 159 us; the launch traced here: 158 us
  starting transfers between devices  56.5 us (36%)
  Pallas kernels  33.4 us (21%)
  waiting for transfers between devices  32.7 us (21%)
  blocking collectives  27 us (17%)
  local copies, waits for them, and re-layouts  3.77 us (2%)
  other arithmetic  3.62 us (2%)
    pallas_call x8, Pallas kernels, call(): pl.pallas_call(kernel, out_shape=[jax.ShapeDtypeStruct(*o) for o in outs]...  33.4 us
    ppermute x10, starting transfers between devices, swap_cores(): return lax.ppermute(v, 'core', [(0, 1), (1, 0)])  15.6 us
    all_to_all x1, blocking collectives, on_device(): pieces = lax.all_to_all(copies, ('x', 'y', 'core'), 0, 0, tiled=True)  14.9 us
    all_to_all x1, starting transfers between devices, on_device(): small = lax.all_to_all(small, ('x', 'y', 'core'), 0, 0, tiled=True)  13.3 us
    ppermute x6, waiting for transfers between devices, chips_on(): return lax.ppermute(v, SPACE, up + down)  12.7 us
    all_to_all x1, starting transfers between devices, on_device(): two = lax.all_to_all(two, ('x', 'y', 'core'), 0, 0, tiled=True)  12.4 us
    all_to_all x1, blocking collectives, on_device(): lax.all_to_all(jnp.concatenate([mine, mine]), ('zh', 'dp'), 0, 0, tiled=T...  12.1 us
    all_to_all x1, waiting for transfers between devices, on_device(): small = lax.all_to_all(small, ('x', 'y', 'core'), 0, 0, tiled=True)  11.6 us
  transfers between devices with their start and end apart: 24, of which 11 were waited for; matrix products, arithmetic and copies ran while one was open for 0% of the time, Pallas kernels for 14%

profile of v4, /device:TPU:1, one launch (start us, length us, event | category | flops | bytes accessed | tf_op | source)
XLA Modules:
  0.0 157.9 jit_solution(5410233657464312004)
XLA Ops:
  2.1 2.3 %shard_map.102 = (bf16[3,64,256]{2,1,0:T(8,128)(2,1)}, bf16[80,640]{1,0:T(8,128)(2,1)}) custom-call(s32[8]{0:T(128)} %compare_select_fusion.4.sc, s32[128]{0:T(128)} %home.5, bf16[3,64,1024]{2,1,0:T(8,128)(2,1)} %bitcast.10, bf16[16,1728]{1,0:T(8,128)(2,1)} %w_ref.1, bf16[32,512]{1,0:T(8,128)(2,1)} %d_ref.1), custom_call_target="tpu_custom_call" | custom-call | tf_op jit(solution)/shard_map/pallas_call | solution.py:530
  4.3 3.2 %collective-permute-start = (bf16[3,64,256]{2,1,0:T(8,128)(2,1)}, bf16[3,64,256]{2,1,0:T(8,128)(2,1)S(1)}, u32[]{:S(2)}, u32[]{:S(2)}) collective-permute-start(bf16[3,64,256]{2,1,0:T(8,128)(2,1)} %get-tuple-element.22.own), channel_id=1, source_target_pairs={{0,1},{1,0},{2,3},{3,2},{4,5},{5,4},{6,7},{7,6},{8,9},{9,8},{10,11... | collective-permute-start | bytes 294920 | tf_op jit(solution)/shard_map/ppermute | solution.py:542
  7.5 2.6 %collective-permute-start.7 = (bf16[80,640]{1,0:T(8,128)(2,1)}, bf16[80,640]{1,0:T(8,128)(2,1)S(1)}, u32[]{:S(2)}, u32[]{:S(2)}) collective-permute-start(bf16[80,640]{1,0:T(8,128)(2,1)} %get-tuple-element.23.w_a), channel_id=1, source_target_pairs={{0,192},{64,128},{128,64},{192,0},{1,193},{65,129},{129,65},{193,1... | collective-permute-start | bytes 307208 | tf_op jit(solution)/shard_map/ppermute | solution.py:552
  11.7 1.8 %shard_map.103 = bf16[64,256]{1,0:T(8,128)(2,1)} custom-call(s32[8]{0:T(128)} %compare_select_fusion.4.sc, bf16[3,64,256]{2,1,0:T(8,128)(2,1)} %get-tuple-element.22.own, bf16[3,64,256]{2,1,0:T(8,128)(2,1)} %copy-done), custom_call_target="tpu_custom_call" | custom-call | tf_op jit(solution)/shard_map/pallas_call | solution.py:530
  13.5 1.3 collective-permute-start.2
  14.8 1.3 collective-permute-start.1
  16.1 1.5 collective-permute-start.14
  17.7 1.3 collective-permute-done.6.w_c
  19.1 2.2 %collective-permute-start.15 = (bf16[32,3456]{1,0:T(8,128)(2,1)}, bf16[32,3456]{1,0:T(8,128)(2,1)S(1)}, u32[]{:S(2)}, u32[]{:S(2)}) collective-permute-start(bf16[32,3456]{1,0:T(8,128)(2,1)} %w_a.1), channel_id=1, source_target_pairs={{0,192},{64,128},{128,64},{192,0},{1,193},{65,129},{129,65},{193,1... | collective-permute-start | bytes 663560 | tf_op jit(solution)/shard_map/ppermute | solution.py:552
  21.3 4.4 %collective-permute-start.4 = (bf16[64,256]{1,0:T(8,128)(2,1)S(1)}, bf16[64,256]{1,0:T(8,128)(2,1)S(1)}, u32[]{:S(2)}, u32[]{:S(2)}) collective-permute-start(bf16[64,256]{1,0:T(8,128)(2,1)S(1)} %collective-permute-done.2.got2), channel_id=1, source_target_pairs={{0,1},{1,0},{2,3},{3,2},{4,5},{5,4},{6,7},{7,6},{8,9},{9,8},{10,11... | collective-permute-start | bytes 98312 | tf_op jit(solution)/shard_map/ppermute | solution.py:542
  27.6 8.8 %shard_map.104 = (bf16[3,640,1152]{2,1,0:T(8,128)(2,1)}, bf16[512,384]{1,0:T(8,128)(2,1)}, f32[512,384]{1,0:T(8,128)}, bf16[128,384]{1,0:T(8,128)(2,1)}, bf16[3,...) custom-call(s32[8]{0:T(128)} %compare_select_fusion.4.sc, s32[128]{0:T(128)} %home.5, s32[4,128]{1,0:T(4,128)} %bitcast.13, ...), custom_call_target="tpu_custom_call" | custom-call | tf_op jit(solution)/shard_map/pallas_call | solution.py:530
  36.7 1.4 collective-permute-done.8.other
  38.7 1.8 %shard_map.105 = bf16[128,128]{1,0:T(8,128)(2,1)} custom-call(s32[8]{0:T(128)} %compare_select_fusion.4.sc, bf16[3,128,128]{2,1,0:T(8,128)(2,1)} %get-tuple-element.25.own, bf16[3,128,128]{2,1,0:T(8,128)(2,1)} %copy-done.1), custom_call_target="tpu_custom_call" | custom-call | tf_op jit(solution)/shard_map/pallas_call | solution.py:530
  40.4 1.3 collective-permute-start.10
  41.7 1.3 collective-permute-start.9
  43.0 8.1 %collective-permute-done.10.got2 = bf16[128,128]{1,0:T(8,128)(2,1)S(1)} collective-permute-done((bf16[128,128]{1,0:T(8,128)(2,1)}, bf16[128,128]{1,0:T(8,128)(2,1)S(1)}, u32[]{:S(2)}, u32[]{:S(2)}) %collective-permute-start.10) | collective-permute-done | bytes 32800 | tf_op jit(solution)/shard_map/ppermute | solution.py:548
  51.1 2.5 %collective-permute-start.12 = (bf16[128,128]{1,0:T(8,128)(2,1)S(1)}, bf16[128,128]{1,0:T(8,128)(2,1)S(1)}, u32[]{:S(2)}, u32[]{:S(2)}) collective-permute-start(bf16[128,128]{1,0:T(8,128)(2,1)S(1)} %collective-permute-done.10.got2), channel_id=1, source_target_pairs={{0,1},{1,0},{2,3},{3,2},{4,5},{5,4},{6,7},{7,6},{8,9},{9,8},{10,11... | collective-permute-start | bytes 98312 | tf_op jit(solution)/shard_map/ppermute | solution.py:542
  53.7 1.8 %collective-permute-start.11 = (bf16[128,128]{1,0:T(8,128)(2,1)S(1)}, bf16[128,128]{1,0:T(8,128)(2,1)S(1)}, u32[]{:S(2)}, u32[]{:S(2)}) collective-permute-start(bf16[128,128]{1,0:T(8,128)(2,1)S(1)} %collective-permute-done.9.got1), channel_id=1, source_target_pairs={{0,1},{1,0},{2,3},{3,2},{4,5},{5,4},{6,7},{7,6},{8,9},{9,8},{10,11... | collective-permute-start | bytes 98312 | tf_op jit(solution)/shard_map/ppermute | solution.py:542
  56.9 7.5 %shard_map.106 = (bf16[3,128,128]{2,1,0:T(8,128)(2,1)}, bf16[32,4,16,128]{3,2,1,0:T(8,128)(2,1)}, bf16[32,4,16,128]{3,2,1,0:T(8,128)(2,1)}, f32[128,384]{1,0:T(8,128)}, bf16[3,128,128]{2,1,0:T(8,128)(2,1)}) custom-call(s32[8]{0:T(128)} %compare_select_fusion.4.sc, s32[128]{0:T(128)} %home.5, s32[4,128]{1,0:T(4,128)} %bitcast.14, ...), custom_call_target="tpu_custom_call" | custom-call | tf_op jit(solution)/shard_map/pallas_call | solution.py:530
  64.8 1.8 %collective-permute-done.16 = bf16[32,4,16,128]{3,2,1,0:T(8,128)(2,1)S(1)} collective-permute-done((bf16[32,4,16,128]{3,2,1,0:T(8,128)(2,1)}, bf16[32,4,16,128]{3,2,1,0:T(8,128)(2,1)S(1)}, u32[]{:S(2)}, u32[]{:S(2)}) %collective-permute-start.16) | collective-permute-done | bytes 524320 | tf_op jit(solution)/shard_map/ppermute | solution.py:542
  66.6 2.0 %add_convert_fusion = bf16[32,4,16,128]{3,2,1,0:T(8,128)(2,1)} fusion(bf16[32,4,16,128]{3,2,1,0:T(8,128)(2,1)S(1)} %collective-permute-done.16, bf16[32,4,16,128]{3,2,1,0:T(8,128)(2,1)} %get-tuple-element.27), kind=kLoop, calls=%fused_computation | loop fusion | flops 1048576 | bytes 1572864 | tf_op jit(solution)/shard_map/convert_element_type | solution.py:610
  68.6 12.4 %all-to-all-start = ((bf16[32,4,16,128]{3,2,1,0:T(8,128)(2,1)}), bf16[32,4,16,128]{3,2,1,0:T(8,128)(2,1)S(1)}, u32[]{:S(2)}, u32[]{:S(2)}) async-start(bf16[32,4,16,128]{3,2,1,0:T(8,128)(2,1)} %add_convert_fusion), calls=%async_computation | async-start | bytes 1048576 | tf_op jit(solution)/shard_map/all_to_all | solution.py:611
  83.2 1.9 %shard_map.107 = bf16[128,128]{1,0:T(8,128)(2,1)} custom-call(s32[8]{0:T(128)} %compare_select_fusion.4.sc, bf16[3,128,128]{2,1,0:T(8,128)(2,1)} %get-tuple-element.30.own, bf16[3,128,128]{2,1,0:T(8,128)(2,1)} %copy-done.2), custom_call_target="tpu_custom_call" | custom-call | tf_op jit(solution)/shard_map/pallas_call | solution.py:530
  86.3 1.3 collective-permute-start.18
  87.6 4.6 %collective-permute-done.19.got2 = bf16[128,128]{1,0:T(8,128)(2,1)S(1)} collective-permute-done((bf16[128,128]{1,0:T(8,128)(2,1)}, bf16[128,128]{1,0:T(8,128)(2,1)S(1)}, u32[]{:S(2)}, u32[]{:S(2)}) %collective-permute-start.19) | collective-permute-done | bytes 32800 | tf_op jit(solution)/shard_map/ppermute | solution.py:548
  93.1 1.8 %collective-permute-start.20 = (bf16[128,128]{1,0:T(8,128)(2,1)S(1)}, bf16[128,128]{1,0:T(8,128)(2,1)S(1)}, u32[]{:S(2)}, u32[]{:S(2)}) collective-permute-start(bf16[128,128]{1,0:T(8,128)(2,1)S(1)} %collective-permute-done.18.got1), channel_id=1, source_target_pairs={{0,1},{1,0},{2,3},{3,2},{4,5},{5,4},{6,7},{7,6},{8,9},{9,8},{10,11... | collective-permute-start | bytes 98312 | tf_op jit(solution)/shard_map/ppermute | solution.py:542
  96.3 7.5 %shard_map.108 = bf16[32,4,16,128]{3,2,1,0:T(8,128)(2,1)} custom-call(s32[8]{0:T(128)} %compare_select_fusion.4.sc, s32[4,128]{1,0:T(4,128)} %bitcast.15, f32[128,384]{1,0:T(8,128)} %get-tuple-element.29.grad, bf16[3,128,128]{2,1,0:T(8,128)(2,1)} %get-tuple-element.30.own, bf16[3,128,128]{2,1,0:T(8,128)(2,1)} %copy-done.2, bf16[128,128]{1,0:T(8,128)(2,1)} %copy-done.10, ...), custom_call_target="tpu_custom_call" | custom-call | tf_op jit(solution)/shard_map/pallas_call | solution.py:530
  103.9 13.3 %all-to-all-start.1 = ((bf16[32,4,16,128]{3,2,1,0:T(8,128)(2,1)}), bf16[32,4,16,128]{3,2,1,0:T(8,128)(2,1)S(1)}, u32[]{:S(2)}, u32[]{:S(2)}) async-start(bf16[32,4,16,128]{3,2,1,0:T(8,128)(2,1)} %shard_map.108), calls=%async_computation.1 | async-start | bytes 1048576 | tf_op jit(solution)/shard_map/all_to_all | solution.py:622
  117.3 11.6 %all-to-all-done.1 = bf16[32,4,16,128]{3,2,1,0:T(8,128)(2,1)S(1)} async-done(((bf16[32,4,16,128]{3,2,1,0:T(8,128)(2,1)}), bf16[32,4,16,128]{3,2,1,0:T(8,128)(2,1)S(1)}, u32[]{:S(2)}, u32[]{:S(2)}) %all-to-all-start.1) | async-done | bytes 524320 | tf_op jit(solution)/shard_map/all_to_all | solution.py:622
  129.0 12.1 %all_to_all.20 = bf16[8,48,128]{2,1,0:T(8,128)(2,1)S(1)} all-to-all(bf16[8,48,128]{2,1,0:T(8,128)(2,1)S(1)} %maximum_maximum_fusion), channel_id=1, replica_groups=mesh['dp'=4,'x'=4,'zh'=2,'y'=4,'core'=2] {'zh','dp'}, dimensions={0} | all-to-all | bytes 196608 | tf_op jit(solution)/shard_map/all_to_all | solution.py:625
  141.2 14.9 %all_to_all.21.pieces = bf16[32,48,128]{2,1,0:T(8,128)(2,1)} all-to-all(bf16[32,48,128]{2,1,0:T(8,128)(2,1)S(1)} %broadcast_in_dim.33), channel_id=1, replica_groups=mesh['dp'=4,'x'=4,'zh'=2,'y'=4,'core'=2] {'x','y','core'}, dimensions={0} | all-to-all | bytes 786432 | tf_op jit(solution)/shard_map/all_to_all | solution.py:628
  156.1 1.8 %shard_map.109 = (f32[16,1728]{1,0:T(8,128)}, f32[32,512]{1,0:T(8,128)}, f32[32,3456]{1,0:T(8,128)}) custom-call(bf16[32,48,128]{2,1,0:T(8,128)(2,1)} %all_to_all.21.pieces), custom_call_target="tpu_custom_call" | custom-call | tf_op jit(solution)/shard_map/pallas_call | solution.py:530
  (78 shorter events, 13.7 us)
Async XLA Ops:
  4.3 6.8 %collective-permute-start = (bf16[3,64,256]{2,1,0:T(8,128)(2,1)}, bf16[3,64,256]{2,1,0:T(8,128)(2,1)S(1)}, u32[]{:S(2)}, u32[]{:S(2)}) collective-permute-start(bf16[3,64,256]{2,1,0:T(8,128)(2,1)} %get-tuple-element.22.own), channel_id=1, source_target_pairs={{0,1},{1,0},{2,3},{3,2},{4,5},{5,4},{6,7},{7,6},{8,9},{9,8},{10,11... | collective-permute-start | bytes 294920 | tf_op jit(solution)/shard_map/ppermute | solution.py:542
  7.5 8.5 %collective-permute-start.7 = (bf16[80,640]{1,0:T(8,128)(2,1)}, bf16[80,640]{1,0:T(8,128)(2,1)S(1)}, u32[]{:S(2)}, u32[]{:S(2)}) collective-permute-start(bf16[80,640]{1,0:T(8,128)(2,1)} %get-tuple-element.23.w_a), channel_id=1, source_target_pairs={{0,192},{64,128},{128,64},{192,0},{1,193},{65,129},{129,65},{193,1... | collective-permute-start | bytes 307208 | tf_op jit(solution)/shard_map/ppermute | solution.py:552
  10.2 8.8 %collective-permute-start.6 = (bf16[80,640]{1,0:T(8,128)(2,1)}, bf16[80,640]{1,0:T(8,128)(2,1)S(1)}, u32[]{:S(2)}, u32[]{:S(2)}) collective-permute-start(bf16[80,640]{1,0:T(8,128)(2,1)} %get-tuple-element.23.w_a), channel_id=1, source_target_pairs={{0,128},{64,192},{128,0},{192,64},{1,129},{65,193},{129,1},{193,65... | collective-permute-start | bytes 307208 | tf_op jit(solution)/shard_map/ppermute | solution.py:552
  10.2 8.9 %collective-permute-start.5 = (bf16[80,640]{1,0:T(8,128)(2,1)}, bf16[80,640]{1,0:T(8,128)(2,1)S(1)}, u32[]{:S(2)}, u32[]{:S(2)}) collective-permute-start(bf16[80,640]{1,0:T(8,128)(2,1)} %get-tuple-element.23.w_a), channel_id=1, source_target_pairs={{0,64},{64,0},{128,192},{192,128},{1,65},{65,1},{129,193},{193,129... | collective-permute-start | bytes 307208 | tf_op jit(solution)/shard_map/ppermute | solution.py:552
  13.5 7.8 %collective-permute-start.2 = (bf16[64,256]{1,0:T(8,128)(2,1)}, bf16[64,256]{1,0:T(8,128)(2,1)S(1)}, u32[]{:S(2)}, u32[]{:S(2)}) collective-permute-start(bf16[64,256]{1,0:T(8,128)(2,1)} %shard_map.103), channel_id=1, source_target_pairs={{0,4},{2,6},{4,8},{6,10},{8,12},{10,14},{12,16},{14,18},{16,20},{1... | collective-permute-start | bytes 98312 | tf_op jit(solution)/shard_map/ppermute | solution.py:548
  14.8 11.0 %collective-permute-start.1 = (bf16[64,256]{1,0:T(8,128)(2,1)}, bf16[64,256]{1,0:T(8,128)(2,1)S(1)}, u32[]{:S(2)}, u32[]{:S(2)}) collective-permute-start(bf16[64,256]{1,0:T(8,128)(2,1)} %shard_map.103), channel_id=1, source_target_pairs={{0,2},{2,4},{4,6},{6,8},{8,10},{10,12},{12,14},{14,16},{16,18},{18... | collective-permute-start | bytes 98312 | tf_op jit(solution)/shard_map/ppermute | solution.py:548
  16.1 10.9 %copy-start.6 = (bf16[80,640]{1,0:T(8,128)(2,1)}, bf16[80,640]{1,0:T(8,128)(2,1)S(1)}, u32[]{:S(2)}) copy-start(bf16[80,640]{1,0:T(8,128)(2,1)S(1)} %collective-permute-done.7.w_d) | copy-start | bytes 307204
  16.1 39.3 %collective-permute-start.14 = (bf16[32,3456]{1,0:T(8,128)(2,1)}, bf16[32,3456]{1,0:T(8,128)(2,1)S(1)}, u32[]{:S(2)}, u32[]{:S(2)}) collective-permute-start(bf16[32,3456]{1,0:T(8,128)(2,1)} %w_a.1), channel_id=1, source_target_pairs={{0,128},{64,192},{128,0},{192,64},{1,129},{65,193},{129,1},{193,65... | collective-permute-start | bytes 663560 | tf_op jit(solution)/shard_map/ppermute | solution.py:552
  18.9 8.0 %copy-start.7 = (bf16[80,640]{1,0:T(8,128)(2,1)}, bf16[80,640]{1,0:T(8,128)(2,1)S(1)}, u32[]{:S(2)}) copy-start(bf16[80,640]{1,0:T(8,128)(2,1)S(1)} %collective-permute-done.6.w_c) | copy-start | bytes 307204
  18.9 36.5 %collective-permute-start.13 = (bf16[32,3456]{1,0:T(8,128)(2,1)}, bf16[32,3456]{1,0:T(8,128)(2,1)S(1)}, u32[]{:S(2)}, u32[]{:S(2)}) collective-permute-start(bf16[32,3456]{1,0:T(8,128)(2,1)} %w_a.1), channel_id=1, source_target_pairs={{0,64},{64,0},{128,192},{192,128},{1,65},{65,1},{129,193},{193,129... | collective-permute-start | bytes 663560 | tf_op jit(solution)/shard_map/ppermute | solution.py:552
  19.1 7.8 %copy-start.8 = (bf16[80,640]{1,0:T(8,128)(2,1)}, bf16[80,640]{1,0:T(8,128)(2,1)S(1)}, u32[]{:S(2)}) copy-start(bf16[80,640]{1,0:T(8,128)(2,1)S(1)} %collective-permute-done.5.w_b) | copy-start | bytes 307204
  19.1 36.3 %collective-permute-start.15 = (bf16[32,3456]{1,0:T(8,128)(2,1)}, bf16[32,3456]{1,0:T(8,128)(2,1)S(1)}, u32[]{:S(2)}, u32[]{:S(2)}) collective-permute-start(bf16[32,3456]{1,0:T(8,128)(2,1)} %w_a.1), channel_id=1, source_target_pairs={{0,192},{64,128},{128,64},{192,0},{1,193},{65,129},{129,65},{193,1... | collective-permute-start | bytes 663560 | tf_op jit(solution)/shard_map/ppermute | solution.py:552
  21.3 5.6 %copy-start.13 = (bf16[64,256]{1,0:T(8,128)(2,1)}, bf16[64,256]{1,0:T(8,128)(2,1)S(1)}, u32[]{:S(2)}) copy-start(bf16[64,256]{1,0:T(8,128)(2,1)S(1)} %collective-permute-done.2.got2) | copy-start | bytes 98308
  21.3 5.3 %collective-permute-start.4 = (bf16[64,256]{1,0:T(8,128)(2,1)S(1)}, bf16[64,256]{1,0:T(8,128)(2,1)S(1)}, u32[]{:S(2)}, u32[]{:S(2)}) collective-permute-start(bf16[64,256]{1,0:T(8,128)(2,1)S(1)} %collective-permute-done.2.got2), channel_id=1, source_target_pairs={{0,1},{1,0},{2,3},{3,2},{4,5},{5,4},{6,7},{7,6},{8,9},{9,8},{10,11... | collective-permute-start | bytes 98312 | tf_op jit(solution)/shard_map/ppermute | solution.py:542
  25.8 1.2 collective-permute-start.3
  36.4 1.6 %collective-permute-start.8 = (bf16[3,128,128]{2,1,0:T(8,128)(2,1)}, bf16[3,128,128]{2,1,0:T(8,128)(2,1)S(1)}, u32[]{:S(2)}, u32[]{:S(2)}) collective-permute-start(bf16[3,128,128]{2,1,0:T(8,128)(2,1)} %get-tuple-element.25.own), channel_id=1, source_target_pairs={{0,1},{1,0},{2,3},{3,2},{4,5},{5,4},{6,7},{7,6},{8,9},{9,8},{10,11... | collective-permute-start | bytes 294920 | tf_op jit(solution)/shard_map/ppermute | solution.py:542
  40.4 10.7 %collective-permute-start.10 = (bf16[128,128]{1,0:T(8,128)(2,1)}, bf16[128,128]{1,0:T(8,128)(2,1)S(1)}, u32[]{:S(2)}, u32[]{:S(2)}) collective-permute-start(bf16[128,128]{1,0:T(8,128)(2,1)} %shard_map.105), channel_id=1, source_target_pairs={{0,4},{2,6},{4,8},{6,10},{8,12},{10,14},{12,16},{14,18},{16,20},{1... | collective-permute-start | bytes 98312 | tf_op jit(solution)/shard_map/ppermute | solution.py:548
  41.7 11.9 %collective-permute-start.9 = (bf16[128,128]{1,0:T(8,128)(2,1)}, bf16[128,128]{1,0:T(8,128)(2,1)S(1)}, u32[]{:S(2)}, u32[]{:S(2)}) collective-permute-start(bf16[128,128]{1,0:T(8,128)(2,1)} %shard_map.105), channel_id=1, source_target_pairs={{0,2},{2,4},{4,6},{6,8},{8,10},{10,12},{12,14},{14,16},{16,18},{18... | collective-permute-start | bytes 98312 | tf_op jit(solution)/shard_map/ppermute | solution.py:548
  51.1 5.2 %copy-start.15 = (bf16[128,128]{1,0:T(8,128)(2,1)}, bf16[128,128]{1,0:T(8,128)(2,1)S(1)}, u32[]{:S(2)}) copy-start(bf16[128,128]{1,0:T(8,128)(2,1)S(1)} %collective-permute-done.10.got2) | copy-start | bytes 98308
  51.1 4.4 %collective-permute-start.12 = (bf16[128,128]{1,0:T(8,128)(2,1)S(1)}, bf16[128,128]{1,0:T(8,128)(2,1)S(1)}, u32[]{:S(2)}, u32[]{:S(2)}) collective-permute-start(bf16[128,128]{1,0:T(8,128)(2,1)S(1)} %collective-permute-done.10.got2), channel_id=1, source_target_pairs={{0,1},{1,0},{2,3},{3,2},{4,5},{5,4},{6,7},{7,6},{8,9},{9,8},{10,11... | collective-permute-start | bytes 98312 | tf_op jit(solution)/shard_map/ppermute | solution.py:542
  53.7 2.7 %copy-start.16 = (bf16[128,128]{1,0:T(8,128)(2,1)}, bf16[128,128]{1,0:T(8,128)(2,1)S(1)}, u32[]{:S(2)}) copy-start(bf16[128,128]{1,0:T(8,128)(2,1)S(1)} %collective-permute-done.9.got1) | copy-start | bytes 98308
  53.7 2.6 %collective-permute-start.11 = (bf16[128,128]{1,0:T(8,128)(2,1)S(1)}, bf16[128,128]{1,0:T(8,128)(2,1)S(1)}, u32[]{:S(2)}, u32[]{:S(2)}) collective-permute-start(bf16[128,128]{1,0:T(8,128)(2,1)S(1)} %collective-permute-done.9.got1), channel_id=1, source_target_pairs={{0,1},{1,0},{2,3},{3,2},{4,5},{5,4},{6,7},{7,6},{8,9},{9,8},{10,11... | collective-permute-start | bytes 98312 | tf_op jit(solution)/shard_map/ppermute | solution.py:542
  64.4 2.1 %collective-permute-start.16 = (bf16[32,4,16,128]{3,2,1,0:T(8,128)(2,1)}, bf16[32,4,16,128]{3,2,1,0:T(8,128)(2,1)S(1)}, u32[]{:S(2)}, u32[]{:S(2)}) collective-permute-start(bf16[32,4,16,128]{3,2,1,0:T(8,128)(2,1)} %get-tuple-element.28), channel_id=1, source_target_pairs={{0,1},{1,0},{2,3},{3,2},{4,5},{5,4},{6,7},{7,6},{8,9},{9,8},{10,11... | collective-permute-start | bytes 1572872 | tf_op jit(solution)/shard_map/ppermute | solution.py:542
  68.6 35.3 %all-to-all-start = ((bf16[32,4,16,128]{3,2,1,0:T(8,128)(2,1)}), bf16[32,4,16,128]{3,2,1,0:T(8,128)(2,1)S(1)}, u32[]{:S(2)}, u32[]{:S(2)}) async-start(bf16[32,4,16,128]{3,2,1,0:T(8,128)(2,1)} %add_convert_fusion), calls=%async_computation | async-start | bytes 1048576 | tf_op jit(solution)/shard_map/all_to_all | solution.py:611
  80.9 1.6 %collective-permute-start.17 = (bf16[3,128,128]{2,1,0:T(8,128)(2,1)}, bf16[3,128,128]{2,1,0:T(8,128)(2,1)S(1)}, u32[]{:S(2)}, u32[]{:S(2)}) collective-permute-start(bf16[3,128,128]{2,1,0:T(8,128)(2,1)} %get-tuple-element.30.own), channel_id=1, source_target_pairs={{0,1},{1,0},{2,3},{3,2},{4,5},{5,4},{6,7},{7,6},{8,9},{9,8},{10,11... | collective-permute-start | bytes 294920 | tf_op jit(solution)/shard_map/ppermute | solution.py:542
  85.1 7.2 %collective-permute-start.19 = (bf16[128,128]{1,0:T(8,128)(2,1)}, bf16[128,128]{1,0:T(8,128)(2,1)S(1)}, u32[]{:S(2)}, u32[]{:S(2)}) collective-permute-start(bf16[128,128]{1,0:T(8,128)(2,1)} %shard_map.107), channel_id=1, source_target_pairs={{0,4},{2,6},{4,8},{6,10},{8,12},{10,14},{12,16},{14,18},{16,20},{1... | collective-permute-start | bytes 98312 | tf_op jit(solution)/shard_map/ppermute | solution.py:548
  86.3 6.7 %collective-permute-start.18 = (bf16[128,128]{1,0:T(8,128)(2,1)}, bf16[128,128]{1,0:T(8,128)(2,1)S(1)}, u32[]{:S(2)}, u32[]{:S(2)}) collective-permute-start(bf16[128,128]{1,0:T(8,128)(2,1)} %shard_map.107), channel_id=1, source_target_pairs={{0,2},{2,4},{4,6},{6,8},{8,10},{10,12},{12,14},{14,16},{16,18},{18... | collective-permute-start | bytes 98312 | tf_op jit(solution)/shard_map/ppermute | solution.py:548
  92.2 3.5 %copy-start.9 = (bf16[128,128]{1,0:T(8,128)(2,1)}, bf16[128,128]{1,0:T(8,128)(2,1)S(1)}, u32[]{:S(2)}) copy-start(bf16[128,128]{1,0:T(8,128)(2,1)S(1)} %collective-permute-done.19.got2) | copy-start | bytes 98308
  92.2 2.7 %collective-permute-start.21 = (bf16[128,128]{1,0:T(8,128)(2,1)S(1)}, bf16[128,128]{1,0:T(8,128)(2,1)S(1)}, u32[]{:S(2)}, u32[]{:S(2)}) collective-permute-start(bf16[128,128]{1,0:T(8,128)(2,1)S(1)} %collective-permute-done.19.got2), channel_id=1, source_target_pairs={{0,1},{1,0},{2,3},{3,2},{4,5},{5,4},{6,7},{7,6},{8,9},{9,8},{10,11... | collective-permute-start | bytes 98312 | tf_op jit(solution)/shard_map/ppermute | solution.py:542
  93.1 2.7 %copy-start.10 = (bf16[128,128]{1,0:T(8,128)(2,1)}, bf16[128,128]{1,0:T(8,128)(2,1)S(1)}, u32[]{:S(2)}) copy-start(bf16[128,128]{1,0:T(8,128)(2,1)S(1)} %collective-permute-done.18.got1) | copy-start | bytes 98308
  93.1 2.6 %collective-permute-start.20 = (bf16[128,128]{1,0:T(8,128)(2,1)S(1)}, bf16[128,128]{1,0:T(8,128)(2,1)S(1)}, u32[]{:S(2)}, u32[]{:S(2)}) collective-permute-start(bf16[128,128]{1,0:T(8,128)(2,1)S(1)} %collective-permute-done.18.got1), channel_id=1, source_target_pairs={{0,1},{1,0},{2,3},{3,2},{4,5},{5,4},{6,7},{7,6},{8,9},{9,8},{10,11... | collective-permute-start | bytes 98312 | tf_op jit(solution)/shard_map/ppermute | solution.py:542
  103.9 24.9 %all-to-all-start.1 = ((bf16[32,4,16,128]{3,2,1,0:T(8,128)(2,1)}), bf16[32,4,16,128]{3,2,1,0:T(8,128)(2,1)S(1)}, u32[]{:S(2)}, u32[]{:S(2)}) async-start(bf16[32,4,16,128]{3,2,1,0:T(8,128)(2,1)} %shard_map.108), calls=%async_computation.1 | async-start | bytes 1048576 | tf_op jit(solution)/shard_map/all_to_all | solution.py:622
  (13 other events, 9.9 us)

commit v5 on v4

--- a/solution.py
+++ b/solution.py
@@ -27,6 +27,14 @@
 TN = ((0,), (0,))
 
 
+def div(v, n):
+    return lax.shift_right_arithmetic(v, jnp.int32(n.bit_length() - 1))
+
+
+def mod(v, n):
+    return lax.bitwise_and(v, jnp.int32(n - 1))
+
+
 def one_hot(shape, rule):
     r = lax.broadcasted_iota(jnp.int32, shape, 0)
     l = lax.broadcasted_iota(jnp.int32, shape, 1)
@@ -44,7 +52,7 @@
     g, zs = level.g, level.zs
     return one_hot(
         (level.R, 128),
-        lambda r, l: (r - off == l - g) & (l >= g) & (l < 2 * g) & ((l - g) // zs == xc),
+        lambda r, l: (r - off == l - g) & (l >= g) & (l < 2 * g) & (div(l - g, zs) == xc),
     )
 
 
@@ -52,7 +60,7 @@
     g, zs, N, W = level.g, level.zs, level.N, level.W
 
     def rule(r, l):
-        face = (r < g) & (l == (r // zs) * g + r % zs + y_off)
+        face = (r < g) & (l == div(r, zs) * g + mod(r, zs) + y_off)
         q = r - g
         low = (q >= 0) & (q < zs) & (l == N + q + y_off)
         high = (q >= g - zs) & (q < g) & (l == W - g + q - (g - zs) + y_off)
@@ -156,7 +164,7 @@
 
 def coords(level):
     lane = lax.broadcasted_iota(jnp.int32, (level.C, level.W), 1)
-    return (lane % level.g) // level.zs, lane % level.zs
+    return div(mod(lane, level.g), level.zs), mod(lane, level.zs)
 
 
 def tap_rows(level, block, low, high, store):
@@ -187,15 +195,15 @@
 
 def parity_order():
     def rule(r, l):
-        y, z = (r % 64) // 4, r % 4
-        e = 4 * (r // 64) + 2 * (y % 2) + z % 2
-        return l == e * 16 + (y // 2) * 2 + z // 2
+        y, z = div(mod(r, 64), 4), mod(r, 4)
+        e = 4 * div(r, 64) + 2 * mod(y, 2) + mod(z, 2)
+        return l == e * 16 + div(y, 2) * 2 + div(z, 2)
 
     return one_hot((128, 128), rule)
 
 
 def swap_groups(arrays):
-    group = lax.broadcasted_iota(jnp.int32, (64, 128), 1) // 16
+    group = div(lax.broadcasted_iota(jnp.int32, (64, 128), 1), 16)
     arrays = list(arrays)
     for b in (1, 2, 4):
         bit = (group & b) != 0
@@ -212,10 +220,10 @@
     s = where_am_i(sc)
 
     def rule(r, l):
-        group, m = l // 64, l % 64
-        high = (group == 0) & (r == (m // 4) * 64 + 60 + m % 4)
-        low = (group == 1) & (r == (m // 4) * 64 + m % 4)
-        return high | low | ((group == 2) & (r == m)) | ((group == 3) & (r == 960 + m))
+        group, m = div(l, 64), mod(l, 64)
+        at = div(m, 4) * 64 + mod(m, 4)
+        at = jnp.where(group == 0, at + 60, at)
+        return r == jnp.where(group == 2, m, jnp.where(group == 3, m + 960, at))
 
     pick = one_hot((1024, 256), rule)
     for i in range(3):
@@ -316,10 +324,11 @@
     red[...] = mm(down_out[...], hid[...]).astype(BF)
 
     def rule(r, l):
-        group, m = l // 16, l % 16
-        high = (group == 0) & (r == (m // 2) * 16 + 14 + m % 2)
-        low = (group == 1) & (r == (m // 2) * 16 + m % 2)
-        return high | low | ((group == 2) & (r == m)) | ((group == 3) & (r == 112 + m))
+        group, m = div(l, 16), mod(l, 16)
+        at = div(m, 2) * 16 + mod(m, 2)
+        at = jnp.where(group == 0, at + 14, at)
+        at = jnp.where(group == 2, m, jnp.where(group == 3, m + 112, at))
+        return (group < 4) & (r == at)
 
     pick = one_hot((128, 128), rule)
     for i in range(3):
@@ -414,7 +423,7 @@
             def rule(r, l):
                 main = (l >= main_to) & (l < main_to + 16) & (r == l - main_to)
                 m = l - corner_to
-                return main | ((m >= 0) & (m < 16) & (r - 16 == m) & (m // 2 == xc))
+                return main | ((m >= 0) & (m < 16) & (r - 16 == m) & (div(m, 2) == xc))
 
             return one_hot((128, 128), rule)
 
@@ -436,7 +445,7 @@
 
     def rows(y_off):
         return one_hot(
-            (128, 128), lambda r, l: (r < 32) & (l == ((r % 16) // 2) * 16 + r % 2 + y_off)
+            (128, 128), lambda r, l: (r < 32) & (l == div(mod(r, 16), 2) * 16 + mod(r, 2) + y_off)
         )
 
     side_rows = (rows(0), rows(14))

time: 159 us -> 158 us (level)
  no operation moved by 1% of the time
where the time goes in v5:
time: 158 us
  starting transfers between devices  56.5 us (36%)
  Pallas kernels  33.1 us (21%)
  waiting for transfers between devices  32.7 us (21%)
  blocking collectives  27 us (17%)
  local copies, waits for them, and re-layouts  3.77 us (2%)
  other arithmetic  3.62 us (2%)
    pallas_call x8, Pallas kernels, call(): pl.pallas_call(kernel, out_shape=[jax.ShapeDtypeStruct(*o) for o in outs]...  33.1 us
    ppermute x10, starting transfers between devices, swap_cores(): return lax.ppermute(v, 'core', [(0, 1), (1, 0)])  15.6 us
    all_to_all x1, blocking collectives, on_device(): pieces = lax.all_to_all(copies, ('x', 'y', 'core'), 0, 0, tiled=True)  14.9 us
    all_to_all x1, starting transfers between devices, on_device(): small = lax.all_to_all(small, ('x', 'y', 'core'), 0, 0, tiled=True)  13.3 us
    ppermute x6, waiting for transfers between devices, chips_on(): return lax.ppermute(v, SPACE, up + down)  12.7 us
    all_to_all x1, starting transfers between devices, on_device(): two = lax.all_to_all(two, ('x', 'y', 'core'), 0, 0, tiled=True)  12.3 us
    all_to_all x1, blocking collectives, on_device(): lax.all_to_all(jnp.concatenate([mine, mine]), ('zh', 'dp'), 0, 0, tiled=T...  12.1 us
    all_to_all x1, waiting for transfers between devices, on_device(): small = lax.all_to_all(small, ('x', 'y', 'core'), 0, 0, tiled=True)  11.6 us
  transfers between devices with their start and end apart: 24, of which 11 were waited for; matrix products, arithmetic and copies ran while one was open for 0% of the time, Pallas kernels for 14%

profile of v5, /device:TPU:1, one launch (start us, length us, event | category | flops | bytes accessed | tf_op | source)
XLA Modules:
  0.0 157.6 jit_solution(3259538596092267913)
XLA Ops:
  2.1 2.1 %shard_map.102 = (bf16[3,64,256]{2,1,0:T(8,128)(2,1)}, bf16[80,640]{1,0:T(8,128)(2,1)}) custom-call(s32[8]{0:T(128)} %compare_select_fusion.4.sc, s32[128]{0:T(128)} %home.5, bf16[3,64,1024]{2,1,0:T(8,128)(2,1)} %bitcast.10, bf16[16,1728]{1,0:T(8,128)(2,1)} %w_ref.1, bf16[32,512]{1,0:T(8,128)(2,1)} %d_ref.1), custom_call_target="tpu_custom_call" | custom-call | tf_op jit(solution)/shard_map/pallas_call | solution.py:539
  4.1 3.2 %collective-permute-start = (bf16[3,64,256]{2,1,0:T(8,128)(2,1)}, bf16[3,64,256]{2,1,0:T(8,128)(2,1)S(1)}, u32[]{:S(2)}, u32[]{:S(2)}) collective-permute-start(bf16[3,64,256]{2,1,0:T(8,128)(2,1)} %get-tuple-element.22.own), channel_id=1, source_target_pairs={{0,1},{1,0},{2,3},{3,2},{4,5},{5,4},{6,7},{7,6},{8,9},{9,8},{10,11... | collective-permute-start | bytes 294920 | tf_op jit(solution)/shard_map/ppermute | solution.py:551
  7.3 2.6 %collective-permute-start.7 = (bf16[80,640]{1,0:T(8,128)(2,1)}, bf16[80,640]{1,0:T(8,128)(2,1)S(1)}, u32[]{:S(2)}, u32[]{:S(2)}) collective-permute-start(bf16[80,640]{1,0:T(8,128)(2,1)} %get-tuple-element.23.w_a), channel_id=1, source_target_pairs={{0,192},{64,128},{128,64},{192,0},{1,193},{65,129},{129,65},{193,1... | collective-permute-start | bytes 307208 | tf_op jit(solution)/shard_map/ppermute | solution.py:561
  11.5 1.8 %shard_map.103 = bf16[64,256]{1,0:T(8,128)(2,1)} custom-call(s32[8]{0:T(128)} %compare_select_fusion.4.sc, bf16[3,64,256]{2,1,0:T(8,128)(2,1)} %get-tuple-element.22.own, bf16[3,64,256]{2,1,0:T(8,128)(2,1)} %copy-done), custom_call_target="tpu_custom_call" | custom-call | tf_op jit(solution)/shard_map/pallas_call | solution.py:539
  13.3 1.3 collective-permute-start.2
  14.6 1.3 collective-permute-start.1
  15.9 1.5 collective-permute-start.14
  17.5 1.3 collective-permute-done.6.w_c
  18.9 2.2 %collective-permute-start.15 = (bf16[32,3456]{1,0:T(8,128)(2,1)}, bf16[32,3456]{1,0:T(8,128)(2,1)S(1)}, u32[]{:S(2)}, u32[]{:S(2)}) collective-permute-start(bf16[32,3456]{1,0:T(8,128)(2,1)} %w_a.1), channel_id=1, source_target_pairs={{0,192},{64,128},{128,64},{192,0},{1,193},{65,129},{129,65},{193,1... | collective-permute-start | bytes 663560 | tf_op jit(solution)/shard_map/ppermute | solution.py:561
  21.1 4.4 %collective-permute-start.4 = (bf16[64,256]{1,0:T(8,128)(2,1)S(1)}, bf16[64,256]{1,0:T(8,128)(2,1)S(1)}, u32[]{:S(2)}, u32[]{:S(2)}) collective-permute-start(bf16[64,256]{1,0:T(8,128)(2,1)S(1)} %collective-permute-done.2.got2), channel_id=1, source_target_pairs={{0,1},{1,0},{2,3},{3,2},{4,5},{5,4},{6,7},{7,6},{8,9},{9,8},{10,11... | collective-permute-start | bytes 98312 | tf_op jit(solution)/shard_map/ppermute | solution.py:551
  27.4 8.8 %shard_map.104 = (bf16[3,640,1152]{2,1,0:T(8,128)(2,1)}, bf16[512,384]{1,0:T(8,128)(2,1)}, f32[512,384]{1,0:T(8,128)}, bf16[128,384]{1,0:T(8,128)(2,1)}, bf16[3,...) custom-call(s32[8]{0:T(128)} %compare_select_fusion.4.sc, s32[128]{0:T(128)} %home.5, s32[4,128]{1,0:T(4,128)} %bitcast.13, ...), custom_call_target="tpu_custom_call" | custom-call | tf_op jit(solution)/shard_map/pallas_call | solution.py:539
  36.4 1.4 collective-permute-done.8.other
  38.4 1.8 %shard_map.105 = bf16[128,128]{1,0:T(8,128)(2,1)} custom-call(s32[8]{0:T(128)} %compare_select_fusion.4.sc, bf16[3,128,128]{2,1,0:T(8,128)(2,1)} %get-tuple-element.25.own, bf16[3,128,128]{2,1,0:T(8,128)(2,1)} %copy-done.1), custom_call_target="tpu_custom_call" | custom-call | tf_op jit(solution)/shard_map/pallas_call | solution.py:539
  40.2 1.3 collective-permute-start.10
  41.5 1.3 collective-permute-start.9
  42.8 8.1 %collective-permute-done.10.got2 = bf16[128,128]{1,0:T(8,128)(2,1)S(1)} collective-permute-done((bf16[128,128]{1,0:T(8,128)(2,1)}, bf16[128,128]{1,0:T(8,128)(2,1)S(1)}, u32[]{:S(2)}, u32[]{:S(2)}) %collective-permute-start.10) | collective-permute-done | bytes 32800 | tf_op jit(solution)/shard_map/ppermute | solution.py:557
  50.8 2.5 %collective-permute-start.12 = (bf16[128,128]{1,0:T(8,128)(2,1)S(1)}, bf16[128,128]{1,0:T(8,128)(2,1)S(1)}, u32[]{:S(2)}, u32[]{:S(2)}) collective-permute-start(bf16[128,128]{1,0:T(8,128)(2,1)S(1)} %collective-permute-done.10.got2), channel_id=1, source_target_pairs={{0,1},{1,0},{2,3},{3,2},{4,5},{5,4},{6,7},{7,6},{8,9},{9,8},{10,11... | collective-permute-start | bytes 98312 | tf_op jit(solution)/shard_map/ppermute | solution.py:551
  53.4 1.8 %collective-permute-start.11 = (bf16[128,128]{1,0:T(8,128)(2,1)S(1)}, bf16[128,128]{1,0:T(8,128)(2,1)S(1)}, u32[]{:S(2)}, u32[]{:S(2)}) collective-permute-start(bf16[128,128]{1,0:T(8,128)(2,1)S(1)} %collective-permute-done.9.got1), channel_id=1, source_target_pairs={{0,1},{1,0},{2,3},{3,2},{4,5},{5,4},{6,7},{7,6},{8,9},{9,8},{10,11... | collective-permute-start | bytes 98312 | tf_op jit(solution)/shard_map/ppermute | solution.py:551
  56.7 7.5 %shard_map.106 = (bf16[3,128,128]{2,1,0:T(8,128)(2,1)}, bf16[32,4,16,128]{3,2,1,0:T(8,128)(2,1)}, bf16[32,4,16,128]{3,2,1,0:T(8,128)(2,1)}, f32[128,384]{1,0:T(8,128)}, bf16[3,128,128]{2,1,0:T(8,128)(2,1)}) custom-call(s32[8]{0:T(128)} %compare_select_fusion.4.sc, s32[128]{0:T(128)} %home.5, s32[4,128]{1,0:T(4,128)} %bitcast.14, ...), custom_call_target="tpu_custom_call" | custom-call | tf_op jit(solution)/shard_map/pallas_call | solution.py:539
  64.5 1.8 %collective-permute-done.16 = bf16[32,4,16,128]{3,2,1,0:T(8,128)(2,1)S(1)} collective-permute-done((bf16[32,4,16,128]{3,2,1,0:T(8,128)(2,1)}, bf16[32,4,16,128]{3,2,1,0:T(8,128)(2,1)S(1)}, u32[]{:S(2)}, u32[]{:S(2)}) %collective-permute-start.16) | collective-permute-done | bytes 524320 | tf_op jit(solution)/shard_map/ppermute | solution.py:551
  66.2 2.0 %add_convert_fusion = bf16[32,4,16,128]{3,2,1,0:T(8,128)(2,1)} fusion(bf16[32,4,16,128]{3,2,1,0:T(8,128)(2,1)S(1)} %collective-permute-done.16, bf16[32,4,16,128]{3,2,1,0:T(8,128)(2,1)} %get-tuple-element.27), kind=kLoop, calls=%fused_computation | loop fusion | flops 1048576 | bytes 1572864 | tf_op jit(solution)/shard_map/convert_element_type | solution.py:619
  68.3 12.3 %all-to-all-start = ((bf16[32,4,16,128]{3,2,1,0:T(8,128)(2,1)}), bf16[32,4,16,128]{3,2,1,0:T(8,128)(2,1)S(1)}, u32[]{:S(2)}, u32[]{:S(2)}) async-start(bf16[32,4,16,128]{3,2,1,0:T(8,128)(2,1)} %add_convert_fusion), calls=%async_computation | async-start | bytes 1048576 | tf_op jit(solution)/shard_map/all_to_all | solution.py:620
  82.9 1.9 %shard_map.107 = bf16[128,128]{1,0:T(8,128)(2,1)} custom-call(s32[8]{0:T(128)} %compare_select_fusion.4.sc, bf16[3,128,128]{2,1,0:T(8,128)(2,1)} %get-tuple-element.30.own, bf16[3,128,128]{2,1,0:T(8,128)(2,1)} %copy-done.2), custom_call_target="tpu_custom_call" | custom-call | tf_op jit(solution)/shard_map/pallas_call | solution.py:539
  86.0 1.3 collective-permute-start.18
  87.3 4.6 %collective-permute-done.19.got2 = bf16[128,128]{1,0:T(8,128)(2,1)S(1)} collective-permute-done((bf16[128,128]{1,0:T(8,128)(2,1)}, bf16[128,128]{1,0:T(8,128)(2,1)S(1)}, u32[]{:S(2)}, u32[]{:S(2)}) %collective-permute-start.19) | collective-permute-done | bytes 32800 | tf_op jit(solution)/shard_map/ppermute | solution.py:557
  92.8 1.8 %collective-permute-start.20 = (bf16[128,128]{1,0:T(8,128)(2,1)S(1)}, bf16[128,128]{1,0:T(8,128)(2,1)S(1)}, u32[]{:S(2)}, u32[]{:S(2)}) collective-permute-start(bf16[128,128]{1,0:T(8,128)(2,1)S(1)} %collective-permute-done.18.got1), channel_id=1, source_target_pairs={{0,1},{1,0},{2,3},{3,2},{4,5},{5,4},{6,7},{7,6},{8,9},{9,8},{10,11... | collective-permute-start | bytes 98312 | tf_op jit(solution)/shard_map/ppermute | solution.py:551
  96.0 7.5 %shard_map.108 = bf16[32,4,16,128]{3,2,1,0:T(8,128)(2,1)} custom-call(s32[8]{0:T(128)} %compare_select_fusion.4.sc, s32[4,128]{1,0:T(4,128)} %bitcast.15, f32[128,384]{1,0:T(8,128)} %get-tuple-element.29.grad, bf16[3,128,128]{2,1,0:T(8,128)(2,1)} %get-tuple-element.30.own, bf16[3,128,128]{2,1,0:T(8,128)(2,1)} %copy-done.2, bf16[128,128]{1,0:T(8,128)(2,1)} %copy-done.10, ...), custom_call_target="tpu_custom_call" | custom-call | tf_op jit(solution)/shard_map/pallas_call | solution.py:539
  103.6 13.3 %all-to-all-start.1 = ((bf16[32,4,16,128]{3,2,1,0:T(8,128)(2,1)}), bf16[32,4,16,128]{3,2,1,0:T(8,128)(2,1)S(1)}, u32[]{:S(2)}, u32[]{:S(2)}) async-start(bf16[32,4,16,128]{3,2,1,0:T(8,128)(2,1)} %shard_map.108), calls=%async_computation.1 | async-start | bytes 1048576 | tf_op jit(solution)/shard_map/all_to_all | solution.py:631
  117.0 11.6 %all-to-all-done.1 = bf16[32,4,16,128]{3,2,1,0:T(8,128)(2,1)S(1)} async-done(((bf16[32,4,16,128]{3,2,1,0:T(8,128)(2,1)}), bf16[32,4,16,128]{3,2,1,0:T(8,128)(2,1)S(1)}, u32[]{:S(2)}, u32[]{:S(2)}) %all-to-all-start.1) | async-done | bytes 524320 | tf_op jit(solution)/shard_map/all_to_all | solution.py:631
  128.7 12.1 %all_to_all.20 = bf16[8,48,128]{2,1,0:T(8,128)(2,1)S(1)} all-to-all(bf16[8,48,128]{2,1,0:T(8,128)(2,1)S(1)} %maximum_maximum_fusion), channel_id=1, replica_groups=mesh['dp'=4,'x'=4,'zh'=2,'y'=4,'core'=2] {'zh','dp'}, dimensions={0} | all-to-all | bytes 196608 | tf_op jit(solution)/shard_map/all_to_all | solution.py:634
  140.9 14.9 %all_to_all.21.pieces = bf16[32,48,128]{2,1,0:T(8,128)(2,1)} all-to-all(bf16[32,48,128]{2,1,0:T(8,128)(2,1)S(1)} %broadcast_in_dim.33), channel_id=1, replica_groups=mesh['dp'=4,'x'=4,'zh'=2,'y'=4,'core'=2] {'x','y','core'}, dimensions={0} | all-to-all | bytes 786432 | tf_op jit(solution)/shard_map/all_to_all | solution.py:637
  155.7 1.8 %shard_map.109 = (f32[16,1728]{1,0:T(8,128)}, f32[32,512]{1,0:T(8,128)}, f32[32,3456]{1,0:T(8,128)}) custom-call(bf16[32,48,128]{2,1,0:T(8,128)(2,1)} %all_to_all.21.pieces), custom_call_target="tpu_custom_call" | custom-call | tf_op jit(solution)/shard_map/pallas_call | solution.py:539
  (78 shorter events, 13.7 us)
Async XLA Ops:
  4.1 6.8 %collective-permute-start = (bf16[3,64,256]{2,1,0:T(8,128)(2,1)}, bf16[3,64,256]{2,1,0:T(8,128)(2,1)S(1)}, u32[]{:S(2)}, u32[]{:S(2)}) collective-permute-start(bf16[3,64,256]{2,1,0:T(8,128)(2,1)} %get-tuple-element.22.own), channel_id=1, source_target_pairs={{0,1},{1,0},{2,3},{3,2},{4,5},{5,4},{6,7},{7,6},{8,9},{9,8},{10,11... | collective-permute-start | bytes 294920 | tf_op jit(solution)/shard_map/ppermute | solution.py:551
  7.3 8.5 %collective-permute-start.7 = (bf16[80,640]{1,0:T(8,128)(2,1)}, bf16[80,640]{1,0:T(8,128)(2,1)S(1)}, u32[]{:S(2)}, u32[]{:S(2)}) collective-permute-start(bf16[80,640]{1,0:T(8,128)(2,1)} %get-tuple-element.23.w_a), channel_id=1, source_target_pairs={{0,192},{64,128},{128,64},{192,0},{1,193},{65,129},{129,65},{193,1... | collective-permute-start | bytes 307208 | tf_op jit(solution)/shard_map/ppermute | solution.py:561
  10.0 8.8 %collective-permute-start.6 = (bf16[80,640]{1,0:T(8,128)(2,1)}, bf16[80,640]{1,0:T(8,128)(2,1)S(1)}, u32[]{:S(2)}, u32[]{:S(2)}) collective-permute-start(bf16[80,640]{1,0:T(8,128)(2,1)} %get-tuple-element.23.w_a), channel_id=1, source_target_pairs={{0,128},{64,192},{128,0},{192,64},{1,129},{65,193},{129,1},{193,65... | collective-permute-start | bytes 307208 | tf_op jit(solution)/shard_map/ppermute | solution.py:561
  10.0 8.9 %collective-permute-start.5 = (bf16[80,640]{1,0:T(8,128)(2,1)}, bf16[80,640]{1,0:T(8,128)(2,1)S(1)}, u32[]{:S(2)}, u32[]{:S(2)}) collective-permute-start(bf16[80,640]{1,0:T(8,128)(2,1)} %get-tuple-element.23.w_a), channel_id=1, source_target_pairs={{0,64},{64,0},{128,192},{192,128},{1,65},{65,1},{129,193},{193,129... | collective-permute-start | bytes 307208 | tf_op jit(solution)/shard_map/ppermute | solution.py:561
  13.3 7.8 %collective-permute-start.2 = (bf16[64,256]{1,0:T(8,128)(2,1)}, bf16[64,256]{1,0:T(8,128)(2,1)S(1)}, u32[]{:S(2)}, u32[]{:S(2)}) collective-permute-start(bf16[64,256]{1,0:T(8,128)(2,1)} %shard_map.103), channel_id=1, source_target_pairs={{0,4},{2,6},{4,8},{6,10},{8,12},{10,14},{12,16},{14,18},{16,20},{1... | collective-permute-start | bytes 98312 | tf_op jit(solution)/shard_map/ppermute | solution.py:557
  14.6 11.0 %collective-permute-start.1 = (bf16[64,256]{1,0:T(8,128)(2,1)}, bf16[64,256]{1,0:T(8,128)(2,1)S(1)}, u32[]{:S(2)}, u32[]{:S(2)}) collective-permute-start(bf16[64,256]{1,0:T(8,128)(2,1)} %shard_map.103), channel_id=1, source_target_pairs={{0,2},{2,4},{4,6},{6,8},{8,10},{10,12},{12,14},{14,16},{16,18},{18... | collective-permute-start | bytes 98312 | tf_op jit(solution)/shard_map/ppermute | solution.py:557
  15.9 10.9 %copy-start.6 = (bf16[80,640]{1,0:T(8,128)(2,1)}, bf16[80,640]{1,0:T(8,128)(2,1)S(1)}, u32[]{:S(2)}) copy-start(bf16[80,640]{1,0:T(8,128)(2,1)S(1)} %collective-permute-done.7.w_d) | copy-start | bytes 307204
  15.9 39.3 %collective-permute-start.14 = (bf16[32,3456]{1,0:T(8,128)(2,1)}, bf16[32,3456]{1,0:T(8,128)(2,1)S(1)}, u32[]{:S(2)}, u32[]{:S(2)}) collective-permute-start(bf16[32,3456]{1,0:T(8,128)(2,1)} %w_a.1), channel_id=1, source_target_pairs={{0,128},{64,192},{128,0},{192,64},{1,129},{65,193},{129,1},{193,65... | collective-permute-start | bytes 663560 | tf_op jit(solution)/shard_map/ppermute | solution.py:561
  18.7 8.0 %copy-start.7 = (bf16[80,640]{1,0:T(8,128)(2,1)}, bf16[80,640]{1,0:T(8,128)(2,1)S(1)}, u32[]{:S(2)}) copy-start(bf16[80,640]{1,0:T(8,128)(2,1)S(1)} %collective-permute-done.6.w_c) | copy-start | bytes 307204
  18.7 36.4 %collective-permute-start.13 = (bf16[32,3456]{1,0:T(8,128)(2,1)}, bf16[32,3456]{1,0:T(8,128)(2,1)S(1)}, u32[]{:S(2)}, u32[]{:S(2)}) collective-permute-start(bf16[32,3456]{1,0:T(8,128)(2,1)} %w_a.1), channel_id=1, source_target_pairs={{0,64},{64,0},{128,192},{192,128},{1,65},{65,1},{129,193},{193,129... | collective-permute-start | bytes 663560 | tf_op jit(solution)/shard_map/ppermute | solution.py:561
  18.9 7.8 %copy-start.8 = (bf16[80,640]{1,0:T(8,128)(2,1)}, bf16[80,640]{1,0:T(8,128)(2,1)S(1)}, u32[]{:S(2)}) copy-start(bf16[80,640]{1,0:T(8,128)(2,1)S(1)} %collective-permute-done.5.w_b) | copy-start | bytes 307204
  18.9 36.3 %collective-permute-start.15 = (bf16[32,3456]{1,0:T(8,128)(2,1)}, bf16[32,3456]{1,0:T(8,128)(2,1)S(1)}, u32[]{:S(2)}, u32[]{:S(2)}) collective-permute-start(bf16[32,3456]{1,0:T(8,128)(2,1)} %w_a.1), channel_id=1, source_target_pairs={{0,192},{64,128},{128,64},{192,0},{1,193},{65,129},{129,65},{193,1... | collective-permute-start | bytes 663560 | tf_op jit(solution)/shard_map/ppermute | solution.py:561
  21.1 5.6 %copy-start.13 = (bf16[64,256]{1,0:T(8,128)(2,1)}, bf16[64,256]{1,0:T(8,128)(2,1)S(1)}, u32[]{:S(2)}) copy-start(bf16[64,256]{1,0:T(8,128)(2,1)S(1)} %collective-permute-done.2.got2) | copy-start | bytes 98308
  21.1 5.3 %collective-permute-start.4 = (bf16[64,256]{1,0:T(8,128)(2,1)S(1)}, bf16[64,256]{1,0:T(8,128)(2,1)S(1)}, u32[]{:S(2)}, u32[]{:S(2)}) collective-permute-start(bf16[64,256]{1,0:T(8,128)(2,1)S(1)} %collective-permute-done.2.got2), channel_id=1, source_target_pairs={{0,1},{1,0},{2,3},{3,2},{4,5},{5,4},{6,7},{7,6},{8,9},{9,8},{10,11... | collective-permute-start | bytes 98312 | tf_op jit(solution)/shard_map/ppermute | solution.py:551
  25.5 1.2 collective-permute-start.3
  36.1 1.6 %collective-permute-start.8 = (bf16[3,128,128]{2,1,0:T(8,128)(2,1)}, bf16[3,128,128]{2,1,0:T(8,128)(2,1)S(1)}, u32[]{:S(2)}, u32[]{:S(2)}) collective-permute-start(bf16[3,128,128]{2,1,0:T(8,128)(2,1)} %get-tuple-element.25.own), channel_id=1, source_target_pairs={{0,1},{1,0},{2,3},{3,2},{4,5},{5,4},{6,7},{7,6},{8,9},{9,8},{10,11... | collective-permute-start | bytes 294920 | tf_op jit(solution)/shard_map/ppermute | solution.py:551
  40.2 10.7 %collective-permute-start.10 = (bf16[128,128]{1,0:T(8,128)(2,1)}, bf16[128,128]{1,0:T(8,128)(2,1)S(1)}, u32[]{:S(2)}, u32[]{:S(2)}) collective-permute-start(bf16[128,128]{1,0:T(8,128)(2,1)} %shard_map.105), channel_id=1, source_target_pairs={{0,4},{2,6},{4,8},{6,10},{8,12},{10,14},{12,16},{14,18},{16,20},{1... | collective-permute-start | bytes 98312 | tf_op jit(solution)/shard_map/ppermute | solution.py:557
  41.5 11.9 %collective-permute-start.9 = (bf16[128,128]{1,0:T(8,128)(2,1)}, bf16[128,128]{1,0:T(8,128)(2,1)S(1)}, u32[]{:S(2)}, u32[]{:S(2)}) collective-permute-start(bf16[128,128]{1,0:T(8,128)(2,1)} %shard_map.105), channel_id=1, source_target_pairs={{0,2},{2,4},{4,6},{6,8},{8,10},{10,12},{12,14},{14,16},{16,18},{18... | collective-permute-start | bytes 98312 | tf_op jit(solution)/shard_map/ppermute | solution.py:557
  50.8 5.2 %copy-start.15 = (bf16[128,128]{1,0:T(8,128)(2,1)}, bf16[128,128]{1,0:T(8,128)(2,1)S(1)}, u32[]{:S(2)}) copy-start(bf16[128,128]{1,0:T(8,128)(2,1)S(1)} %collective-permute-done.10.got2) | copy-start | bytes 98308
  50.8 4.4 %collective-permute-start.12 = (bf16[128,128]{1,0:T(8,128)(2,1)S(1)}, bf16[128,128]{1,0:T(8,128)(2,1)S(1)}, u32[]{:S(2)}, u32[]{:S(2)}) collective-permute-start(bf16[128,128]{1,0:T(8,128)(2,1)S(1)} %collective-permute-done.10.got2), channel_id=1, source_target_pairs={{0,1},{1,0},{2,3},{3,2},{4,5},{5,4},{6,7},{7,6},{8,9},{9,8},{10,11... | collective-permute-start | bytes 98312 | tf_op jit(solution)/shard_map/ppermute | solution.py:551
  53.4 2.7 %copy-start.16 = (bf16[128,128]{1,0:T(8,128)(2,1)}, bf16[128,128]{1,0:T(8,128)(2,1)S(1)}, u32[]{:S(2)}) copy-start(bf16[128,128]{1,0:T(8,128)(2,1)S(1)} %collective-permute-done.9.got1) | copy-start | bytes 98308
  53.4 2.6 %collective-permute-start.11 = (bf16[128,128]{1,0:T(8,128)(2,1)S(1)}, bf16[128,128]{1,0:T(8,128)(2,1)S(1)}, u32[]{:S(2)}, u32[]{:S(2)}) collective-permute-start(bf16[128,128]{1,0:T(8,128)(2,1)S(1)} %collective-permute-done.9.got1), channel_id=1, source_target_pairs={{0,1},{1,0},{2,3},{3,2},{4,5},{5,4},{6,7},{7,6},{8,9},{9,8},{10,11... | collective-permute-start | bytes 98312 | tf_op jit(solution)/shard_map/ppermute | solution.py:551
  64.1 2.1 %collective-permute-start.16 = (bf16[32,4,16,128]{3,2,1,0:T(8,128)(2,1)}, bf16[32,4,16,128]{3,2,1,0:T(8,128)(2,1)S(1)}, u32[]{:S(2)}, u32[]{:S(2)}) collective-permute-start(bf16[32,4,16,128]{3,2,1,0:T(8,128)(2,1)} %get-tuple-element.28), channel_id=1, source_target_pairs={{0,1},{1,0},{2,3},{3,2},{4,5},{5,4},{6,7},{7,6},{8,9},{9,8},{10,11... | collective-permute-start | bytes 1572872 | tf_op jit(solution)/shard_map/ppermute | solution.py:551
  68.3 35.3 %all-to-all-start = ((bf16[32,4,16,128]{3,2,1,0:T(8,128)(2,1)}), bf16[32,4,16,128]{3,2,1,0:T(8,128)(2,1)S(1)}, u32[]{:S(2)}, u32[]{:S(2)}) async-start(bf16[32,4,16,128]{3,2,1,0:T(8,128)(2,1)} %add_convert_fusion), calls=%async_computation | async-start | bytes 1048576 | tf_op jit(solution)/shard_map/all_to_all | solution.py:620
  80.6 1.6 %collective-permute-start.17 = (bf16[3,128,128]{2,1,0:T(8,128)(2,1)}, bf16[3,128,128]{2,1,0:T(8,128)(2,1)S(1)}, u32[]{:S(2)}, u32[]{:S(2)}) collective-permute-start(bf16[3,128,128]{2,1,0:T(8,128)(2,1)} %get-tuple-element.30.own), channel_id=1, source_target_pairs={{0,1},{1,0},{2,3},{3,2},{4,5},{5,4},{6,7},{7,6},{8,9},{9,8},{10,11... | collective-permute-start | bytes 294920 | tf_op jit(solution)/shard_map/ppermute | solution.py:551
  84.7 7.2 %collective-permute-start.19 = (bf16[128,128]{1,0:T(8,128)(2,1)}, bf16[128,128]{1,0:T(8,128)(2,1)S(1)}, u32[]{:S(2)}, u32[]{:S(2)}) collective-permute-start(bf16[128,128]{1,0:T(8,128)(2,1)} %shard_map.107), channel_id=1, source_target_pairs={{0,4},{2,6},{4,8},{6,10},{8,12},{10,14},{12,16},{14,18},{16,20},{1... | collective-permute-start | bytes 98312 | tf_op jit(solution)/shard_map/ppermute | solution.py:557
  86.0 6.7 %collective-permute-start.18 = (bf16[128,128]{1,0:T(8,128)(2,1)}, bf16[128,128]{1,0:T(8,128)(2,1)S(1)}, u32[]{:S(2)}, u32[]{:S(2)}) collective-permute-start(bf16[128,128]{1,0:T(8,128)(2,1)} %shard_map.107), channel_id=1, source_target_pairs={{0,2},{2,4},{4,6},{6,8},{8,10},{10,12},{12,14},{14,16},{16,18},{18... | collective-permute-start | bytes 98312 | tf_op jit(solution)/shard_map/ppermute | solution.py:557
  91.9 3.5 %copy-start.9 = (bf16[128,128]{1,0:T(8,128)(2,1)}, bf16[128,128]{1,0:T(8,128)(2,1)S(1)}, u32[]{:S(2)}) copy-start(bf16[128,128]{1,0:T(8,128)(2,1)S(1)} %collective-permute-done.19.got2) | copy-start | bytes 98308
  91.9 2.7 %collective-permute-start.21 = (bf16[128,128]{1,0:T(8,128)(2,1)S(1)}, bf16[128,128]{1,0:T(8,128)(2,1)S(1)}, u32[]{:S(2)}, u32[]{:S(2)}) collective-permute-start(bf16[128,128]{1,0:T(8,128)(2,1)S(1)} %collective-permute-done.19.got2), channel_id=1, source_target_pairs={{0,1},{1,0},{2,3},{3,2},{4,5},{5,4},{6,7},{7,6},{8,9},{9,8},{10,11... | collective-permute-start | bytes 98312 | tf_op jit(solution)/shard_map/ppermute | solution.py:551
  92.8 2.7 %copy-start.10 = (bf16[128,128]{1,0:T(8,128)(2,1)}, bf16[128,128]{1,0:T(8,128)(2,1)S(1)}, u32[]{:S(2)}) copy-start(bf16[128,128]{1,0:T(8,128)(2,1)S(1)} %collective-permute-done.18.got1) | copy-start | bytes 98308
  92.8 2.6 %collective-permute-start.20 = (bf16[128,128]{1,0:T(8,128)(2,1)S(1)}, bf16[128,128]{1,0:T(8,128)(2,1)S(1)}, u32[]{:S(2)}, u32[]{:S(2)}) collective-permute-start(bf16[128,128]{1,0:T(8,128)(2,1)S(1)} %collective-permute-done.18.got1), channel_id=1, source_target_pairs={{0,1},{1,0},{2,3},{3,2},{4,5},{5,4},{6,7},{7,6},{8,9},{9,8},{10,11... | collective-permute-start | bytes 98312 | tf_op jit(solution)/shard_map/ppermute | solution.py:551
  103.6 24.9 %all-to-all-start.1 = ((bf16[32,4,16,128]{3,2,1,0:T(8,128)(2,1)}), bf16[32,4,16,128]{3,2,1,0:T(8,128)(2,1)S(1)}, u32[]{:S(2)}, u32[]{:S(2)}) async-start(bf16[32,4,16,128]{3,2,1,0:T(8,128)(2,1)} %shard_map.108), calls=%async_computation.1 | async-start | bytes 1048576 | tf_op jit(solution)/shard_map/all_to_all | solution.py:631
  (13 other events, 9.9 us)
